TPU v7x, 256 devices: a whole 4x4x8 slice. The times are simulated.
256 devices in a mesh: sec: 4 (over z_lo), row: 8 (over y, core), rad: 8 (over z_hi, x).
Axes of the slice: x: 4, y: 4, z: 8 (z_hi: 2, z_lo: 4; z = z_hi * 4 + z_lo), core: 2. Of those that a mesh axis runs over, the one named last changes fastest.
Arguments:
- state: float32 [5, 4, 16, 64, 1024], P(None, 'sec', None, 'rad', 'row'), may hold values from -6 to 6
- volume: float32 [4, 16, 64, 1024], P('sec', None, 'rad', 'row'), may hold values from 0.5 to 2
- face_axial: float32 [4, 16, 64, 1024], P('sec', None, 'rad', 'row'), may hold values from 0.5 to 1.5
- face_radial: float32 [4, 16, 64, 1024], P('sec', None, 'rad', 'row'), may hold values from 0.5 to 1.5
- face_circum: float32 [4, 16, 64, 1024], P('sec', None, 'rad', 'row'), may hold values from 0.5 to 1.5
- viscosity: float32 [4, 16, 64, 1024], P('sec', None, 'rad', 'row'), may hold values from 0.05 to 0.5
- flux_matrix: float32 [4, 3, 5, 5], P('sec'), may hold values from -2.5 to 2.5
- inflow_plane: float32 [5, 64, 1024], P(None, 'rad', 'row'), may hold values from -6 to 6
- outflow_plane: float32 [5, 64, 1024], P(None, 'rad', 'row'), may hold values from -6 to 6
- down_donors: int32 [4, 512], P('sec', ('row', 'rad')), may hold values from 0 to 511, each once within a row
- up_donors: int32 [4, 512], P('sec', ('row', 'rad')), may hold values from 0 to 511, each once within a row
- pressure_weight: float32 [5], replicated, may hold values from -3 to 3
- boundary_coupling: float32 [5], replicated, may hold values from -4 to 4
Outputs:
- advanced: float32 [5, 4, 16, 64, 1024], P(None, 'sec', None, 'rad', 'row')
Inputs may be any that keep to these rules, and one draw needn't show every extreme that they name: `down_donors`: each row names each of the 512 tiles exactly once. `up_donors`: each row names each of the 512 tiles exactly once.
All inputs are finite; a program needn't handle non-finite values.
Results may differ from a plain program's by a relative error of at most 0.0001.
Values sent between devices are 32-bit elements; how exact they have to be, the bound alone decides.
No kernel may reach another device: no remote copies, remote signals or barrier semaphores. Data moves between devices by JAX's collectives and lax.ppermute only.
A program may use at most 64 MiB of HBM per device.

v0:
```python
import jax
import jax.numpy as jnp
from jax import lax
from jax.sharding import PartitionSpec as P

STEPS = 4


time_step = 0.08


def padded_2(shard, sides, width):
    for axis, dim in sides:
        size, length = (lax.axis_size(axis), shard.shape[dim])
        up = [(i, (i + 1) % size) for i in range(size)]
        down = [(j, i) for i, j in up]
        last = lax.slice_in_dim(shard, length - width, length, axis=dim)
        first = lax.slice_in_dim(shard, 0, width, axis=dim)
        before = lax.ppermute(last, axis, up)
        after = lax.ppermute(first, axis, down)
        shard = jnp.concatenate([before, shard, after], axis=dim)
    return shard


def shifted(shard, axis, by):
    length = lax.axis_size(axis)
    pairs = [(i, i + by) for i in range(length) if 0 <= i + by < length]
    return lax.ppermute(shard, axis, pairs)


def to_tiles(plane):
    components, radial, beside_all = plane.shape
    shaped = plane.reshape(components, radial, beside_all // 128, 128)
    return shaped.transpose(1, 2, 0, 3).reshape(radial * (beside_all // 128), components, 128)


def from_tiles(tiles, radial, beside_all):
    components = tiles.shape[1]
    shaped = tiles.reshape(radial, beside_all // 128, components, 128)
    return shaped.transpose(2, 0, 1, 3).reshape(components, radial, beside_all)


def face_divergence(padded, face_area, viscous, matrix, direction):
    length = padded.shape[direction]
    lower_cells = lax.slice_in_dim(padded, 0, length - 1, axis=direction)
    upper_cells = lax.slice_in_dim(padded, 1, length, axis=direction)
    mixed = jnp.einsum(
        "uv,v...->u...", matrix, lower_cells + upper_cells, precision=lax.Precision.HIGHEST
    )
    fluxes = face_area * (0.5 * mixed - viscous * (upper_cells - lower_cells))
    return lax.slice_in_dim(fluxes, 1, length - 1, axis=direction) - lax.slice_in_dim(
        fluxes, 0, length - 2, axis=direction
    )


def select_tiles(piece, wanted):
    offsets = lax.broadcasted_iota(jnp.int32, (1, piece.shape[0]), 1)
    onehot = (wanted[:, None] == offsets).astype(jnp.float32)
    return jnp.einsum("tn,n...->t...", onehot, piece, precision=lax.Precision.HIGHEST)


def tile_pressure(weights, tiles):
    return jnp.einsum("v,tvc->tc", weights, tiles, precision=lax.Precision.HIGHEST)


def body(
    state,
    volume,
    face_axial,
    face_radial,
    face_circum,
    viscosity,
    flux_matrix,
    inflow_plane,
    outflow_plane,
    down_donors,
    up_donors,
    pressure_weight,
    boundary_coupling,
):
    section = lax.axis_index("sec")
    last_section = lax.axis_size("sec") - 1
    at_casing = lax.axis_index("rad") == lax.axis_size("rad") - 1
    field = state[:, 0]
    radial_cells = field.shape[2]
    around_cells = field.shape[3]
    cell_volume = volume[0]
    radial_face = face_radial[0]
    radial_rows = lax.broadcasted_iota(jnp.int32, radial_face.shape, 1)
    radial_face = jnp.where(
        jnp.logical_and(at_casing, radial_rows == radial_cells - 1), 0.0, radial_face
    )
    stacked = jnp.stack([radial_face, face_circum[0], viscosity[0]])
    rims = padded_2(stacked, (("row", 3), ("rad", 2)), 1)
    radial_area = rims[0, :, :-1, 1:-1]
    mu_radial = rims[2, :, :, 1:-1]
    nu_radial = 0.5 * (mu_radial[:, :-1] + mu_radial[:, 1:])
    circ_area = rims[1, :, 1:-1, :-1]
    mu_circ = rims[2, :, 1:-1, :]
    nu_circ = 0.5 * (mu_circ[:, :, :-1] + mu_circ[:, :, 1:])
    own_face = face_axial[0]
    axial_area = jnp.concatenate([own_face[:1], own_face], axis=0)
    own_mu = viscosity[0]
    mu_axial = jnp.concatenate([own_mu[:1], own_mu, own_mu[-1:]], axis=0)
    nu_axial = 0.5 * (mu_axial[:-1] + mu_axial[1:])
    down_local = down_donors[0]
    up_local = up_donors[0]
    inflow_tiles = to_tiles(inflow_plane)
    outflow_tiles = to_tiles(outflow_plane)
    matrices = flux_matrix[0]
    for step_index in range(STEPS):
        outlet_tiles = to_tiles(field[:, -1])
        inlet_tiles = to_tiles(field[:, 0])
        arrived = shifted(outlet_tiles, "sec", 1)
        donor_flow = jnp.where(section == 0, inflow_tiles, arrived)
        rising = shifted(inlet_tiles, "sec", -1)
        donor_beyond = jnp.where(section == last_section, outflow_tiles, rising)
        ghost_tiles = select_tiles(
            lax.all_gather(donor_flow, ("row", "rad"), axis=0, tiled=True), down_local
        )
        beyond_tiles = select_tiles(
            lax.all_gather(donor_beyond, ("row", "rad"), axis=0, tiled=True), up_local
        )
        mapped_tiles = tile_pressure(pressure_weight, beyond_tiles)
        inlet_ghost = from_tiles(ghost_tiles, radial_cells, around_cells)
        outlet = field[:, -1]
        own_pressure = jnp.einsum(
            "v,vjk->jk", pressure_weight, outlet, precision=lax.Precision.HIGHEST
        )
        outlet_ghost = (
            outlet + boundary_coupling[:, None, None] * (mapped_tiles - own_pressure)[None]
        )
        axial_padded = jnp.concatenate([inlet_ghost[:, None], field, outlet_ghost[:, None]], axis=1)
        halo_field = padded_2(field, (("row", 3), ("rad", 2)), 1)
        radial_padded = halo_field[:, :, :, 1:-1]
        circ_padded = halo_field[:, :, 1:-1, :]
        divergence = face_divergence(axial_padded, axial_area, nu_axial, matrices[0], 1)
        divergence = divergence + face_divergence(
            radial_padded, radial_area, nu_radial, matrices[1], 2
        )
        divergence = divergence + face_divergence(circ_padded, circ_area, nu_circ, matrices[2], 3)
        field = field - time_step / cell_volume * divergence
    return field[:, None]


def solution(mesh):
    in_specs = (
        P(None, "sec", None, "rad", "row"),
        P("sec", None, "rad", "row"),
        P("sec", None, "rad", "row"),
        P("sec", None, "rad", "row"),
        P("sec", None, "rad", "row"),
        P("sec", None, "rad", "row"),
        P("sec", None, None, None),
        P(None, "rad", "row"),
        P(None, "rad", "row"),
        P("sec", ("row", "rad")),
        P("sec", ("row", "rad")),
        P(),
        P(),
    )
    out_specs = P(None, "sec", None, "rad", "row")
    return jax.shard_map(body, mesh=mesh, in_specs=in_specs, out_specs=out_specs, check_vma=False)
```

profile of v0, /device:TPU:1, one launch (start us, length us, event | category | flops | bytes accessed | tf_op | source)
XLA Modules:
  0.0 676.1 jit_solution(16294852401820777609)
XLA Ops:
  9.4 3.2 collective-permute-start.6
  14.4 3.4 collective-permute-start.3
  17.8 3.0 collective-permute-start
  22.9 8.4 %collective-permute-start.9 = (f32[3,16,1,130]{3,2,1,0:T(1,128)S(1)}, f32[3,16,1,130]{3,2,1,0:T(1,128)S(1)}, u32[]{:S(2)}, u32[]{:S(2)}) collective-permute-start(f32[3,16,1,130]{3,2,1,0:T(1,128)S(1)} %get-tuple-element.14), channel_id=1, source_target_pairs={{1,0},{2,1},{3,2},{4,3},{5,4},{6,5},{7,6},{0,7},{9,8},{10,9},{11,1... | collective-permute-start | bytes 74888 | tf_op jit(solution)/shard_map/ppermute | solution.py:20
  31.6 7.6 %collective-permute-start.8 = (f32[5,16,1,130]{3,1,0,2:T(8,128)S(1)}, f32[5,16,1,130]{3,1,0,2:T(8,128)S(1)}, u32[]{:S(2)}, u32[]{:S(2)}) collective-permute-start(f32[5,16,1,130]{3,1,0,2:T(8,128)S(1)} %get-tuple-element.11), channel_id=1, source_target_pairs={{1,0},{2,1},{3,2},{4,3},{5,4},{6,5},{7,6},{0,7},{9,8},{10,9},{11,1... | collective-permute-start | bytes 124808 | tf_op jit(solution)/shard_map/ppermute | solution.py:20
  44.1 55.8 %all-gather.11.cloned.1.call-done = f32[512,5,128]{2,0,1:T(8,128)} async-done(((f32[8,5,128]{2,0,1:T(8,128)}), f32[512,5,128]{2,0,1:T(8,128)}) %all-gather.11.cloned.1.call-update) | async-done | bytes 1310736 | tf_op jit(solution)/shard_map/all_gather | solution.py:122
  101.9 76.2 %all-gather.9.cloned.1.call-done = f32[512,5,128]{2,0,1:T(8,128)} async-done(((f32[8,5,128]{2,0,1:T(8,128)}), f32[512,5,128]{2,0,1:T(8,128)}) %all-gather.9.cloned.1.call-update) | async-done | bytes 1310736 | tf_op jit(solution)/shard_map/all_gather | solution.py:119
  182.8 3.2 collective-permute-done.11
  190.4 2.3 collective-permute-start.13
  192.8 4.9 collective-permute-done.13
  198.2 7.3 %collective-permute-start.15 = (f32[5,16,1,130]{3,1,0,2:T(8,128)S(1)}, f32[5,16,1,130]{3,1,0,2:T(8,128)S(1)}, u32[]{:S(2)}, u32[]{:S(2)}) collective-permute-start(f32[5,16,1,130]{3,1,0,2:T(8,128)S(1)} %get-tuple-element.9), channel_id=1, source_target_pairs={{1,0},{2,1},{3,2},{4,3},{5,4},{6,5},{7,6},{0,7},{9,8},{10,9},{11,1... | collective-permute-start | bytes 124808 | tf_op jit(solution)/shard_map/ppermute | solution.py:20
  209.1 53.4 %all-gather.15.cloned.1.call-done = f32[512,5,128]{2,0,1:T(8,128)} async-done(((f32[8,5,128]{2,0,1:T(8,128)}), f32[512,5,128]{2,0,1:T(8,128)}) %all-gather.15.cloned.1.call-update) | async-done | bytes 1310736 | tf_op jit(solution)/shard_map/all_gather | solution.py:122
  264.7 76.0 %all-gather.13.cloned.1.call-done = f32[512,5,128]{2,0,1:T(8,128)} async-done(((f32[8,5,128]{2,0,1:T(8,128)}), f32[512,5,128]{2,0,1:T(8,128)}) %all-gather.13.cloned.1.call-update) | async-done | bytes 1310736 | tf_op jit(solution)/shard_map/all_gather | solution.py:119
  345.1 3.2 collective-permute-done.17
  352.6 2.3 collective-permute-start.19
  355.1 4.8 collective-permute-done.19
  360.3 7.3 %collective-permute-start.21 = (f32[5,16,1,130]{3,1,0,2:T(8,128)S(1)}, f32[5,16,1,130]{3,1,0,2:T(8,128)S(1)}, u32[]{:S(2)}, u32[]{:S(2)}) collective-permute-start(f32[5,16,1,130]{3,1,0,2:T(8,128)S(1)} %get-tuple-element.7), channel_id=1, source_target_pairs={{1,0},{2,1},{3,2},{4,3},{5,4},{6,5},{7,6},{0,7},{9,8},{10,9},{11,1... | collective-permute-start | bytes 124808 | tf_op jit(solution)/shard_map/ppermute | solution.py:20
  371.2 53.6 %all-gather.19.cloned.1.call-done = f32[512,5,128]{2,0,1:T(8,128)} async-done(((f32[8,5,128]{2,0,1:T(8,128)}), f32[512,5,128]{2,0,1:T(8,128)}) %all-gather.19.cloned.1.call-update) | async-done | bytes 1310736 | tf_op jit(solution)/shard_map/all_gather | solution.py:122
  426.9 76.0 %all-gather.17.cloned.1.call-done = f32[512,5,128]{2,0,1:T(8,128)} async-done(((f32[8,5,128]{2,0,1:T(8,128)}), f32[512,5,128]{2,0,1:T(8,128)}) %all-gather.17.cloned.1.call-update) | async-done | bytes 1310736 | tf_op jit(solution)/shard_map/all_gather | solution.py:119
  507.4 3.2 collective-permute-done.23
  517.4 4.7 collective-permute-done.25
  522.6 7.2 %collective-permute-start.27 = (f32[5,16,1,130]{3,1,0,2:T(8,128)S(1)}, f32[5,16,1,130]{3,1,0,2:T(8,128)S(1)}, u32[]{:S(2)}, u32[]{:S(2)}) collective-permute-start(f32[5,16,1,130]{3,1,0,2:T(8,128)S(1)} %get-tuple-element.5), channel_id=1, source_target_pairs={{1,0},{2,1},{3,2},{4,3},{5,4},{6,5},{7,6},{0,7},{9,8},{10,9},{11,1... | collective-permute-start | bytes 124808 | tf_op jit(solution)/shard_map/ppermute | solution.py:20
  533.3 53.8 %all-gather.23.cloned.1.call-done = f32[512,5,128]{2,0,1:T(8,128)} async-done(((f32[8,5,128]{2,0,1:T(8,128)}), f32[512,5,128]{2,0,1:T(8,128)}) %all-gather.23.cloned.1.call-update) | async-done | bytes 1310736 | tf_op jit(solution)/shard_map/all_gather | solution.py:122
  589.2 76.2 %all-gather.21.cloned.1.call-done = f32[512,5,128]{2,0,1:T(8,128)} async-done(((f32[8,5,128]{2,0,1:T(8,128)}), f32[512,5,128]{2,0,1:T(8,128)}) %all-gather.21.cloned.1.call-update) | async-done | bytes 1310736 | tf_op jit(solution)/shard_map/all_gather | solution.py:119
  (204 shorter events, 64.5 us)
Async XLA Ops:
  6.5 93.4 %all-gather.11.cloned.1.call-start = ((), (), s32[]{:S(2)}) async-start(), calls=%async_computation.1 | async-start | bytes 1331200 | tf_op jit(solution)/shard_map/all_gather | solution.py:122
  9.4 22.0 %collective-permute-start.6 = (f32[5,16,8,1]{3,1,0,2:T(8,128)S(1)}, f32[5,16,8,1]{3,1,0,2:T(8,128)S(1)}, u32[]{:S(2)}, u32[]{:S(2)}) collective-permute-start(f32[5,16,8,1]{3,1,0,2:T(8,128)S(1)} %get-tuple-element.30), channel_id=1, source_target_pairs={{8,0},{16,8},{24,16},{32,24},{40,32},{48,40},{56,48},{0,56},{9,1},... | collective-permute-start | bytes 7688 | tf_op jit(solution)/shard_map/ppermute | solution.py:20
  12.6 18.8 %collective-permute-start.5 = (f32[5,16,8,1]{3,1,0,2:T(8,128)S(1)}, f32[5,16,8,1]{3,1,0,2:T(8,128)S(1)}, u32[]{:S(2)}, u32[]{:S(2)}) collective-permute-start(f32[5,16,8,1]{3,1,0,2:T(8,128)S(1)} %get-tuple-element.29), channel_id=1, source_target_pairs={{0,8},{8,16},{16,24},{24,32},{32,40},{40,48},{48,56},{56,0},{1,9},... | collective-permute-start | bytes 7688 | tf_op jit(solution)/shard_map/ppermute | solution.py:19
  14.1 164.1 %all-gather.9.cloned.1.call-start = ((), (), s32[]{:S(2)}) async-start(), calls=%async_computation | async-start | bytes 1331200 | tf_op jit(solution)/shard_map/all_gather | solution.py:119
  14.4 6.8 %collective-permute-start.3 = (f32[3,16,8,1]{3,2,1,0:T(8,128)S(1)}, f32[3,16,8,1]{3,2,1,0:T(8,128)S(1)}, u32[]{:S(2)}, u32[]{:S(2)}) collective-permute-start(f32[3,16,8,1]{3,2,1,0:T(8,128)S(1)} %get-tuple-element.32), channel_id=1, source_target_pairs={{8,0},{16,8},{24,16},{32,24},{40,32},{48,40},{56,48},{0,56},{9,1},... | collective-permute-start | bytes 4616 | tf_op jit(solution)/shard_map/ppermute | solution.py:20
  22.3 240.2 %all-gather.15.cloned.1.call-start = ((), (), s32[]{:S(2)}) async-start(), calls=%async_computation.3 | async-start | bytes 1331200 | tf_op jit(solution)/shard_map/all_gather | solution.py:122
  22.9 18.4 %collective-permute-start.9 = (f32[3,16,1,130]{3,2,1,0:T(1,128)S(1)}, f32[3,16,1,130]{3,2,1,0:T(1,128)S(1)}, u32[]{:S(2)}, u32[]{:S(2)}) collective-permute-start(f32[3,16,1,130]{3,2,1,0:T(1,128)S(1)} %get-tuple-element.14), channel_id=1, source_target_pairs={{1,0},{2,1},{3,2},{4,3},{5,4},{6,5},{7,6},{0,7},{9,8},{10,9},{11,1... | collective-permute-start | bytes 74888 | tf_op jit(solution)/shard_map/ppermute | solution.py:20
  31.3 10.6 %collective-permute-start.4 = (f32[3,16,1,130]{3,2,1,0:T(1,128)S(1)}, f32[3,16,1,130]{3,2,1,0:T(1,128)S(1)}, u32[]{:S(2)}, u32[]{:S(2)}) collective-permute-start(f32[3,16,1,130]{3,2,1,0:T(1,128)S(1)} %get-tuple-element.13), channel_id=1, source_target_pairs={{0,1},{1,2},{2,3},{3,4},{4,5},{5,6},{6,7},{7,0},{8,9},{9,10},{10,1... | collective-permute-start | bytes 74888 | tf_op jit(solution)/shard_map/ppermute | solution.py:19
  31.5 11.3 %collective-permute-start.7 = (f32[5,16,1,130]{3,1,0,2:T(8,128)S(1)}, f32[5,16,1,130]{3,1,0,2:T(8,128)S(1)}, u32[]{:S(2)}, u32[]{:S(2)}) collective-permute-start(f32[5,16,1,130]{3,1,0,2:T(8,128)S(1)} %get-tuple-element.12), channel_id=1, source_target_pairs={{0,1},{1,2},{2,3},{3,4},{4,5},{5,6},{6,7},{7,0},{8,9},{9,10},{10,1... | collective-permute-start | bytes 124808 | tf_op jit(solution)/shard_map/ppermute | solution.py:19
  31.6 11.2 %collective-permute-start.8 = (f32[5,16,1,130]{3,1,0,2:T(8,128)S(1)}, f32[5,16,1,130]{3,1,0,2:T(8,128)S(1)}, u32[]{:S(2)}, u32[]{:S(2)}) collective-permute-start(f32[5,16,1,130]{3,1,0,2:T(8,128)S(1)} %get-tuple-element.11), channel_id=1, source_target_pairs={{1,0},{2,1},{3,2},{4,3},{5,4},{6,5},{7,6},{0,7},{9,8},{10,9},{11,1... | collective-permute-start | bytes 124808 | tf_op jit(solution)/shard_map/ppermute | solution.py:20
  186.7 154.0 %all-gather.13.cloned.1.call-start = ((), (), s32[]{:S(2)}) async-start(), calls=%async_computation.2 | async-start | bytes 1331200 | tf_op jit(solution)/shard_map/all_gather | solution.py:119
  190.1 234.7 %all-gather.19.cloned.1.call-start = ((), (), s32[]{:S(2)}) async-start(), calls=%async_computation.5 | async-start | bytes 1331200 | tf_op jit(solution)/shard_map/all_gather | solution.py:122
  190.4 7.3 %collective-permute-start.13 = (f32[5,16,8,1]{3,1,0,2:T(8,128)S(1)}, f32[5,16,8,1]{3,1,0,2:T(8,128)S(1)}, u32[]{:S(2)}, u32[]{:S(2)}) collective-permute-start(f32[5,16,8,1]{3,1,0,2:T(8,128)S(1)} %get-tuple-element.26), channel_id=1, source_target_pairs={{8,0},{16,8},{24,16},{32,24},{40,32},{48,40},{56,48},{0,56},{9,1},... | collective-permute-start | bytes 7688 | tf_op jit(solution)/shard_map/ppermute | solution.py:20
  197.8 10.0 %collective-permute-start.14 = (f32[5,16,1,130]{3,1,0,2:T(8,128)S(1)}, f32[5,16,1,130]{3,1,0,2:T(8,128)S(1)}, u32[]{:S(2)}, u32[]{:S(2)}) collective-permute-start(f32[5,16,1,130]{3,1,0,2:T(8,128)S(1)} %get-tuple-element.10), channel_id=1, source_target_pairs={{0,1},{1,2},{2,3},{3,4},{4,5},{5,6},{6,7},{7,0},{8,9},{9,10},{10,1... | collective-permute-start | bytes 124808 | tf_op jit(solution)/shard_map/ppermute | solution.py:19
  198.2 9.6 %collective-permute-start.15 = (f32[5,16,1,130]{3,1,0,2:T(8,128)S(1)}, f32[5,16,1,130]{3,1,0,2:T(8,128)S(1)}, u32[]{:S(2)}, u32[]{:S(2)}) collective-permute-start(f32[5,16,1,130]{3,1,0,2:T(8,128)S(1)} %get-tuple-element.9), channel_id=1, source_target_pairs={{1,0},{2,1},{3,2},{4,3},{5,4},{6,5},{7,6},{0,7},{9,8},{10,9},{11,1... | collective-permute-start | bytes 124808 | tf_op jit(solution)/shard_map/ppermute | solution.py:20
  349.0 154.0 %all-gather.17.cloned.1.call-start = ((), (), s32[]{:S(2)}) async-start(), calls=%async_computation.4 | async-start | bytes 1331200 | tf_op jit(solution)/shard_map/all_gather | solution.py:119
  352.4 234.7 %all-gather.23.cloned.1.call-start = ((), (), s32[]{:S(2)}) async-start(), calls=%async_computation.7 | async-start | bytes 1331200 | tf_op jit(solution)/shard_map/all_gather | solution.py:122
  352.6 7.3 %collective-permute-start.19 = (f32[5,16,8,1]{3,1,0,2:T(8,128)S(1)}, f32[5,16,8,1]{3,1,0,2:T(8,128)S(1)}, u32[]{:S(2)}, u32[]{:S(2)}) collective-permute-start(f32[5,16,8,1]{3,1,0,2:T(8,128)S(1)} %get-tuple-element.22), channel_id=1, source_target_pairs={{8,0},{16,8},{24,16},{32,24},{40,32},{48,40},{56,48},{0,56},{9,1},... | collective-permute-start | bytes 7688 | tf_op jit(solution)/shard_map/ppermute | solution.py:20
  360.1 9.8 %collective-permute-start.20 = (f32[5,16,1,130]{3,1,0,2:T(8,128)S(1)}, f32[5,16,1,130]{3,1,0,2:T(8,128)S(1)}, u32[]{:S(2)}, u32[]{:S(2)}) collective-permute-start(f32[5,16,1,130]{3,1,0,2:T(8,128)S(1)} %get-tuple-element.8), channel_id=1, source_target_pairs={{0,1},{1,2},{2,3},{3,4},{4,5},{5,6},{6,7},{7,0},{8,9},{9,10},{10,1... | collective-permute-start | bytes 124808 | tf_op jit(solution)/shard_map/ppermute | solution.py:19
  360.3 9.6 %collective-permute-start.21 = (f32[5,16,1,130]{3,1,0,2:T(8,128)S(1)}, f32[5,16,1,130]{3,1,0,2:T(8,128)S(1)}, u32[]{:S(2)}, u32[]{:S(2)}) collective-permute-start(f32[5,16,1,130]{3,1,0,2:T(8,128)S(1)} %get-tuple-element.7), channel_id=1, source_target_pairs={{1,0},{2,1},{3,2},{4,3},{5,4},{6,5},{7,6},{0,7},{9,8},{10,9},{11,1... | collective-permute-start | bytes 124808 | tf_op jit(solution)/shard_map/ppermute | solution.py:20
  511.3 154.1 %all-gather.21.cloned.1.call-start = ((), (), s32[]{:S(2)}) async-start(), calls=%async_computation.6 | async-start | bytes 1331200 | tf_op jit(solution)/shard_map/all_gather | solution.py:119
  514.9 7.2 %collective-permute-start.25 = (f32[5,16,8,1]{3,1,0,2:T(8,128)S(1)}, f32[5,16,8,1]{3,1,0,2:T(8,128)S(1)}, u32[]{:S(2)}, u32[]{:S(2)}) collective-permute-start(f32[5,16,8,1]{3,1,0,2:T(8,128)S(1)} %get-tuple-element.18), channel_id=1, source_target_pairs={{8,0},{16,8},{24,16},{32,24},{40,32},{48,40},{56,48},{0,56},{9,1},... | collective-permute-start | bytes 7688 | tf_op jit(solution)/shard_map/ppermute | solution.py:20
  522.2 9.8 %collective-permute-start.26 = (f32[5,16,1,130]{3,1,0,2:T(8,128)S(1)}, f32[5,16,1,130]{3,1,0,2:T(8,128)S(1)}, u32[]{:S(2)}, u32[]{:S(2)}) collective-permute-start(f32[5,16,1,130]{3,1,0,2:T(8,128)S(1)} %get-tuple-element.6), channel_id=1, source_target_pairs={{0,1},{1,2},{2,3},{3,4},{4,5},{5,6},{6,7},{7,0},{8,9},{9,10},{10,1... | collective-permute-start | bytes 124808 | tf_op jit(solution)/shard_map/ppermute | solution.py:19
  522.6 9.5 %collective-permute-start.27 = (f32[5,16,1,130]{3,1,0,2:T(8,128)S(1)}, f32[5,16,1,130]{3,1,0,2:T(8,128)S(1)}, u32[]{:S(2)}, u32[]{:S(2)}) collective-permute-start(f32[5,16,1,130]{3,1,0,2:T(8,128)S(1)} %get-tuple-element.5), channel_id=1, source_target_pairs={{1,0},{2,1},{3,2},{4,3},{5,4},{6,5},{7,6},{0,7},{9,8},{10,9},{11,1... | collective-permute-start | bytes 124808 | tf_op jit(solution)/shard_map/ppermute | solution.py:20
  (25 other events, 412.5 us)
Sparse Core Ops, SparseCore 0:
  14.2 85.6 all-gather.10
  103.3 74.8 all-gather.8
  186.8 75.6 all-gather.14
  265.8 74.8 all-gather.12
  349.1 75.6 all-gather.18
  428.0 74.8 all-gather.16
  511.4 75.6 all-gather.22
  590.5 74.8 all-gather.20
where the time goes:
time: 677 us; the launch traced here: 676 us
  waiting for transfers between devices  550 us (81%)
  starting transfers between devices  66.7 us (10%)
  matrix products  27.3 us (4%)
  between operations  14.4 us (2%)
  other arithmetic  14.3 us (2%)
    all_gather x4, waiting for transfers between devices, body(): lax.all_gather(donor_flow, ('row', 'rad'), axis=0, tiled=True)  304 us
    all_gather x4, waiting for transfers between devices, body(): lax.all_gather(donor_beyond, ('row', 'rad'), axis=0, tiled=True)  217 us
    ppermute x10, starting transfers between devices, padded_2(): after = lax.ppermute(first, axis, down)  51.3 us
    dot_general x8, matrix products, select_tiles(): jnp.einsum('tn,n...->t...', onehot, piece, precision=lax.Precision.HIGHEST)  14.8 us
    ppermute x10, waiting for transfers between devices, padded_2(): after = lax.ppermute(first, axis, down)  14.5 us
    ppermute x8, starting transfers between devices, shifted(): return lax.ppermute(shard, axis, pairs)  14 us
  transfers between devices with their start and end apart: 36, of which 21 were waited for; matrix products, arithmetic and copies ran while one was open for 4% of the time, Pallas kernels for 0%

commit v1 on v0

v1 whole, which is shorter than its diff:
```python
import functools

import jax
import jax.numpy as jnp
from jax import lax
from jax.experimental import pallas as pl
from jax.experimental.pallas import tpu as pltpu
from jax.sharding import PartitionSpec as P

STEPS = 4
time_step = 0.08
INTERPRET = False

NV = 5
TILE_ROWS = 48
FIELD_ROWS = 80
COEF_ROWS = 32
EDGE_ROWS = 8


def vmem():
    return pl.BlockSpec(memory_space=pltpu.VMEM)


def smem():
    return pl.BlockSpec(memory_space=pltpu.SMEM)


def call(kernel, outs, args, specs, name, flops=0, scratch=()):
    moved = sum(a.size * 4 for a in args) + sum(4 * functools.reduce(lambda x, y: x * y, o) for o in outs)
    return pl.pallas_call(
        kernel,
        out_shape=[jax.ShapeDtypeStruct(o, jnp.float32) for o in outs],
        in_specs=specs,
        out_specs=[vmem() for _ in outs],
        scratch_shapes=list(scratch),
        name=name,
        cost_estimate=pl.CostEstimate(flops=flops, bytes_accessed=moved, transcendentals=0),
        interpret=INTERPRET,
    )(*args)


def lanes_of(shape):
    return lax.broadcasted_iota(jnp.int32, shape, 1)


def rows_of(shape):
    return lax.broadcasted_iota(jnp.int32, shape, 0)


def roll(x, by, axis):
    size = x.shape[axis]
    if not isinstance(by, int):
        return pltpu.roll(x, lax.rem(by + 2 * size, size), axis)
    by %= size
    return x if by == 0 else pltpu.roll(x, by, axis)


def pressure(weight_ref, values):
    total = weight_ref[0] * values[0]
    for v in range(1, NV):
        total = total + weight_ref[v] * values[v]
    return total


def first_kernel(ids, weight, state, outflow, radial, circ, mu, halo, edges, down, up, out_pressure):
    planes = state.shape[1]
    lanes = lanes_of((8, 128))
    rows = rows_of((8, 128))
    casing = ids[2] == ids[3] - 1

    def one(k, carry):
        last, first = carry
        for v in range(NV):
            cell = state[v, k]
            at = v * 16 + k
            halo[0, pl.ds(at, 1), :] = cell[7:8]
            halo[1, pl.ds(at, 1), :] = cell[0:1]
            here = lanes == at
            last = jnp.where(here, roll(cell, at + 1, 1), last)
            first = jnp.where(here, roll(cell, at, 1), first)
        m, c = mu[k], circ[k]
        face = jnp.where(jnp.logical_and(casing, rows == 7), 0.0, radial[k])
        halo[0, pl.ds(80 + k, 1), :] = m[7:8]
        halo[1, pl.ds(80 + k, 1), :] = m[0:1]
        halo[0, pl.ds(96 + k, 1), :] = face[7:8]
        halo[1, pl.ds(96 + k, 1), :] = face[0:1]
        here = lanes == 80 + k
        last = jnp.where(here, roll(m, 81 + k, 1), last)
        first = jnp.where(here, roll(m, 80 + k, 1), first)
        here = lanes == 96 + k
        last = jnp.where(here, roll(c, 97 + k, 1), last)
        return last, first

    zero = jnp.zeros((8, 128), jnp.float32)
    last, first = lax.fori_loop(0, planes, one, (zero, zero))
    edges[0] = last
    edges[1] = first
    for v in range(NV):
        down[v] = state[v, planes - 1]
    up[...] = pressure(weight, [state[v, 0] for v in range(NV)])
    out_pressure[...] = pressure(weight, [outflow[v] for v in range(NV)])


def gather_kernel(ids, down, up, inflow, out_pressure, halo, send):
    section, rad = ids[0], ids[2]
    size = send.shape[0]
    halo_rows = halo.shape[1]
    for v in range(NV):
        value = jnp.where(section == 0, inflow[v], down[v])
        for j in range(size):
            send[j, v * 8 : v * 8 + 8, :] = value
    value = jnp.where(section == ids[4] - 1, out_pressure[...], up[...])
    for j in range(size):
        send[j, 40:48, :] = value

    @pl.when(rad < size - 1)
    def _():
        send[jnp.minimum(rad + 1, size - 1), 48 : 48 + halo_rows, :] = halo[0]

    @pl.when(rad > 0)
    def _():
        send[jnp.maximum(rad - 1, 0), 48 : 48 + halo_rows, :] = halo[1]


def select_kernel(ids, wanted, got, edges, send):
    size = send.shape[0]
    row = ids[1]

    def one(j, carry):
        for a in range(8):
            d = wanted[j, a] & 63
            r, b = d >> 3, d & 7
            for v in range(NV):
                send[j, v * 8 + a : v * 8 + a + 1, :] = got[r, pl.ds(v * 8 + b, 1), :]
            e = wanted[j, 8 + a] & 63
            send[j, 40 + a : 41 + a, :] = got[e >> 3, pl.ds(40 + (e & 7), 1), :]
        return carry

    lax.fori_loop(0, size, one, 0)
    send[lax.rem(row + 1, size), 48:56, :] = edges[0]
    send[lax.rem(row + size - 1, size), 48:56, :] = edges[1]


def coef_kernel(ids, volume, axial, radial, circ, mu, got, across, coef):
    row, rad = ids[1], ids[2]
    row_size, rad_size = ids[5], ids[3]
    planes = volume.shape[0]
    lanes = lanes_of((8, 128))
    rows = rows_of((8, 128))
    below, above = jnp.maximum(rad - 1, 0), jnp.minimum(rad + 1, rad_size - 1)
    left = across[lax.rem(row + row_size - 1, row_size), 48:56, :]
    right = across[lax.rem(row + 1, row_size), 48:56, :]

    def one(k, carry):
        m = mu[k]
        c = time_step / volume[k]
        half = 0.5 * c

        def put(at, area, viscous):
            coef[at, k] = half * area
            coef[at + 1, k] = c * area * viscous

        put(0, axial[jnp.maximum(k - 1, 0)], 0.5 * (m + mu[jnp.maximum(k - 1, 0)]))
        put(2, axial[k], 0.5 * (m + mu[jnp.minimum(k + 1, planes - 1)]))
        face = jnp.where(jnp.logical_and(rad == rad_size - 1, rows == 7), 0.0, radial[k])
        mu_below = jnp.where(rad == 0, m, jnp.broadcast_to(got[below, pl.ds(128 + k, 1), :], (8, 128)))
        mu_above = jnp.where(rad == rad_size - 1, m, jnp.broadcast_to(got[above, pl.ds(128 + k, 1), :], (8, 128)))
        face_below = jnp.where(rad == 0, 0.0, jnp.broadcast_to(got[below, pl.ds(144 + k, 1), :], (8, 128)))
        put(4, jnp.where(rows == 0, face_below, roll(face, 1, 0)), 0.5 * (m + jnp.where(rows == 0, mu_below, roll(m, 1, 0))))
        put(6, face, 0.5 * (m + jnp.where(rows == 7, mu_above, roll(m, 7, 0))))
        around = circ[k]
        at = 80 + k
        mu_left = jnp.where(lanes == 0, roll(left, -at, 1), roll(m, 1, 1))
        mu_right = jnp.where(lanes == 127, roll(right, 127 - at, 1), roll(m, 127, 1))
        circ_left = jnp.where(lanes == 0, roll(left, -(at + 16), 1), roll(around, 1, 1))
        put(8, circ_left, 0.5 * (mu_left + m))
        put(10, around, 0.5 * (m + mu_right))
        return carry

    lax.fori_loop(0, planes, one, 0)


def update_kernel(last_step, ids, donors, weight, coupling, state, coef, matrix, got, across, *outs):
    if last_step:
        new, ghost = outs
    else:
        new, halo, edges, down, up, ghost = outs
    row, rad = ids[1], ids[2]
    row_size, rad_size = ids[5], ids[3]
    planes = state.shape[1]
    lanes = lanes_of((8, 128))
    rows = rows_of((8, 128))
    below, above = jnp.maximum(rad - 1, 0), jnp.minimum(rad + 1, rad_size - 1)
    wall_below, wall_above = rad == 0, rad == rad_size - 1
    left = across[lax.rem(row + row_size - 1, row_size), 48:56, :]
    right = across[lax.rem(row + 1, row_size), 48:56, :]
    for a in range(8):
        d = donors[a] >> 6
        for v in range(NV):
            ghost[v, a : a + 1, :] = across[d, v * 8 + a : v * 8 + a + 1, :]
        e = donors[8 + a] >> 6
        ghost[NV, a : a + 1, :] = across[e, 40 + a : 41 + a, :]
    outlet = [state[v, planes - 1] for v in range(NV)]
    jump = ghost[NV] - pressure(weight, outlet)
    outlet_ghost = [outlet[v] + coupling[v] * jump for v in range(NV)]

    def one(k, carry, after=None):
        before, here, last, first = carry
        if after is None:
            after = [state[v, k + 1] for v in range(NV)]
        total = list(here)
        for d in range(3):
            low_a, low_b = coef[4 * d, k], coef[4 * d + 1, k]
            high_a, high_b = coef[4 * d + 2, k], coef[4 * d + 3, k]
            mixed = []
            for v in range(NV):
                cell = here[v]
                at = v * 16 + k
                if d == 0:
                    lower, upper = before[v], after[v]
                elif d == 1:
                    low = jnp.broadcast_to(got[below, pl.ds(48 + at, 1), :], (8, 128))
                    high = jnp.broadcast_to(got[above, pl.ds(48 + at, 1), :], (8, 128))
                    low = jnp.where(wall_below, cell, low)
                    high = jnp.where(wall_above, cell, high)
                    lower = jnp.where(rows == 0, low, roll(cell, 1, 0))
                    upper = jnp.where(rows == 7, high, roll(cell, 7, 0))
                else:
                    lower = jnp.where(lanes == 0, roll(left, -at, 1), roll(cell, 1, 1))
                    upper = jnp.where(lanes == 127, roll(right, 127 - at, 1), roll(cell, 127, 1))
                mixed.append(high_a * (cell + upper) - low_a * (lower + cell))
                total[v] = total[v] + (high_b * (upper - cell) - low_b * (cell - lower))
            for u in range(NV):
                flow = matrix[25 * d + 5 * u] * mixed[0]
                for v in range(1, NV):
                    flow = flow + matrix[25 * d + 5 * u + v] * mixed[v]
                total[u] = total[u] - flow
        for v in range(NV):
            new[v, k] = total[v]
            if not last_step:
                at = v * 16 + k
                halo[0, pl.ds(at, 1), :] = total[v][7:8]
                halo[1, pl.ds(at, 1), :] = total[v][0:1]
                spot = lanes == at
                last = jnp.where(spot, roll(total[v], at + 1, 1), last)
                first = jnp.where(spot, roll(total[v], at, 1), first)
        return here, after, last, first

    zero = jnp.zeros((8, 128), jnp.float32)
    carry = ([ghost[v] for v in range(NV)], [state[v, 0] for v in range(NV)], zero, zero)
    carry = lax.fori_loop(0, planes - 1, one, carry)
    _, _, last, first = one(planes - 1, carry, outlet_ghost)
    if not last_step:
        edges[0] = last
        edges[1] = first
        for v in range(NV):
            down[v] = new[v, planes - 1]
        up[...] = pressure(weight, [new[v, 0] for v in range(NV)])


def body(
    state,
    volume,
    face_axial,
    face_radial,
    face_circum,
    viscosity,
    flux_matrix,
    inflow_plane,
    outflow_plane,
    down_donors,
    up_donors,
    pressure_weight,
    boundary_coupling,
):
    sections, row_size, rad_size = lax.axis_size("sec"), lax.axis_size("row"), lax.axis_size("rad")
    ids = jnp.stack(
        [
            lax.axis_index("sec"),
            lax.axis_index("row"),
            lax.axis_index("rad"),
            jnp.int32(rad_size),
            jnp.int32(sections),
            jnp.int32(row_size),
        ]
    ).astype(jnp.int32)
    field = state[:, 0]
    planes = field.shape[1]
    volume, axial, radial, circ, mu = volume[0], face_axial[0], face_radial[0], face_circum[0], viscosity[0]
    donors = jnp.concatenate([down_donors[0], up_donors[0]])
    mine = jnp.broadcast_to(jnp.pad(donors, (0, 112))[None, None], (row_size, 8, 128))
    wanted = lax.all_to_all(mine, "row", 0, 0)[:, 0, :16]
    matrix = jnp.broadcast_to(flux_matrix[0].reshape(75)[:, None, None], (75, 8, 128))
    plane = (NV, 8, 128)
    strips = (2, 8, 128)

    halo, edges, down, up, out_pressure = call(
        first_kernel,
        [(2, FIELD_ROWS + COEF_ROWS, 128), strips, plane, (8, 128), (8, 128)],
        [ids, pressure_weight, field, outflow_plane, radial, circ, mu],
        [smem(), smem()] + [vmem()] * 5,
        "first",
    )
    forward = [(i, i + 1) for i in range(sections - 1)]
    backward = [(i + 1, i) for i in range(sections - 1)]
    coef = None
    for step in range(STEPS):
        last_step = step == STEPS - 1
        down = lax.ppermute(down, "sec", forward)
        up = lax.ppermute(up, "sec", backward)
        (send,) = call(
            gather_kernel,
            [(rad_size, TILE_ROWS + halo.shape[1], 128)],
            [ids, down, up, inflow_plane, out_pressure, halo],
            [smem()] + [vmem()] * 5,
            "gather",
        )
        got = lax.all_to_all(send, "rad", 0, 0)
        (send,) = call(
            select_kernel,
            [(row_size, TILE_ROWS + EDGE_ROWS, 128)],
            [ids, wanted, got, edges],
            [smem(), smem()] + [vmem()] * 2,
            "select",
        )
        across = lax.all_to_all(send, "row", 0, 0)
        if step == 0:
            (coef,) = call(
                coef_kernel,
                [(12, planes, 8, 128)],
                [ids, volume, axial, radial, circ, mu, got, across],
                [smem()] + [vmem()] * 7,
                "coef",
            )
        outs = [(NV, planes, 8, 128)]
        if not last_step:
            outs += [(2, FIELD_ROWS, 128), strips, plane, (8, 128)]
        result = call(
            functools.partial(update_kernel, last_step),
            outs,
            [ids, donors, pressure_weight, boundary_coupling, field, coef, matrix, got, across],
            [smem()] * 4 + [vmem()] * 5,
            "update_last" if last_step else "update",
            flops=planes * 1024 * 350,
            scratch=[pltpu.VMEM((NV + 1, 8, 128), jnp.float32)],
        )
        field = result[0]
        if not last_step:
            halo, edges, down, up = result[1:]
    return field[:, None]


def solution(mesh):
    in_specs = (
        P(None, "sec", None, "rad", "row"),
        P("sec", None, "rad", "row"),
        P("sec", None, "rad", "row"),
        P("sec", None, "rad", "row"),
        P("sec", None, "rad", "row"),
        P("sec", None, "rad", "row"),
        P("sec", None, None, None),
        P(None, "rad", "row"),
        P(None, "rad", "row"),
        P("sec", ("row", "rad")),
        P("sec", ("row", "rad")),
        P(),
        P(),
    )
    out_specs = P(None, "sec", None, "rad", "row")
    return jax.shard_map(body, mesh=mesh, in_specs=in_specs, out_specs=out_specs, check_vma=False)
```

time: 677 us -> 229 us (0.34)
  waiting for transfers between devices: 550 us -> 31.2 us
  blocking collectives: 0 us -> 94.9 us
  Pallas kernels: 0 us -> 41.4 us
  matrix products: 27.3 us -> 0 us
  starting transfers between devices: 66.7 us -> 51 us
  between operations: 14.4 us -> 0.11 us
  other arithmetic: 14.3 us -> 0.1 us
    all_gather x8 -> x0, waiting for transfers between devices: 521 us -> none  [the longest x4 304 us: body(): lax.all_gather(donor_flow, ('row', 'rad'), axis=0, tiled=True)]
    all_to_all x0 -> x6, blocking collectives: none -> 94.9 us  [the longest x3 47.9 us: body(): across = lax.all_to_all(send, 'row', 0, 0)]
    ppermute x28 -> x8, starting transfers between devices: 66.4 us -> 22.6 us  [the longest x4 17.5 us: body(): down = lax.ppermute(down, 'sec', forward)]
    pallas_call x0 -> x14, Pallas kernels: none -> 41.4 us  [call(): pl.pallas_call(kernel, out_shape=[jax.ShapeDtypeStruct(o, jnp.float32) fo...]
    all_to_all x0 -> x3, starting transfers between devices: none -> 28.4 us  [the longest x1 12.4 us: body(): across = lax.all_to_all(send, 'row', 0, 0)]
    dot_general x28 -> x0, matrix products: 27.3 us -> none  [the longest x8 14.8 us: select_tiles(): jnp.einsum('tn,n...->t...', onehot, piece, precision=lax.Precision.HIGHEST)]
    all_to_all x0 -> x3, waiting for transfers between devices: none -> 18 us  [the longest x1 12 us: body(): got = lax.all_to_all(send, 'rad', 0, 0)]
    ppermute x28 -> x8, waiting for transfers between devices: 29 us -> 13.2 us  [the longest x4 13.2 us: body(): up = lax.ppermute(up, 'sec', backward)]
  transfers between devices with their start and end apart: 36 -> 11, of which waited for: 21 -> 6; matrix products, arithmetic and copies ran while one was open for 4% -> 1% of each run, Pallas kernels for 0% -> 2%
where the time goes in v1:
time: 229 us; the launch traced here: 227 us
  blocking collectives  94.9 us (41%)
  starting transfers between devices  51 us (22%)
  Pallas kernels  41.4 us (18%)
  waiting for transfers between devices  31.2 us (14%)
  local copies, waits for them, and re-layouts  8 us (3%)
    all_to_all x3, blocking collectives, body(): across = lax.all_to_all(send, 'row', 0, 0)  47.9 us
    all_to_all x3, blocking collectives, body(): got = lax.all_to_all(send, 'rad', 0, 0)  47 us
    pallas_call x14, Pallas kernels, call(): pl.pallas_call(kernel, out_shape=[jax.ShapeDtypeStruct(o, jnp.float32) fo...  41.4 us
    ppermute x4, starting transfers between devices, body(): down = lax.ppermute(down, 'sec', forward)  17.5 us
    ppermute x4, waiting for transfers between devices, body(): up = lax.ppermute(up, 'sec', backward)  13.2 us
    all_to_all x1, starting transfers between devices, body(): across = lax.all_to_all(send, 'row', 0, 0)  12.4 us
    all_to_all x1, waiting for transfers between devices, body(): got = lax.all_to_all(send, 'rad', 0, 0)  12 us
    all_to_all x1, starting transfers between devices, body(): got = lax.all_to_all(send, 'rad', 0, 0)  9.57 us
  transfers between devices with their start and end apart: 11, of which 6 were waited for; matrix products, arithmetic and copies ran while one was open for 1% of the time, Pallas kernels for 2%

profile of v1, /device:TPU:1, one launch (start us, length us, event | category | flops | bytes accessed | tf_op | source)
XLA Modules:
  0.0 226.8 jit_solution(4128661366035440554)
XLA Ops:
  1.9 6.4 %all-to-all-start.1 = ((s32[8,8,128]{2,1,0:T(8,128)}), s32[8,8,128]{2,1,0:T(8,128)S(1)}, u32[]{:S(2)}, u32[]{:S(2)}) async-start(s32[8,8,128]{2,1,0:T(8,128)} %broadcast_in_dim.16), calls=%async_computation.1 | async-start | bytes 65536 | tf_op jit(solution)/shard_map/all_to_all | solution.py:293
  9.0 3.2 %first.1 = (f32[2,112,128]{2,1,0:T(8,128)}, f32[2,8,128]{2,1,0:T(8,128)}, f32[5,8,128]{2,1,0:T(8,128)}, f32[8,128]{1,0:T(8,128)}, f32[8,128]{1,0:T(8,128)}) custom-call(s32[6]{0:T(128)} %stack.15.ids, f32[5]{0:T(128)} %weight.9, f32[5,16,8,128]{3,2,1,0:T(8,128)} %bitcast.17, f32[5,8,128]{2,1,0:T(8,128)} %outflow.1, f32[16,8,128]{2,1,0:T(8,128)} %bitcast.19, ...), custom_call_target="tpu_custom_call" | custom-call | bytes 696364 | tf_op jit(solution)/shard_map/first/pallas_call | solution.py:31
  16.5 3.4 %collective-permute-done.1.up = f32[8,128]{1,0:T(8,128)S(1)} collective-permute-done((f32[8,128]{1,0:T(8,128)}, f32[8,128]{1,0:T(8,128)S(1)}, u32[]{:S(2)}, u32[]{:S(2)}) %collective-permute-start.1) | collective-permute-done | bytes 4128 | tf_op jit(solution)/shard_map/ppermute | solution.py:311
  22.4 9.6 %all-to-all-start = ((f32[8,160,128]{2,1,0:T(8,128)}), f32[8,160,128]{2,1,0:T(8,128)S(1)}, u32[]{:S(2)}, u32[]{:S(2)}) async-start(f32[8,160,128]{2,1,0:T(8,128)} %gather.4), calls=%async_computation | async-start | bytes 1310720 | tf_op jit(solution)/shard_map/all_to_all | solution.py:319
  32.6 12.0 %all-to-all-done.got = f32[8,160,128]{2,1,0:T(8,128)S(1)} async-done(((f32[8,160,128]{2,1,0:T(8,128)}), f32[8,160,128]{2,1,0:T(8,128)S(1)}, u32[]{:S(2)}, u32[]{:S(2)}) %all-to-all-start) | async-done | bytes 655392 | tf_op jit(solution)/shard_map/all_to_all | solution.py:319
  47.5 12.4 %all-to-all-start.2 = ((f32[8,56,128]{2,1,0:T(8,128)}), f32[8,56,128]{2,1,0:T(8,128)S(1)}, u32[]{:S(2)}, u32[]{:S(2)}) async-start(f32[8,56,128]{2,1,0:T(8,128)} %select.5), calls=%async_computation.2 | async-start | bytes 458752 | tf_op jit(solution)/shard_map/all_to_all | solution.py:327
  60.0 6.0 %all-to-all-done.2.across = f32[8,56,128]{2,1,0:T(8,128)S(1)} async-done(((f32[8,56,128]{2,1,0:T(8,128)}), f32[8,56,128]{2,1,0:T(8,128)S(1)}, u32[]{:S(2)}, u32[]{:S(2)}) %all-to-all-start.2) | async-done | bytes 229408 | tf_op jit(solution)/shard_map/all_to_all | solution.py:327
  66.8 3.6 %coef.1 = f32[12,16,8,128]{3,2,1,0:T(8,128)} custom-call(s32[6]{0:T(128)} %stack.15.ids, f32[16,8,128]{2,1,0:T(8,128)} %bitcast.29, f32[16,8,128]{2,1,0:T(8,128)} %bitcast.30, f32[16,8,128]{2,1,0:T(8,128)} %bitcast.20, f32[16,8,128]{2,1,0:T(8,128)} %bitcast.22, f32[16,8,128]{2,1,0:T(8,128)} %bitcast.24, f32[8,160,128]{2,1,0:T(8,128)} %copy-done, ...), custom_call_target="tpu_custom_call" | custom-call | bytes 1998872 | tf_op jit(solution)/shard_map/coef/pallas_call | solution.py:31
  71.2 5.1 %update.3 = (f32[5,16,8,128]{3,2,1,0:T(8,128)}, f32[2,80,128]{2,1,0:T(8,128)}, f32[2,8,128]{2,1,0:T(8,128)}, f32[5,8,128]{2,1,0:T(8,128)}, f32[8,128]{1,0:T(8,128)}) custom-call(s32[6]{0:T(128)} %stack.15.ids, s32[16]{0:T(128)} %copy-done.6, f32[5]{0:T(128)} %weight.9, f32[5]{0:T(128)} %coupling.7, f32[5,16,8,128]{3,2,1,0:T(8,128)} %bitcast.18, ...), custom_call_target="tpu_custom_call" | custom-call | flops 5734400 | bytes 2748544 | tf_op jit(solution)/shard_map/update/pallas_call | solution.py:31
  76.3 4.1 %collective-permute-start.2 = (f32[5,8,128]{2,1,0:T(8,128)}, f32[5,8,128]{2,1,0:T(8,128)S(1)}, u32[]{:S(2)}, u32[]{:S(2)}) collective-permute-start(f32[5,8,128]{2,1,0:T(8,128)} %get-tuple-element.31), channel_id=1, source_target_pairs={{0,64},{64,128},{128,192},{1,65},{65,129},{129,193},{2,66},{66,130... | collective-permute-start | bytes 61448 | tf_op jit(solution)/shard_map/ppermute | solution.py:310
  81.7 3.3 %collective-permute-done.3.up = f32[8,128]{1,0:T(8,128)S(1)} collective-permute-done((f32[8,128]{1,0:T(8,128)}, f32[8,128]{1,0:T(8,128)S(1)}, u32[]{:S(2)}, u32[]{:S(2)}) %collective-permute-start.3) | collective-permute-done | bytes 4128 | tf_op jit(solution)/shard_map/ppermute | solution.py:311
  87.4 15.7 %all_to_all.45.got = f32[8,128,128]{2,1,0:T(8,128)} all-to-all(f32[8,128,128]{2,1,0:T(8,128)} %gather.5), channel_id=1, replica_groups=mesh['sec'=4,'row'=8,'rad'=8] {'rad'}, dimensions={0} | all-to-all | bytes 1048576 | tf_op jit(solution)/shard_map/all_to_all | solution.py:319
  105.2 16.1 %all_to_all.46.across = f32[8,56,128]{2,1,0:T(8,128)} all-to-all(f32[8,56,128]{2,1,0:T(8,128)} %select.6), channel_id=1, replica_groups=mesh['sec'=4,'row'=8,'rad'=8] {'row'}, dimensions={0} | all-to-all | bytes 458752 | tf_op jit(solution)/shard_map/all_to_all | solution.py:327
  121.3 5.0 %update.4 = (f32[5,16,8,128]{3,2,1,0:T(8,128)}, f32[2,80,128]{2,1,0:T(8,128)}, f32[2,8,128]{2,1,0:T(8,128)}, f32[5,8,128]{2,1,0:T(8,128)}, f32[8,128]{1,0:T(8,128)}) custom-call(s32[6]{0:T(128)} %stack.15.ids, s32[16]{0:T(128)} %copy-done.6, f32[5]{0:T(128)} %weight.9, f32[5]{0:T(128)} %coupling.7, f32[5,16,8,128]{3,2,1,0:T(8,128)} %get-tuple-element.30.state, ...), custom_call_target="tpu_custom_call" | custom-call | flops 5734400 | bytes 2617472 | tf_op jit(solution)/shard_map/update/pallas_call | solution.py:31
  126.3 5.1 %collective-permute-start.4 = (f32[5,8,128]{2,1,0:T(8,128)}, f32[5,8,128]{2,1,0:T(8,128)S(1)}, u32[]{:S(2)}, u32[]{:S(2)}) collective-permute-start(f32[5,8,128]{2,1,0:T(8,128)} %get-tuple-element.36), channel_id=1, source_target_pairs={{0,64},{64,128},{128,192},{1,65},{65,129},{129,193},{2,66},{66,130... | collective-permute-start | bytes 61448 | tf_op jit(solution)/shard_map/ppermute | solution.py:310
  132.8 3.3 %collective-permute-done.5.up = f32[8,128]{1,0:T(8,128)S(1)} collective-permute-done((f32[8,128]{1,0:T(8,128)}, f32[8,128]{1,0:T(8,128)S(1)}, u32[]{:S(2)}, u32[]{:S(2)}) %collective-permute-start.5) | collective-permute-done | bytes 4128 | tf_op jit(solution)/shard_map/ppermute | solution.py:311
  138.4 15.6 %all_to_all.47.got = f32[8,128,128]{2,1,0:T(8,128)} all-to-all(f32[8,128,128]{2,1,0:T(8,128)} %gather.6), channel_id=1, replica_groups=mesh['sec'=4,'row'=8,'rad'=8] {'rad'}, dimensions={0} | all-to-all | bytes 1048576 | tf_op jit(solution)/shard_map/all_to_all | solution.py:319
  156.2 15.9 %all_to_all.48.across = f32[8,56,128]{2,1,0:T(8,128)} all-to-all(f32[8,56,128]{2,1,0:T(8,128)} %select.7), channel_id=1, replica_groups=mesh['sec'=4,'row'=8,'rad'=8] {'row'}, dimensions={0} | all-to-all | bytes 458752 | tf_op jit(solution)/shard_map/all_to_all | solution.py:327
  172.1 5.0 %update.5 = (f32[5,16,8,128]{3,2,1,0:T(8,128)}, f32[2,80,128]{2,1,0:T(8,128)}, f32[2,8,128]{2,1,0:T(8,128)}, f32[5,8,128]{2,1,0:T(8,128)}, f32[8,128]{1,0:T(8,128)}) custom-call(s32[6]{0:T(128)} %stack.15.ids, s32[16]{0:T(128)} %copy-done.6, f32[5]{0:T(128)} %weight.9, f32[5]{0:T(128)} %coupling.7, f32[5,16,8,128]{3,2,1,0:T(8,128)} %get-tuple-element.35.state, ...), custom_call_target="tpu_custom_call" | custom-call | flops 5734400 | bytes 2617472 | tf_op jit(solution)/shard_map/update/pallas_call | solution.py:31
  177.2 5.1 %collective-permute-start.6 = (f32[5,8,128]{2,1,0:T(8,128)}, f32[5,8,128]{2,1,0:T(8,128)S(1)}, u32[]{:S(2)}, u32[]{:S(2)}) collective-permute-start(f32[5,8,128]{2,1,0:T(8,128)} %get-tuple-element.41), channel_id=1, source_target_pairs={{0,64},{64,128},{128,192},{1,65},{65,129},{129,193},{2,66},{66,130... | collective-permute-start | bytes 61448 | tf_op jit(solution)/shard_map/ppermute | solution.py:310
  183.6 3.3 %collective-permute-done.7.up = f32[8,128]{1,0:T(8,128)S(1)} collective-permute-done((f32[8,128]{1,0:T(8,128)}, f32[8,128]{1,0:T(8,128)S(1)}, u32[]{:S(2)}, u32[]{:S(2)}) %collective-permute-start.7) | collective-permute-done | bytes 4128 | tf_op jit(solution)/shard_map/ppermute | solution.py:311
  189.2 15.6 %all_to_all.49.got = f32[8,128,128]{2,1,0:T(8,128)} all-to-all(f32[8,128,128]{2,1,0:T(8,128)} %gather.7), channel_id=1, replica_groups=mesh['sec'=4,'row'=8,'rad'=8] {'rad'}, dimensions={0} | all-to-all | bytes 1048576 | tf_op jit(solution)/shard_map/all_to_all | solution.py:319
  207.0 15.9 %all_to_all.50.across = f32[8,56,128]{2,1,0:T(8,128)} all-to-all(f32[8,56,128]{2,1,0:T(8,128)} %select.8), channel_id=1, replica_groups=mesh['sec'=4,'row'=8,'rad'=8] {'row'}, dimensions={0} | all-to-all | bytes 458752 | tf_op jit(solution)/shard_map/all_to_all | solution.py:327
  222.9 3.9 %update_last.1 = f32[5,16,8,128]{3,2,1,0:T(8,128)} custom-call(s32[6]{0:T(128)} %stack.15.ids, s32[16]{0:T(128)} %copy-done.6, f32[5]{0:T(128)} %weight.9, f32[5]{0:T(128)} %coupling.7, f32[5,16,8,128]{3,2,1,0:T(8,128)} %get-tuple-element.40.state, f32[12,16,8,128]{3,2,1,0:T(8,128)} %coef.1, f32[75,8,128]{2,1,0:T(8,128)} %broadcast_in_dim.18.matrix, ...), custom_call_target="tpu_custom_call" | custom-call | flops 5734400 | bytes 2502784 | tf_op jit(solution)/shard_map/update_last/pallas_call | solution.py:31
  (54 shorter events, 32.0 us)
Async XLA Ops:
  0.0 0.7 copy-start.12
  0.0 0.7 copy-start.13
  1.9 20.5 %all-to-all-start.1 = ((s32[8,8,128]{2,1,0:T(8,128)}), s32[8,8,128]{2,1,0:T(8,128)S(1)}, u32[]{:S(2)}, u32[]{:S(2)}) async-start(s32[8,8,128]{2,1,0:T(8,128)} %broadcast_in_dim.16), calls=%async_computation.1 | async-start | bytes 65536 | tf_op jit(solution)/shard_map/all_to_all | solution.py:293
  12.2 7.8 %collective-permute-start = (f32[5,8,128]{2,1,0:T(8,128)}, f32[5,8,128]{2,1,0:T(8,128)S(1)}, u32[]{:S(2)}, u32[]{:S(2)}) collective-permute-start(f32[5,8,128]{2,1,0:T(8,128)} %get-tuple-element.25), channel_id=1, source_target_pairs={{0,64},{64,128},{128,192},{1,65},{65,129},{129,193},{2,66},{66,130... | collective-permute-start | bytes 61448 | tf_op jit(solution)/shard_map/ppermute | solution.py:310
  15.2 4.7 %collective-permute-start.1 = (f32[8,128]{1,0:T(8,128)}, f32[8,128]{1,0:T(8,128)S(1)}, u32[]{:S(2)}, u32[]{:S(2)}) collective-permute-start(f32[8,128]{1,0:T(8,128)} %get-tuple-element.26), channel_id=1, source_target_pairs={{64,0},{128,64},{192,128},{65,1},{129,65},{193,129},{66,2},{130,66... | collective-permute-start | bytes 12296 | tf_op jit(solution)/shard_map/ppermute | solution.py:311
  20.0 0.6 copy-start.9
  20.0 0.6 copy-start.3
  22.4 22.1 %all-to-all-start = ((f32[8,160,128]{2,1,0:T(8,128)}), f32[8,160,128]{2,1,0:T(8,128)S(1)}, u32[]{:S(2)}, u32[]{:S(2)}) async-start(f32[8,160,128]{2,1,0:T(8,128)} %gather.4), calls=%async_computation | async-start | bytes 1310720 | tf_op jit(solution)/shard_map/all_to_all | solution.py:319
  44.5 0.9 copy-start
  47.5 12.4 %copy-start.7 = (f32[1,3,5,5]{3,0,2,1:T(1,128)S(1)}, f32[1,3,5,5]{3,0,2,1:T(1,128)}, u32[]{:S(2)}) copy-start(f32[1,3,5,5]{3,0,2,1:T(1,128)} %param.19) | copy-start | bytes 904
  47.5 18.5 %all-to-all-start.2 = ((f32[8,56,128]{2,1,0:T(8,128)}), f32[8,56,128]{2,1,0:T(8,128)S(1)}, u32[]{:S(2)}, u32[]{:S(2)}) async-start(f32[8,56,128]{2,1,0:T(8,128)} %select.5), calls=%async_computation.2 | async-start | bytes 458752 | tf_op jit(solution)/shard_map/all_to_all | solution.py:327
  66.1 0.7 copy-start.1
  76.3 8.7 %collective-permute-start.2 = (f32[5,8,128]{2,1,0:T(8,128)}, f32[5,8,128]{2,1,0:T(8,128)S(1)}, u32[]{:S(2)}, u32[]{:S(2)}) collective-permute-start(f32[5,8,128]{2,1,0:T(8,128)} %get-tuple-element.31), channel_id=1, source_target_pairs={{0,64},{64,128},{128,192},{1,65},{65,129},{129,193},{2,66},{66,130... | collective-permute-start | bytes 61448 | tf_op jit(solution)/shard_map/ppermute | solution.py:310
  80.4 4.6 %collective-permute-start.3 = (f32[8,128]{1,0:T(8,128)}, f32[8,128]{1,0:T(8,128)S(1)}, u32[]{:S(2)}, u32[]{:S(2)}) collective-permute-start(f32[8,128]{1,0:T(8,128)} %get-tuple-element.32), channel_id=1, source_target_pairs={{64,0},{128,64},{192,128},{65,1},{129,65},{193,129},{66,2},{130,66... | collective-permute-start | bytes 12296 | tf_op jit(solution)/shard_map/ppermute | solution.py:311
  85.0 0.6 copy-start.10
  85.0 0.6 copy-start.4
  126.3 9.7 %collective-permute-start.4 = (f32[5,8,128]{2,1,0:T(8,128)}, f32[5,8,128]{2,1,0:T(8,128)S(1)}, u32[]{:S(2)}, u32[]{:S(2)}) collective-permute-start(f32[5,8,128]{2,1,0:T(8,128)} %get-tuple-element.36), channel_id=1, source_target_pairs={{0,64},{64,128},{128,192},{1,65},{65,129},{129,193},{2,66},{66,130... | collective-permute-start | bytes 61448 | tf_op jit(solution)/shard_map/ppermute | solution.py:310
  131.5 4.6 %collective-permute-start.5 = (f32[8,128]{1,0:T(8,128)}, f32[8,128]{1,0:T(8,128)S(1)}, u32[]{:S(2)}, u32[]{:S(2)}) collective-permute-start(f32[8,128]{1,0:T(8,128)} %get-tuple-element.37), channel_id=1, source_target_pairs={{64,0},{128,64},{192,128},{65,1},{129,65},{193,129},{66,2},{130,66... | collective-permute-start | bytes 12296 | tf_op jit(solution)/shard_map/ppermute | solution.py:311
  136.0 0.6 copy-start.11
  136.0 0.6 copy-start.5
  177.2 9.7 %collective-permute-start.6 = (f32[5,8,128]{2,1,0:T(8,128)}, f32[5,8,128]{2,1,0:T(8,128)S(1)}, u32[]{:S(2)}, u32[]{:S(2)}) collective-permute-start(f32[5,8,128]{2,1,0:T(8,128)} %get-tuple-element.41), channel_id=1, source_target_pairs={{0,64},{64,128},{128,192},{1,65},{65,129},{129,193},{2,66},{66,130... | collective-permute-start | bytes 61448 | tf_op jit(solution)/shard_map/ppermute | solution.py:310
  182.3 4.6 %collective-permute-start.7 = (f32[8,128]{1,0:T(8,128)}, f32[8,128]{1,0:T(8,128)S(1)}, u32[]{:S(2)}, u32[]{:S(2)}) collective-permute-start(f32[8,128]{1,0:T(8,128)} %get-tuple-element.42), channel_id=1, source_target_pairs={{64,0},{128,64},{192,128},{65,1},{129,65},{193,129},{66,2},{130,66... | collective-permute-start | bytes 12296 | tf_op jit(solution)/shard_map/ppermute | solution.py:311
  186.9 0.6 copy-start.8
  186.9 0.6 copy-start.2
  (1 other events, 0.6 us)

commit v2 on v1

--- a/solution.py
+++ b/solution.py
@@ -10,6 +10,7 @@
 STEPS = 4
 time_step = 0.08
 INTERPRET = False
+VMEM_LIMIT = 6 * 1024 * 1024
 
 NV = 5
 TILE_ROWS = 48
@@ -35,6 +36,7 @@
         out_specs=[vmem() for _ in outs],
         scratch_shapes=list(scratch),
         name=name,
+        compiler_params=pltpu.CompilerParams(vmem_limit_bytes=VMEM_LIMIT),
         cost_estimate=pl.CostEstimate(flops=flops, bytes_accessed=moved, transcendentals=0),
         interpret=INTERPRET,
     )(*args)

time: 229 us -> 200 us (0.87)
  Pallas kernels: 41.4 us -> 24.7 us
  blocking collectives: 94.9 us -> 85.4 us
  local copies, waits for them, and re-layouts: 8 us -> 5.32 us
    pallas_call x14, Pallas kernels: 41.4 us -> 24.7 us  [call(): pl.pallas_call(kernel, out_shape=[jax.ShapeDtypeStruct(o, jnp.float32) fo...]
    all_to_all x3, blocking collectives: 47.9 us -> 43 us  [body(): across = lax.all_to_all(send, 'row', 0, 0)]
    all_to_all x3, blocking collectives: 47 us -> 42.4 us  [body(): got = lax.all_to_all(send, 'rad', 0, 0)]
    unnamed x28 -> x30, local copies, waits for them, and re-layouts: 5.21 us -> 4.39 us
  transfers between devices with their start and end apart: 11 -> 11, of which waited for: 6 -> 6; matrix products, arithmetic and copies ran while one was open for 1% -> 0% of each run, Pallas kernels for 2% -> 2%
where the time goes in v2:
time: 200 us; the launch traced here: 197 us
  blocking collectives  85.4 us (43%)
  starting transfers between devices  50.8 us (25%)
  waiting for transfers between devices  31 us (16%)
  Pallas kernels  24.7 us (12%)
  local copies, waits for them, and re-layouts  5.32 us (3%)
    all_to_all x3, blocking collectives, body(): across = lax.all_to_all(send, 'row', 0, 0)  43 us
    all_to_all x3, blocking collectives, body(): got = lax.all_to_all(send, 'rad', 0, 0)  42.4 us
    pallas_call x14, Pallas kernels, call(): pl.pallas_call(kernel, out_shape=[jax.ShapeDtypeStruct(o, jnp.float32) fo...  24.7 us
    ppermute x4, starting transfers between devices, body(): down = lax.ppermute(down, 'sec', forward)  17.2 us
    all_to_all x1, waiting for transfers between devices, body(): got = lax.all_to_all(send, 'rad', 0, 0)  12.5 us
    ppermute x4, waiting for transfers between devices, body(): up = lax.ppermute(up, 'sec', backward)  12.4 us
    all_to_all x1, starting transfers between devices, body(): across = lax.all_to_all(send, 'row', 0, 0)  12.4 us
    all_to_all x1, starting transfers between devices, body(): got = lax.all_to_all(send, 'rad', 0, 0)  9.57 us
  transfers between devices with their start and end apart: 11, of which 6 were waited for; matrix products, arithmetic and copies ran while one was open for 0% of the time, Pallas kernels for 2%

profile of v2, /device:TPU:1, one launch (start us, length us, event | category | flops | bytes accessed | tf_op | source)
XLA Modules:
  0.0 197.5 jit_solution(16179980429848867222)
XLA Ops:
  1.4 6.4 %all-to-all-start.1 = ((s32[8,8,128]{2,1,0:T(8,128)}), s32[8,8,128]{2,1,0:T(8,128)S(1)}, u32[]{:S(2)}, u32[]{:S(2)}) async-start(s32[8,8,128]{2,1,0:T(8,128)} %broadcast_in_dim.16), calls=%async_computation.1 | async-start | bytes 65536 | tf_op jit(solution)/shard_map/all_to_all | solution.py:295
  11.1 2.1 %first.1 = (f32[2,112,128]{2,1,0:T(8,128)S(1)}, f32[2,8,128]{2,1,0:T(8,128)S(1)}, f32[5,8,128]{2,1,0:T(8,128)S(1)}, f32[8,128]{1,0:T(8,128)S(1)}, f32[8,128]{1,0:T(8,128)S(1)}) custom-call(s32[6]{0:T(128)S(1)} %stack.15.ids, f32[5]{0:T(128)S(1)} %copy-done.10, f32[5,16,8,128]{3,2,1,0:T(8,128)S(1)} %bitcast.17, f32[5,8,128]{2,1,0:T(8,128)S(1)} %copy-done.9, ...), custom_call_target="tpu_custom_call" | custom-call | bytes 696364 | tf_op jit(solution)/shard_map/first/pallas_call | solution.py:32
  13.2 3.1 %collective-permute-start = (f32[5,8,128]{2,1,0:T(8,128)S(1)}, f32[5,8,128]{2,1,0:T(8,128)S(1)}, u32[]{:S(2)}, u32[]{:S(2)}) collective-permute-start(f32[5,8,128]{2,1,0:T(8,128)S(1)} %get-tuple-element.25), channel_id=1, source_target_pairs={{0,64},{64,128},{128,192},{1,65},{65,129},{129,193},{2,66},{66,130... | collective-permute-start | bytes 61448 | tf_op jit(solution)/shard_map/ppermute | solution.py:312
  17.5 3.2 %collective-permute-done.1.up = f32[8,128]{1,0:T(8,128)S(1)} collective-permute-done((f32[8,128]{1,0:T(8,128)S(1)}, f32[8,128]{1,0:T(8,128)S(1)}, u32[]{:S(2)}, u32[]{:S(2)}) %collective-permute-start.1) | collective-permute-done | bytes 4128 | tf_op jit(solution)/shard_map/ppermute | solution.py:313
  22.2 9.6 %all-to-all-start = ((f32[8,160,128]{2,1,0:T(8,128)}), f32[8,160,128]{2,1,0:T(8,128)S(1)}, u32[]{:S(2)}, u32[]{:S(2)}) async-start(f32[8,160,128]{2,1,0:T(8,128)} %gather.4), calls=%async_computation | async-start | bytes 1310720 | tf_op jit(solution)/shard_map/all_to_all | solution.py:321
  31.8 12.5 %all-to-all-done.got = f32[8,160,128]{2,1,0:T(8,128)S(1)} async-done(((f32[8,160,128]{2,1,0:T(8,128)}), f32[8,160,128]{2,1,0:T(8,128)S(1)}, u32[]{:S(2)}, u32[]{:S(2)}) %all-to-all-start) | async-done | bytes 655392 | tf_op jit(solution)/shard_map/all_to_all | solution.py:321
  46.0 12.4 %all-to-all-start.2 = ((f32[8,56,128]{2,1,0:T(8,128)}), f32[8,56,128]{2,1,0:T(8,128)S(1)}, u32[]{:S(2)}, u32[]{:S(2)}) async-start(f32[8,56,128]{2,1,0:T(8,128)} %select.5), calls=%async_computation.2 | async-start | bytes 458752 | tf_op jit(solution)/shard_map/all_to_all | solution.py:329
  58.5 6.0 %all-to-all-done.2.across = f32[8,56,128]{2,1,0:T(8,128)S(1)} async-done(((f32[8,56,128]{2,1,0:T(8,128)}), f32[8,56,128]{2,1,0:T(8,128)S(1)}, u32[]{:S(2)}, u32[]{:S(2)}) %all-to-all-start.2) | async-done | bytes 229408 | tf_op jit(solution)/shard_map/all_to_all | solution.py:329
  67.2 3.4 %update.3 = (f32[5,16,8,128]{3,2,1,0:T(8,128)S(1)}, f32[2,80,128]{2,1,0:T(8,128)S(1)}, f32[2,8,128]{2,1,0:T(8,128)S(1)}, f32[5,8,128]{2,1,0:T(8,128)S(1)}, f32[8,128]{1,0:T(8,128)S(1)}) custom-call(s32[6]{0:T(128)S(1)} %stack.15.ids, s32[16]{0:T(128)S(1)} %pad_add_fusion.donors, f32[5]{0:T(128)S(1)} %copy-done.10, f32[5]{0:T(128)S(1)} %copy-done.11, ...), custom_call_target="tpu_custom_call" | custom-call | flops 5734400 | bytes 2748544 | tf_op jit(solution)/shard_map/update/pallas_call | solution.py:32
  70.5 4.1 %collective-permute-start.2 = (f32[5,8,128]{2,1,0:T(8,128)S(1)}, f32[5,8,128]{2,1,0:T(8,128)S(1)}, u32[]{:S(2)}, u32[]{:S(2)}) collective-permute-start(f32[5,8,128]{2,1,0:T(8,128)S(1)} %get-tuple-element.31), channel_id=1, source_target_pairs={{0,64},{64,128},{128,192},{1,65},{65,129},{129,193},{2,66},{66,130... | collective-permute-start | bytes 61448 | tf_op jit(solution)/shard_map/ppermute | solution.py:312
  76.0 3.1 %collective-permute-done.3.up = f32[8,128]{1,0:T(8,128)S(1)} collective-permute-done((f32[8,128]{1,0:T(8,128)S(1)}, f32[8,128]{1,0:T(8,128)S(1)}, u32[]{:S(2)}, u32[]{:S(2)}) %collective-permute-start.3) | collective-permute-done | bytes 4128 | tf_op jit(solution)/shard_map/ppermute | solution.py:313
  79.6 14.6 %all_to_all.45.got = f32[8,128,128]{2,1,0:T(8,128)S(1)} all-to-all(f32[8,128,128]{2,1,0:T(8,128)S(1)} %gather.5), channel_id=1, replica_groups=mesh['sec'=4,'row'=8,'rad'=8] {'rad'}, dimensions={0} | all-to-all | bytes 1048576 | tf_op jit(solution)/shard_map/all_to_all | solution.py:321
  95.2 14.3 %all_to_all.46.across = f32[8,56,128]{2,1,0:T(8,128)S(1)} all-to-all(f32[8,56,128]{2,1,0:T(8,128)S(1)} %select.6), channel_id=1, replica_groups=mesh['sec'=4,'row'=8,'rad'=8] {'row'}, dimensions={0} | all-to-all | bytes 458752 | tf_op jit(solution)/shard_map/all_to_all | solution.py:329
  109.5 3.4 %update.4 = (f32[5,16,8,128]{3,2,1,0:T(8,128)S(1)}, f32[2,80,128]{2,1,0:T(8,128)S(1)}, f32[2,8,128]{2,1,0:T(8,128)S(1)}, f32[5,8,128]{2,1,0:T(8,128)S(1)}, f32[8,128]{1,0:T(8,128)S(1)}) custom-call(s32[6]{0:T(128)S(1)} %stack.15.ids, s32[16]{0:T(128)S(1)} %pad_add_fusion.donors, f32[5]{0:T(128)S(1)} %copy-done.10, f32[5]{0:T(128)S(1)} %copy-done.11, ...), custom_call_target="tpu_custom_call" | custom-call | flops 5734400 | bytes 2617472 | tf_op jit(solution)/shard_map/update/pallas_call | solution.py:32
  112.8 4.9 %collective-permute-start.4 = (f32[5,8,128]{2,1,0:T(8,128)S(1)}, f32[5,8,128]{2,1,0:T(8,128)S(1)}, u32[]{:S(2)}, u32[]{:S(2)}) collective-permute-start(f32[5,8,128]{2,1,0:T(8,128)S(1)} %get-tuple-element.36), channel_id=1, source_target_pairs={{0,64},{64,128},{128,192},{1,65},{65,129},{129,193},{2,66},{66,130... | collective-permute-start | bytes 61448 | tf_op jit(solution)/shard_map/ppermute | solution.py:312
  119.0 3.1 %collective-permute-done.5.up = f32[8,128]{1,0:T(8,128)S(1)} collective-permute-done((f32[8,128]{1,0:T(8,128)S(1)}, f32[8,128]{1,0:T(8,128)S(1)}, u32[]{:S(2)}, u32[]{:S(2)}) %collective-permute-start.5) | collective-permute-done | bytes 4128 | tf_op jit(solution)/shard_map/ppermute | solution.py:313
  122.6 13.9 %all_to_all.47.got = f32[8,128,128]{2,1,0:T(8,128)S(1)} all-to-all(f32[8,128,128]{2,1,0:T(8,128)S(1)} %gather.6), channel_id=1, replica_groups=mesh['sec'=4,'row'=8,'rad'=8] {'rad'}, dimensions={0} | all-to-all | bytes 1048576 | tf_op jit(solution)/shard_map/all_to_all | solution.py:321
  137.5 14.3 %all_to_all.48.across = f32[8,56,128]{2,1,0:T(8,128)S(1)} all-to-all(f32[8,56,128]{2,1,0:T(8,128)S(1)} %select.7), channel_id=1, replica_groups=mesh['sec'=4,'row'=8,'rad'=8] {'row'}, dimensions={0} | all-to-all | bytes 458752 | tf_op jit(solution)/shard_map/all_to_all | solution.py:329
  151.9 3.4 %update.5 = (f32[5,16,8,128]{3,2,1,0:T(8,128)S(1)}, f32[2,80,128]{2,1,0:T(8,128)S(1)}, f32[2,8,128]{2,1,0:T(8,128)S(1)}, f32[5,8,128]{2,1,0:T(8,128)S(1)}, f32[8,128]{1,0:T(8,128)S(1)}) custom-call(s32[6]{0:T(128)S(1)} %stack.15.ids, s32[16]{0:T(128)S(1)} %pad_add_fusion.donors, f32[5]{0:T(128)S(1)} %copy-done.10, f32[5]{0:T(128)S(1)} %copy-done.11, ...), custom_call_target="tpu_custom_call" | custom-call | flops 5734400 | bytes 2617472 | tf_op jit(solution)/shard_map/update/pallas_call | solution.py:32
  155.2 5.1 %collective-permute-start.6 = (f32[5,8,128]{2,1,0:T(8,128)S(1)}, f32[5,8,128]{2,1,0:T(8,128)S(1)}, u32[]{:S(2)}, u32[]{:S(2)}) collective-permute-start(f32[5,8,128]{2,1,0:T(8,128)S(1)} %get-tuple-element.41), channel_id=1, source_target_pairs={{0,64},{64,128},{128,192},{1,65},{65,129},{129,193},{2,66},{66,130... | collective-permute-start | bytes 61448 | tf_op jit(solution)/shard_map/ppermute | solution.py:312
  161.7 3.1 %collective-permute-done.7.up = f32[8,128]{1,0:T(8,128)S(1)} collective-permute-done((f32[8,128]{1,0:T(8,128)S(1)}, f32[8,128]{1,0:T(8,128)S(1)}, u32[]{:S(2)}, u32[]{:S(2)}) %collective-permute-start.7) | collective-permute-done | bytes 4128 | tf_op jit(solution)/shard_map/ppermute | solution.py:313
  165.3 13.9 %all_to_all.49.got = f32[8,128,128]{2,1,0:T(8,128)S(1)} all-to-all(f32[8,128,128]{2,1,0:T(8,128)S(1)} %gather.7), channel_id=1, replica_groups=mesh['sec'=4,'row'=8,'rad'=8] {'rad'}, dimensions={0} | all-to-all | bytes 1048576 | tf_op jit(solution)/shard_map/all_to_all | solution.py:321
  180.2 14.3 %all_to_all.50.across = f32[8,56,128]{2,1,0:T(8,128)S(1)} all-to-all(f32[8,56,128]{2,1,0:T(8,128)S(1)} %select.8), channel_id=1, replica_groups=mesh['sec'=4,'row'=8,'rad'=8] {'row'}, dimensions={0} | all-to-all | bytes 458752 | tf_op jit(solution)/shard_map/all_to_all | solution.py:329
  194.5 2.9 %update_last.1 = f32[5,16,8,128]{3,2,1,0:T(8,128)} custom-call(s32[6]{0:T(128)S(1)} %stack.15.ids, s32[16]{0:T(128)S(1)} %pad_add_fusion.donors, f32[5]{0:T(128)S(1)} %copy-done.10, f32[5]{0:T(128)S(1)} %copy-done.11, f32[5,16,8,128]{3,2,1,0:T(8,128)S(1)} %get-tuple-element.40.state, f32[12,16,8,128]{3,2,1,0:T(8,128)S(1)} %coef.1, ...), custom_call_target="tpu_custom_call" | custom-call | flops 5734400 | bytes 2502784 | tf_op jit(solution)/shard_map/update_last/pallas_call | solution.py:32
  (56 shorter events, 20.2 us)
Async XLA Ops:
  0.0 0.7 copy-start.14
  0.8 7.2 %copy-start.3 = (f32[1,16,8,128]{3,2,1,0:T(8,128)S(1)}, f32[1,16,8,128]{3,2,1,0:T(8,128)}, u32[]{:S(2)}) copy-start(f32[1,16,8,128]{3,2,1,0:T(8,128)} %param.16) | copy-start | bytes 196612
  0.8 7.2 %copy-start.4 = (f32[1,16,8,128]{3,2,1,0:T(8,128)S(1)}, f32[1,16,8,128]{3,2,1,0:T(8,128)}, u32[]{:S(2)}) copy-start(f32[1,16,8,128]{3,2,1,0:T(8,128)} %param.17) | copy-start | bytes 196612
  1.4 20.8 %all-to-all-start.1 = ((s32[8,8,128]{2,1,0:T(8,128)}), s32[8,8,128]{2,1,0:T(8,128)S(1)}, u32[]{:S(2)}, u32[]{:S(2)}) async-start(s32[8,8,128]{2,1,0:T(8,128)} %broadcast_in_dim.16), calls=%async_computation.1 | async-start | bytes 65536 | tf_op jit(solution)/shard_map/all_to_all | solution.py:295
  8.6 1.0 copy-start
  9.5 0.8 copy-start.5
  10.4 0.7 copy-start.9
  11.1 9.7 %copy-start.2 = (f32[5,8,128]{2,1,0:T(8,128)S(1)}, f32[5,8,128]{2,1,0:T(8,128)}, u32[]{:S(2)}) copy-start(f32[5,8,128]{2,1,0:T(8,128)} %inflow.7) | copy-start | bytes 61444
  13.2 7.6 %collective-permute-start = (f32[5,8,128]{2,1,0:T(8,128)S(1)}, f32[5,8,128]{2,1,0:T(8,128)S(1)}, u32[]{:S(2)}, u32[]{:S(2)}) collective-permute-start(f32[5,8,128]{2,1,0:T(8,128)S(1)} %get-tuple-element.25), channel_id=1, source_target_pairs={{0,64},{64,128},{128,192},{1,65},{65,129},{129,193},{2,66},{66,130... | collective-permute-start | bytes 61448 | tf_op jit(solution)/shard_map/ppermute | solution.py:312
  16.2 4.5 %collective-permute-start.1 = (f32[8,128]{1,0:T(8,128)S(1)}, f32[8,128]{1,0:T(8,128)S(1)}, u32[]{:S(2)}, u32[]{:S(2)}) collective-permute-start(f32[8,128]{1,0:T(8,128)S(1)} %get-tuple-element.26), channel_id=1, source_target_pairs={{64,0},{128,64},{192,128},{65,1},{129,65},{193,129},{66,2},{130,66... | collective-permute-start | bytes 12296 | tf_op jit(solution)/shard_map/ppermute | solution.py:313
  22.2 22.1 %all-to-all-start = ((f32[8,160,128]{2,1,0:T(8,128)}), f32[8,160,128]{2,1,0:T(8,128)S(1)}, u32[]{:S(2)}, u32[]{:S(2)}) async-start(f32[8,160,128]{2,1,0:T(8,128)} %gather.4), calls=%async_computation | async-start | bytes 1310720 | tf_op jit(solution)/shard_map/all_to_all | solution.py:321
  46.0 12.4 %copy-start.12 = (f32[1,3,5,5]{3,0,2,1:T(1,128)S(1)}, f32[1,3,5,5]{3,0,2,1:T(1,128)}, u32[]{:S(2)}) copy-start(f32[1,3,5,5]{3,0,2,1:T(1,128)} %param.19) | copy-start | bytes 904
  46.0 18.6 %copy-start.6 = (f32[1,16,8,128]{3,2,1,0:T(8,128)S(1)}, f32[1,16,8,128]{3,2,1,0:T(8,128)}, u32[]{:S(2)}) copy-start(f32[1,16,8,128]{3,2,1,0:T(8,128)} %param.18) | copy-start | bytes 196612
  46.0 18.6 %copy-start.7 = (f32[1,16,8,128]{3,2,1,0:T(8,128)S(1)}, f32[1,16,8,128]{3,2,1,0:T(8,128)}, u32[]{:S(2)}) copy-start(f32[1,16,8,128]{3,2,1,0:T(8,128)} %param.14) | copy-start | bytes 196612
  46.0 18.6 %copy-start.8 = (f32[1,16,8,128]{3,2,1,0:T(8,128)S(1)}, f32[1,16,8,128]{3,2,1,0:T(8,128)}, u32[]{:S(2)}) copy-start(f32[1,16,8,128]{3,2,1,0:T(8,128)} %param.15) | copy-start | bytes 196612
  46.0 18.5 %all-to-all-start.2 = ((f32[8,56,128]{2,1,0:T(8,128)}), f32[8,56,128]{2,1,0:T(8,128)S(1)}, u32[]{:S(2)}, u32[]{:S(2)}) async-start(f32[8,56,128]{2,1,0:T(8,128)} %select.5), calls=%async_computation.2 | async-start | bytes 458752 | tf_op jit(solution)/shard_map/all_to_all | solution.py:329
  64.5 2.1 %copy-start.1 = (f32[5,1,16,8,128]{4,3,2,1,0:T(8,128)S(1)}, f32[5,1,16,8,128]{4,3,2,1,0:T(8,128)}, u32[]{:S(2)}) copy-start(f32[5,1,16,8,128]{4,3,2,1,0:T(8,128)} %param.13) | copy-start | bytes 983044
  66.5 0.7 copy-start.11
  70.5 8.5 %collective-permute-start.2 = (f32[5,8,128]{2,1,0:T(8,128)S(1)}, f32[5,8,128]{2,1,0:T(8,128)S(1)}, u32[]{:S(2)}, u32[]{:S(2)}) collective-permute-start(f32[5,8,128]{2,1,0:T(8,128)S(1)} %get-tuple-element.31), channel_id=1, source_target_pairs={{0,64},{64,128},{128,192},{1,65},{65,129},{129,193},{2,66},{66,130... | collective-permute-start | bytes 61448 | tf_op jit(solution)/shard_map/ppermute | solution.py:312
  74.7 4.4 %collective-permute-start.3 = (f32[8,128]{1,0:T(8,128)S(1)}, f32[8,128]{1,0:T(8,128)S(1)}, u32[]{:S(2)}, u32[]{:S(2)}) collective-permute-start(f32[8,128]{1,0:T(8,128)S(1)} %get-tuple-element.32), channel_id=1, source_target_pairs={{64,0},{128,64},{192,128},{65,1},{129,65},{193,129},{66,2},{130,66... | collective-permute-start | bytes 12296 | tf_op jit(solution)/shard_map/ppermute | solution.py:313
  112.8 9.2 %collective-permute-start.4 = (f32[5,8,128]{2,1,0:T(8,128)S(1)}, f32[5,8,128]{2,1,0:T(8,128)S(1)}, u32[]{:S(2)}, u32[]{:S(2)}) collective-permute-start(f32[5,8,128]{2,1,0:T(8,128)S(1)} %get-tuple-element.36), channel_id=1, source_target_pairs={{0,64},{64,128},{128,192},{1,65},{65,129},{129,193},{2,66},{66,130... | collective-permute-start | bytes 61448 | tf_op jit(solution)/shard_map/ppermute | solution.py:312
  117.7 4.4 %collective-permute-start.5 = (f32[8,128]{1,0:T(8,128)S(1)}, f32[8,128]{1,0:T(8,128)S(1)}, u32[]{:S(2)}, u32[]{:S(2)}) collective-permute-start(f32[8,128]{1,0:T(8,128)S(1)} %get-tuple-element.37), channel_id=1, source_target_pairs={{64,0},{128,64},{192,128},{65,1},{129,65},{193,129},{66,2},{130,66... | collective-permute-start | bytes 12296 | tf_op jit(solution)/shard_map/ppermute | solution.py:313
  155.2 9.5 %collective-permute-start.6 = (f32[5,8,128]{2,1,0:T(8,128)S(1)}, f32[5,8,128]{2,1,0:T(8,128)S(1)}, u32[]{:S(2)}, u32[]{:S(2)}) collective-permute-start(f32[5,8,128]{2,1,0:T(8,128)S(1)} %get-tuple-element.41), channel_id=1, source_target_pairs={{0,64},{64,128},{128,192},{1,65},{65,129},{129,193},{2,66},{66,130... | collective-permute-start | bytes 61448 | tf_op jit(solution)/shard_map/ppermute | solution.py:312
  160.4 4.4 %collective-permute-start.7 = (f32[8,128]{1,0:T(8,128)S(1)}, f32[8,128]{1,0:T(8,128)S(1)}, u32[]{:S(2)}, u32[]{:S(2)}) collective-permute-start(f32[8,128]{1,0:T(8,128)S(1)} %get-tuple-element.42), channel_id=1, source_target_pairs={{64,0},{128,64},{192,128},{65,1},{129,65},{193,129},{66,2},{130,66... | collective-permute-start | bytes 12296 | tf_op jit(solution)/shard_map/ppermute | solution.py:313
  (2 other events, 1.3 us)

commit v3 on v2

v3 whole, which is shorter than its diff:
```python
import functools

import jax
import jax.numpy as jnp
from jax import lax
from jax.experimental import pallas as pl
from jax.experimental.pallas import tpu as pltpu
from jax.sharding import PartitionSpec as P

STEPS = 4
time_step = 0.08
INTERPRET = False
VMEM_LIMIT = 8 * 1024 * 1024

NV = 5
WIDE = 4
ROWS = 16
PLANES = 16
TILE_ROWS = 48


def vmem():
    return pl.BlockSpec(memory_space=pltpu.VMEM)


def smem():
    return pl.BlockSpec(memory_space=pltpu.SMEM)


def call(kernel, outs, scalars, arrays, name, flops=0, scratch=()):
    moved = sum(a.size * 4 for a in arrays) + sum(4 * functools.reduce(lambda x, y: x * y, o) for o in outs)
    return pl.pallas_call(
        kernel,
        out_shape=[jax.ShapeDtypeStruct(o, jnp.float32) for o in outs],
        in_specs=[smem() for _ in scalars] + [vmem() for _ in arrays],
        out_specs=[vmem() for _ in outs],
        scratch_shapes=list(scratch),
        name=name,
        compiler_params=pltpu.CompilerParams(vmem_limit_bytes=VMEM_LIMIT),
        cost_estimate=pl.CostEstimate(flops=flops, bytes_accessed=moved, transcendentals=0),
        interpret=INTERPRET,
    )(*scalars, *arrays)


def lanes_of(shape):
    return lax.broadcasted_iota(jnp.int32, shape, 1)


def rows_of(shape):
    return lax.broadcasted_iota(jnp.int32, shape, 0)


def roll(x, by, axis):
    size = x.shape[axis]
    if not isinstance(by, int):
        return pltpu.roll(x, lax.rem(by + 2 * size, size), axis)
    by %= size
    return x if by == 0 else pltpu.roll(x, by, axis)


def pressure(weight_ref, values):
    total = weight_ref[0] * values[0]
    for v in range(1, NV):
        total = total + weight_ref[v] * values[v]
    return total


def picked(step):
    count = 2 * (WIDE - 1 - step) + 8
    return range(step + 1, step + 1 + count), -(-6 * count // 8) * 8


def first_kernel(weight, state, volume, axial, radial, circ, mu, outflow, to_above, to_below, down, up, out_pressure):
    def put(at, half, cell):
        to_above[at, half : half + 4, :] = cell[4:8]
        to_below[at, half : half + 4, :] = cell[0:4]

    def one(k, carry):
        for half in (0, 1):
            plane = 2 * k + half
            for v in range(NV):
                put(v * 8 + k, 4 * half, state[v, plane])
            for at, array in enumerate((volume, axial, radial, circ, mu)):
                put((NV + at) * 8 + k, 4 * half, array[plane])
        return carry

    for v in range(NV):
        down[v] = state[v, PLANES - 1]
    up[...] = pressure(weight, [state[v, 0] for v in range(NV)])
    out_pressure[...] = pressure(weight, [outflow[v] for v in range(NV)])
    lax.fori_loop(0, PLANES // 2, one, 0)


def gather_kernel(first_step, ids, down, up, inflow, out_pressure, *refs):
    if first_step:
        donors, send = refs
    else:
        (send,) = refs
    section = ids[0]
    size = send.shape[0]
    for v in range(NV):
        value = jnp.where(section == 0, inflow[v], down[v])
        for j in range(size):
            send[j, v * 8 : v * 8 + 8, :] = value
    value = jnp.where(section == ids[4] - 1, out_pressure[...], up[...])
    for j in range(size):
        send[j, 40:48, :] = value
        if first_step:
            send[j, 48:56, :] = donors[...]


def wanted_kernel(ids, got, send, mine):
    rad, rad_size = ids[2], ids[3]
    lanes = lanes_of((8, 128))
    below = got[jnp.maximum(rad - 1, 0), 48:56, :]
    above = got[jnp.minimum(rad + 1, rad_size - 1), 48:56, :]
    own = got[rad, 48:56, :]
    down = jnp.where(lanes < 4, roll(below, -4, 1), jnp.where(lanes < 12, roll(own, 4, 1), roll(above, 12, 1)))
    up = jnp.where(lanes < 20, roll(below, 4, 1), jnp.where(lanes < 28, roll(own, 12, 1), roll(above, 20, 1)))
    both = jnp.where(lanes < 16, down, up)
    mine[...] = both
    for j in range(send.shape[0]):
        send[j] = both


def extend_kernel(state, volume, axial, radial, circ, mu, from_below, from_above, field, raw, edges):
    lanes = lanes_of((ROWS, 128))

    def one(k, carry):
        last, first = carry
        for half in (0, 1):
            plane = 2 * k + half
            rows = slice(4 * half, 4 * half + 4)

            def put(at, target, index, cell):
                target[index, plane, 0:4, :] = from_below[at, rows, :]
                target[index, plane, 4:12, :] = cell
                target[index, plane, 12:16, :] = from_above[at, rows, :]
                return target[index, plane]

            for v in range(NV):
                cell = put(v * 8 + k, field, v, state[v, plane])
                at = v * 16 + plane
                last = jnp.where(lanes == at, roll(cell, at + 1, 1), last)
                first = jnp.where(lanes == at, roll(cell, at, 1), first)
            for at, array in enumerate((volume, axial, radial, circ, mu)):
                cell = put((NV + at) * 8 + k, raw, at, array[plane])
                if at == 3:
                    last = jnp.where(lanes == 96 + plane, roll(cell, 97 + plane, 1), last)
                if at == 4:
                    last = jnp.where(lanes == 80 + plane, roll(cell, 81 + plane, 1), last)
                    first = jnp.where(lanes == 80 + plane, roll(cell, 80 + plane, 1), first)
        return last, first

    zero = jnp.zeros((ROWS, 128), jnp.float32)
    last, first = lax.fori_loop(0, PLANES // 2, one, (zero, zero))
    edges[0] = last
    edges[1] = first


def select_kernel(step, ids, wanted, got, edges, send):
    size = send.shape[0]
    row = ids[1]
    rows, base = picked(step)
    count = len(rows)

    def one(j, carry):
        for n, i in enumerate(rows):
            d = wanted[j, i] & 63
            r, b = d >> 3, d & 7
            for v in range(NV):
                send[j, v * count + n : v * count + n + 1, :] = got[r, pl.ds(v * 8 + b, 1), :]
            e = wanted[j, 16 + i] & 63
            send[j, NV * count + n : NV * count + n + 1, :] = got[e >> 3, pl.ds(40 + (e & 7), 1), :]
        return carry

    lax.fori_loop(0, size, one, 0)
    send[lax.rem(row + 1, size), base : base + ROWS, :] = edges[0]
    send[lax.rem(row + size - 1, size), base : base + ROWS, :] = edges[1]


def sides(ids, across, base):
    row, row_size = ids[1], ids[5]
    left = across[lax.rem(row + row_size - 1, row_size), base : base + ROWS, :]
    right = across[lax.rem(row + 1, row_size), base : base + ROWS, :]
    return left, right


def coef_kernel(ids, raw, across, coef):
    rad, rad_size = ids[2], ids[3]
    lanes = lanes_of((ROWS, 128))
    rows = rows_of((ROWS, 128))
    outside = jnp.logical_or(
        jnp.logical_and(rad == 0, rows < WIDE), jnp.logical_and(rad == rad_size - 1, rows >= WIDE + 8)
    )
    casing = jnp.logical_and(rad == rad_size - 1, rows >= WIDE + 7)
    left, right = sides(ids, across, picked(0)[1])

    def one(k, carry):
        m = raw[4, k]
        c = jnp.where(outside, 0.0, time_step / jnp.where(outside, 1.0, raw[0, k]))
        half = 0.5 * c
        diffused = []

        def put(at, area, viscous):
            coef[at, k] = half * area
            b = c * area * viscous
            coef[at + 1, k] = b
            diffused.append(b)

        lower, upper = jnp.maximum(k - 1, 0), jnp.minimum(k + 1, PLANES - 1)
        put(0, raw[1, lower], 0.5 * (m + raw[4, lower]))
        put(2, raw[1, k], 0.5 * (m + raw[4, upper]))
        face = jnp.where(casing, 0.0, raw[2, k])
        put(4, roll(face, 1, 0), 0.5 * (m + roll(m, 1, 0)))
        put(6, face, 0.5 * (m + roll(m, ROWS - 1, 0)))
        around = raw[3, k]
        at = 80 + k
        mu_left = jnp.where(lanes == 0, roll(left, -at, 1), roll(m, 1, 1))
        mu_right = jnp.where(lanes == 127, roll(right, 127 - at, 1), roll(m, 127, 1))
        circ_left = jnp.where(lanes == 0, roll(left, -(at + 16), 1), roll(around, 1, 1))
        put(8, circ_left, 0.5 * (mu_left + m))
        put(10, around, 0.5 * (m + mu_right))
        total = diffused[0]
        for b in diffused[1:]:
            total = total + b
        coef[12, k] = 1.0 - total
        return carry

    lax.fori_loop(0, PLANES, one, 0)


def advance(k, before, here, after, coef, matrix, left, right, lanes):
    rest = coef[12, k]
    total = [rest * here[v] for v in range(NV)]
    for d in range(3):
        low_a, low_b = coef[4 * d, k], coef[4 * d + 1, k]
        high_a, high_b = coef[4 * d + 2, k], coef[4 * d + 3, k]
        own_a = high_a - low_a
        mixed = []
        for v in range(NV):
            cell = here[v]
            if d == 0:
                lower, upper = before[v], after[v]
            elif d == 1:
                lower, upper = roll(cell, 1, 0), roll(cell, ROWS - 1, 0)
            else:
                at = v * 16 + k
                lower = jnp.where(lanes == 0, roll(left, -at, 1), roll(cell, 1, 1))
                upper = jnp.where(lanes == 127, roll(right, 127 - at, 1), roll(cell, 127, 1))
            mixed.append(high_a * upper - low_a * lower + own_a * cell)
            total[v] = total[v] + (high_b * upper + low_b * lower)
        for u in range(NV):
            for v in range(NV):
                at = 25 * d + 5 * u + v
                total[u] = total[u] - jnp.broadcast_to(matrix[at : at + 1, :], (ROWS, 128)) * mixed[v]
    return total


def ghosts_of(step, donors, weight, coupling, field, across, ghost):
    rows, _ = picked(step)
    count = len(rows)
    ghost[...] = jnp.zeros(ghost.shape, jnp.float32)
    for n, i in enumerate(rows):
        d = donors[i] >> 6
        for v in range(NV):
            ghost[v, i : i + 1, :] = across[d, v * count + n : v * count + n + 1, :]
        e = donors[16 + i] >> 6
        ghost[NV, i : i + 1, :] = across[e, NV * count + n : NV * count + n + 1, :]
    outlet = [field[v, PLANES - 1] for v in range(NV)]
    jump = ghost[NV] - pressure(weight, outlet)
    return [ghost[v] for v in range(NV)], [outlet[v] + coupling[v] * jump for v in range(NV)]


def ends_of(step, ids, donors, weight, coupling, field, coef, matrix, across, ghost):
    lanes = lanes_of((ROWS, 128))
    left, right = sides(ids, across, picked(step)[1])
    inlet_ghost, outlet_ghost = ghosts_of(step, donors, weight, coupling, field, across, ghost)
    plane = lambda k: [field[v, k] for v in range(NV)]
    new_inlet = advance(0, inlet_ghost, plane(0), plane(1), coef, matrix, left, right, lanes)
    last = PLANES - 1
    new_outlet = advance(last, plane(last - 1), plane(last), outlet_ghost, coef, matrix, left, right, lanes)
    return new_inlet, new_outlet


def ends_kernel(step, ids, donors, weight, coupling, field, coef, matrix, across, ends, down, up, ghost):
    new_inlet, new_outlet = ends_of(step, ids, donors, weight, coupling, field, coef, matrix, across, ghost)
    for v in range(NV):
        ends[0, v] = new_inlet[v]
        ends[1, v] = new_outlet[v]
        down[v] = new_outlet[v][WIDE : WIDE + 8]
    up[...] = pressure(weight, new_inlet)[WIDE : WIDE + 8]


def bulk_kernel(step, ids, field, coef, matrix, across, ends, new, edges):
    lanes = lanes_of((ROWS, 128))
    left, right = sides(ids, across, picked(step)[1])

    def note(k, total, last, first):
        for v in range(NV):
            new[v, k] = total[v]
            at = v * 16 + k
            spot = lanes == at
            last = jnp.where(spot, roll(total[v], at + 1, 1), last)
            first = jnp.where(spot, roll(total[v], at, 1), first)
        return last, first

    def one(k, carry):
        before, here, last, first = carry
        after = [field[v, k + 1] for v in range(NV)]
        total = advance(k, before, here, after, coef, matrix, left, right, lanes)
        last, first = note(k, total, last, first)
        return here, after, last, first

    zero = jnp.zeros((ROWS, 128), jnp.float32)
    last, first = note(0, [ends[0, v] for v in range(NV)], zero, zero)
    last, first = note(PLANES - 1, [ends[1, v] for v in range(NV)], last, first)
    carry = ([field[v, 0] for v in range(NV)], [field[v, 1] for v in range(NV)], last, first)
    _, _, last, first = lax.fori_loop(1, PLANES - 1, one, carry)
    edges[0] = last
    edges[1] = first


def last_kernel(step, ids, donors, weight, coupling, field, coef, matrix, across, new, ghost):
    lanes = lanes_of((ROWS, 128))
    left, right = sides(ids, across, picked(step)[1])
    new_inlet, new_outlet = ends_of(step, ids, donors, weight, coupling, field, coef, matrix, across, ghost)
    for v in range(NV):
        new[v, 0] = new_inlet[v][WIDE : WIDE + 8]
        new[v, PLANES - 1] = new_outlet[v][WIDE : WIDE + 8]

    def one(k, carry):
        before, here = carry
        after = [field[v, k + 1] for v in range(NV)]
        total = advance(k, before, here, after, coef, matrix, left, right, lanes)
        for v in range(NV):
            new[v, k] = total[v][WIDE : WIDE + 8]
        return here, after

    carry = ([field[v, 0] for v in range(NV)], [field[v, 1] for v in range(NV)])
    lax.fori_loop(1, PLANES - 1, one, carry)


def body(
    state,
    volume,
    face_axial,
    face_radial,
    face_circum,
    viscosity,
    flux_matrix,
    inflow_plane,
    outflow_plane,
    down_donors,
    up_donors,
    pressure_weight,
    boundary_coupling,
):
    sections, row_size, rad_size = lax.axis_size("sec"), lax.axis_size("row"), lax.axis_size("rad")
    ids = jnp.stack(
        [
            lax.axis_index("sec"),
            lax.axis_index("row"),
            lax.axis_index("rad"),
            jnp.int32(rad_size),
            jnp.int32(sections),
            jnp.int32(row_size),
        ]
    ).astype(jnp.int32)
    own = [state[:, 0], volume[0], face_axial[0], face_radial[0], face_circum[0], viscosity[0]]
    donors = jnp.concatenate([down_donors[0], up_donors[0]]).astype(jnp.float32)
    donors = jnp.broadcast_to(jnp.pad(donors, (0, 112))[None], (8, 128))
    matrix = jnp.broadcast_to(jnp.pad(flux_matrix[0].reshape(75), (0, 5))[:, None], (80, 128))
    extended = (NV, PLANES, ROWS, 128)
    strips = (2, ROWS, 128)
    sent = (2 * NV * PLANES // 2, 8, 128)
    scalars = [pressure_weight, boundary_coupling]

    to_above, to_below, down, up, out_pressure = call(
        first_kernel,
        [sent, sent, (NV, 8, 128), (8, 128), (8, 128)],
        [pressure_weight],
        own + [outflow_plane],
        "first",
    )
    forward = [(i, i + 1) for i in range(sections - 1)]
    backward = [(i + 1, i) for i in range(sections - 1)]
    outward = [(i, i + 1) for i in range(rad_size - 1)]
    inward = [(i + 1, i) for i in range(rad_size - 1)]
    field = coef = edges = wanted = mine = None
    for step in range(STEPS):
        last_step = step == STEPS - 1
        rows, base = picked(step)
        down = lax.ppermute(down, "sec", forward)
        up = lax.ppermute(up, "sec", backward)
        if step == 0:
            from_below = lax.ppermute(to_above, "rad", outward)
            from_above = lax.ppermute(to_below, "rad", inward)
        (send,) = call(
            functools.partial(gather_kernel, step == 0),
            [(rad_size, TILE_ROWS + (8 if step == 0 else 0), 128)],
            [ids],
            [down, up, inflow_plane, out_pressure] + ([donors] if step == 0 else []),
            "gather",
        )
        got = lax.all_to_all(send, "rad", 0, 0)
        if step == 0:
            lists, mine = call(wanted_kernel, [(row_size, 8, 128), (8, 128)], [ids], [got], "wanted")
            wanted = lax.all_to_all(lists, "row", 0, 0)[:, 0, :32].astype(jnp.int32)
            mine = mine[0, :32].astype(jnp.int32)
            field, raw, edges = call(
                extend_kernel, [extended, extended, strips], [], own + [from_below, from_above], "extend"
            )
        (send,) = call(
            functools.partial(select_kernel, step),
            [(row_size, base + ROWS, 128)],
            [ids, wanted],
            [got, edges],
            "select",
        )
        across = lax.all_to_all(send, "row", 0, 0)
        if step == 0:
            (coef,) = call(coef_kernel, [(13, PLANES, ROWS, 128)], [ids], [raw, across], "coef")
        ghost = [pltpu.VMEM((NV + 1, ROWS, 128), jnp.float32)]
        if last_step:
            (field,) = call(
                functools.partial(last_kernel, step),
                [(NV, PLANES, 8, 128)],
                [ids, mine] + scalars,
                [field, coef, matrix, across],
                "last",
                flops=PLANES * ROWS * 128 * 300,
                scratch=ghost,
            )
        else:
            ends, down, up = call(
                functools.partial(ends_kernel, step),
                [(2, NV, ROWS, 128), (NV, 8, 128), (8, 128)],
                [ids, mine] + scalars,
                [field, coef, matrix, across],
                "ends",
                flops=2 * ROWS * 128 * 300,
                scratch=ghost,
            )
            field, edges = call(
                functools.partial(bulk_kernel, step),
                [extended, strips],
                [ids],
                [field, coef, matrix, across, ends],
                "bulk",
                flops=PLANES * ROWS * 128 * 300,
            )
    return field[:, None]


def solution(mesh):
    in_specs = (
        P(None, "sec", None, "rad", "row"),
        P("sec", None, "rad", "row"),
        P("sec", None, "rad", "row"),
        P("sec", None, "rad", "row"),
        P("sec", None, "rad", "row"),
        P("sec", None, "rad", "row"),
        P("sec", None, None, None),
        P(None, "rad", "row"),
        P(None, "rad", "row"),
        P("sec", ("row", "rad")),
        P("sec", ("row", "rad")),
        P(),
        P(),
    )
    out_specs = P(None, "sec", None, "rad", "row")
    return jax.shard_map(body, mesh=mesh, in_specs=in_specs, out_specs=out_specs, check_vma=False)
```

time: 200 us -> 195 us (0.975)
  blocking collectives: 85.4 us -> 39.5 us
  starting transfers between devices: 50.8 us -> 66.4 us
  waiting for transfers between devices: 31 us -> 42.1 us
  Pallas kernels: 24.7 us -> 32 us
  local copies, waits for them, and re-layouts: 5.32 us -> 11.9 us
    all_to_all x3 -> x0, blocking collectives: 42.4 us -> none  [body(): got = lax.all_to_all(send, 'rad', 0, 0)]
    all_to_all x1 -> x4, starting transfers between devices: 9.57 us -> 31.5 us  [body(): got = lax.all_to_all(send, 'rad', 0, 0)]
    all_to_all x1 -> x4, waiting for transfers between devices: 12.5 us -> 21.3 us  [body(): got = lax.all_to_all(send, 'rad', 0, 0)]
    all_to_all x1, starting transfers between devices: 12.4 us -> 4.23 us  [body(): across = lax.all_to_all(send, 'row', 0, 0)]
    pallas_call x14 -> x19, Pallas kernels: 24.7 us -> 32 us  [call(): pl.pallas_call(kernel, out_shape=[jax.ShapeDtypeStruct(o, jnp.float32) fo...]
    unnamed x30 -> x50, local copies, waits for them, and re-layouts: 4.39 us -> 11.6 us
    ppermute x0 -> x2, starting transfers between devices: none -> 4.67 us  [the longest x1 3.37 us: body(): from_below = lax.ppermute(to_above, 'rad', outward)]
    ppermute x4, starting transfers between devices: 17.2 us -> 13.1 us  [body(): down = lax.ppermute(down, 'sec', forward)]
  transfers between devices with their start and end apart: 11 -> 16, of which waited for: 6 -> 9; matrix products, arithmetic and copies ran while one was open for 0% -> 0% of each run, Pallas kernels for 2% -> 7%
where the time goes in v3:
time: 195 us; the launch traced here: 193 us
  starting transfers between devices  66.4 us (34%)
  waiting for transfers between devices  42.1 us (22%)
  blocking collectives  39.5 us (20%)
  Pallas kernels  32 us (16%)
  local copies, waits for them, and re-layouts  11.9 us (6%)
    all_to_all x3, blocking collectives, body(): across = lax.all_to_all(send, 'row', 0, 0)  39.5 us
    pallas_call x19, Pallas kernels, call(): pl.pallas_call(kernel, out_shape=[jax.ShapeDtypeStruct(o, jnp.float32) fo...  32 us
    all_to_all x4, starting transfers between devices, body(): got = lax.all_to_all(send, 'rad', 0, 0)  31.5 us
    all_to_all x4, waiting for transfers between devices, body(): got = lax.all_to_all(send, 'rad', 0, 0)  21.3 us
    ppermute x4, starting transfers between devices, body(): down = lax.ppermute(down, 'sec', forward)  13.1 us
    unnamed x50, local copies, waits for them, and re-layouts  11.6 us
    ppermute x4, waiting for transfers between devices, body(): up = lax.ppermute(up, 'sec', backward)  9.31 us
    all_to_all x1, waiting for transfers between devices, body(): across = lax.all_to_all(send, 'row', 0, 0)  7.89 us
  transfers between devices with their start and end apart: 16, of which 9 were waited for; matrix products, arithmetic and copies ran while one was open for 0% of the time, Pallas kernels for 7%

profile of v3, /device:TPU:1, one launch (start us, length us, event | category | flops | bytes accessed | tf_op | source)
XLA Modules:
  0.0 193.1 jit_solution(6602100393578313599)
XLA Ops:
  8.6 5.0 %collective-permute-start = (f32[5,8,128]{2,1,0:T(8,128)S(1)}, f32[5,8,128]{2,1,0:T(8,128)S(1)}, u32[]{:S(2)}, u32[]{:S(2)}) collective-permute-start(f32[5,8,128]{2,1,0:T(8,128)S(1)} %get-tuple-element.30), channel_id=1, source_target_pairs={{0,64},{64,128},{128,192},{1,65},{65,129},{129,193},{2,66},{66,130... | collective-permute-start | bytes 61448 | tf_op jit(solution)/shard_map/ppermute | solution.py:394
  16.4 10.6 %all-to-all-start = ((f32[8,56,128]{2,1,0:T(8,128)}), f32[8,56,128]{2,1,0:T(8,128)S(1)}, u32[]{:S(2)}, u32[]{:S(2)}) async-start(f32[8,56,128]{2,1,0:T(8,128)} %gather.4), calls=%async_computation | async-start | bytes 458752 | tf_op jit(solution)/shard_map/all_to_all | solution.py:406
  27.0 3.4 %collective-permute-start.2 = (f32[80,8,128]{2,1,0:T(8,128)S(1)}, f32[80,8,128]{2,1,0:T(8,128)S(1)}, u32[]{:S(2)}, u32[]{:S(2)}) collective-permute-start(f32[80,8,128]{2,1,0:T(8,128)S(1)} %get-tuple-element.34), channel_id=1, source_target_pairs={{0,1},{1,2},{2,3},{3,4},{4,5},{5,6},{6,7},{8,9},{9,10},{10,11},{11... | collective-permute-start | bytes 983048 | tf_op jit(solution)/shard_map/ppermute | solution.py:397
  31.7 5.2 %all-to-all-done.got = f32[8,56,128]{2,1,0:T(8,128)S(1)} async-done(((f32[8,56,128]{2,1,0:T(8,128)}), f32[8,56,128]{2,1,0:T(8,128)S(1)}, u32[]{:S(2)}, u32[]{:S(2)}) %all-to-all-start) | async-done | bytes 229408 | tf_op jit(solution)/shard_map/all_to_all | solution.py:406
  38.2 7.7 %all-to-all-start.1 = ((f32[8,8,128]{2,1,0:T(8,128)}), f32[8,8,128]{2,1,0:T(8,128)S(1)}, u32[]{:S(2)}, u32[]{:S(2)}) async-start(f32[8,8,128]{2,1,0:T(8,128)} %get-tuple-element.38), calls=%async_computation.1 | async-start | bytes 65536 | tf_op jit(solution)/shard_map/all_to_all | solution.py:409
  47.1 3.5 %all-to-all-done.1 = f32[8,8,128]{2,1,0:T(8,128)S(1)} async-done(((f32[8,8,128]{2,1,0:T(8,128)}), f32[8,8,128]{2,1,0:T(8,128)S(1)}, u32[]{:S(2)}, u32[]{:S(2)}) %all-to-all-start.1) | async-done | bytes 32800 | tf_op jit(solution)/shard_map/all_to_all | solution.py:409
  52.6 4.2 %all-to-all-start.2 = ((f32[8,104,128]{2,1,0:T(8,128)}), f32[8,104,128]{2,1,0:T(8,128)S(1)}, u32[]{:S(2)}, u32[]{:S(2)}) async-start(f32[8,104,128]{2,1,0:T(8,128)} %select.6), calls=%async_computation.2 | async-start | bytes 851968 | tf_op jit(solution)/shard_map/all_to_all | solution.py:421
  57.0 7.9 %all-to-all-done.2.across = f32[8,104,128]{2,1,0:T(8,128)S(1)} async-done(((f32[8,104,128]{2,1,0:T(8,128)}), f32[8,104,128]{2,1,0:T(8,128)S(1)}, u32[]{:S(2)}, u32[]{:S(2)}) %all-to-all-start.2) | async-done | bytes 426016 | tf_op jit(solution)/shard_map/all_to_all | solution.py:421
  68.3 4.0 %collective-permute-start.4 = (f32[5,8,128]{2,1,0:T(8,128)S(1)}, f32[5,8,128]{2,1,0:T(8,128)S(1)}, u32[]{:S(2)}, u32[]{:S(2)}) collective-permute-start(f32[5,8,128]{2,1,0:T(8,128)S(1)} %get-tuple-element.42), channel_id=1, source_target_pairs={{0,64},{64,128},{128,192},{1,65},{65,129},{129,193},{2,66},{66,130... | collective-permute-start | bytes 61448 | tf_op jit(solution)/shard_map/ppermute | solution.py:394
  73.6 3.2 %collective-permute-done.5.up = f32[8,128]{1,0:T(8,128)S(1)} collective-permute-done((f32[8,128]{1,0:T(8,128)S(1)}, f32[8,128]{1,0:T(8,128)S(1)}, u32[]{:S(2)}, u32[]{:S(2)}) %collective-permute-start.5) | collective-permute-done | bytes 4128 | tf_op jit(solution)/shard_map/ppermute | solution.py:395
  78.0 13.5 %all-to-all-start.3 = ((f32[8,48,128]{2,1,0:T(8,128)}), f32[8,48,128]{2,1,0:T(8,128)}, u32[]{:S(2)}, u32[]{:S(2)}) async-start(f32[8,48,128]{2,1,0:T(8,128)} %gather.5), calls=%async_computation.3 | async-start | bytes 393216 | tf_op jit(solution)/shard_map/all_to_all | solution.py:406
  92.5 3.5 %bulk.3 = (f32[5,16,16,128]{3,2,1,0:T(8,128)S(1)}, f32[2,16,128]{2,1,0:T(8,128)S(1)}) custom-call(s32[6]{0:T(128)S(1)} %stack.15.ids, f32[5,16,16,128]{3,2,1,0:T(8,128)S(1)} %get-tuple-element.36.field, f32[13,16,16,128]{3,2,1,0:T(8,128)S(1)} %coef.1, f32[80,128]{1,0:T(8,128)S(1)} %broadcast_in_dim.7.matrix, f32[8,104,128]{2,1,0:T(8,128)S(1)} %all-to-all-done.2.across, ...), custom_call_target="tpu_custom_call" | custom-call | flops 9830400 | bytes 3579904 | tf_op jit(solution)/shard_map/bulk/pallas_call | solution.py:32
  96.0 5.4 %all-to-all-done.3.got = f32[8,48,128]{2,1,0:T(8,128)} async-done(((f32[8,48,128]{2,1,0:T(8,128)}), f32[8,48,128]{2,1,0:T(8,128)}, u32[]{:S(2)}, u32[]{:S(2)}) %all-to-all-start.3) | async-done | bytes 196640 | tf_op jit(solution)/shard_map/all_to_all | solution.py:406
  102.9 14.2 %all_to_all.45.across = f32[8,88,128]{2,1,0:T(8,128)S(1)} all-to-all(f32[8,88,128]{2,1,0:T(8,128)S(1)} %select.7), channel_id=1, replica_groups=mesh['sec'=4,'row'=8,'rad'=8] {'row'}, dimensions={0} | all-to-all | bytes 720896 | tf_op jit(solution)/shard_map/all_to_all | solution.py:421
  121.8 3.1 %collective-permute-done.7.up = f32[8,128]{1,0:T(8,128)S(1)} collective-permute-done((f32[8,128]{1,0:T(8,128)S(1)}, f32[8,128]{1,0:T(8,128)S(1)}, u32[]{:S(2)}, u32[]{:S(2)}) %collective-permute-start.7) | collective-permute-done | bytes 4128 | tf_op jit(solution)/shard_map/ppermute | solution.py:395
  126.1 4.0 %all-to-all-start.5 = ((f32[8,48,128]{2,1,0:T(8,128)}), f32[8,48,128]{2,1,0:T(8,128)}, u32[]{:S(2)}, u32[]{:S(2)}) async-start(f32[8,48,128]{2,1,0:T(8,128)} %gather.6), calls=%async_computation.5 | async-start | bytes 393216 | tf_op jit(solution)/shard_map/all_to_all | solution.py:406
  131.0 3.5 %bulk.4 = (f32[5,16,16,128]{3,2,1,0:T(8,128)S(1)}, f32[2,16,128]{2,1,0:T(8,128)S(1)}) custom-call(s32[6]{0:T(128)S(1)} %stack.15.ids, f32[5,16,16,128]{3,2,1,0:T(8,128)S(1)} %get-tuple-element.41.field, f32[13,16,16,128]{3,2,1,0:T(8,128)S(1)} %coef.1, f32[80,128]{1,0:T(8,128)S(1)} %broadcast_in_dim.7.matrix, f32[8,88,128]{2,1,0:T(8,128)S(1)} %all_to_all.45.across, ...), custom_call_target="tpu_custom_call" | custom-call | flops 9830400 | bytes 3514368 | tf_op jit(solution)/shard_map/bulk/pallas_call | solution.py:32
  134.5 5.5 %all-to-all-done.5.got = f32[8,48,128]{2,1,0:T(8,128)} async-done(((f32[8,48,128]{2,1,0:T(8,128)}), f32[8,48,128]{2,1,0:T(8,128)}, u32[]{:S(2)}, u32[]{:S(2)}) %all-to-all-start.5) | async-done | bytes 196640 | tf_op jit(solution)/shard_map/all_to_all | solution.py:406
  141.4 13.1 %all_to_all.46.across = f32[8,80,128]{2,1,0:T(8,128)S(1)} all-to-all(f32[8,80,128]{2,1,0:T(8,128)S(1)} %select.8), channel_id=1, replica_groups=mesh['sec'=4,'row'=8,'rad'=8] {'row'}, dimensions={0} | all-to-all | bytes 655360 | tf_op jit(solution)/shard_map/all_to_all | solution.py:421
  162.5 3.4 %all-to-all-start.7 = ((f32[8,48,128]{2,1,0:T(8,128)}), f32[8,48,128]{2,1,0:T(8,128)S(1)}, u32[]{:S(2)}, u32[]{:S(2)}) async-start(f32[8,48,128]{2,1,0:T(8,128)} %gather.7), calls=%async_computation.7 | async-start | bytes 393216 | tf_op jit(solution)/shard_map/all_to_all | solution.py:406
  165.9 3.5 %bulk.5 = (f32[5,16,16,128]{3,2,1,0:T(8,128)S(1)}, f32[2,16,128]{2,1,0:T(8,128)S(1)}) custom-call(s32[6]{0:T(128)S(1)} %stack.15.ids, f32[5,16,16,128]{3,2,1,0:T(8,128)S(1)} %get-tuple-element.46.field, f32[13,16,16,128]{3,2,1,0:T(8,128)S(1)} %coef.1, f32[80,128]{1,0:T(8,128)S(1)} %broadcast_in_dim.7.matrix, f32[8,80,128]{2,1,0:T(8,128)S(1)} %all_to_all.46.across, ...), custom_call_target="tpu_custom_call" | custom-call | flops 9830400 | bytes 3481600 | tf_op jit(solution)/shard_map/bulk/pallas_call | solution.py:32
  170.3 5.2 %all-to-all-done.7.got = f32[8,48,128]{2,1,0:T(8,128)S(1)} async-done(((f32[8,48,128]{2,1,0:T(8,128)}), f32[8,48,128]{2,1,0:T(8,128)S(1)}, u32[]{:S(2)}, u32[]{:S(2)}) %all-to-all-start.7) | async-done | bytes 196640 | tf_op jit(solution)/shard_map/all_to_all | solution.py:406
  176.5 12.2 %all_to_all.47.across = f32[8,64,128]{2,1,0:T(8,128)S(1)} all-to-all(f32[8,64,128]{2,1,0:T(8,128)S(1)} %select.9), channel_id=1, replica_groups=mesh['sec'=4,'row'=8,'rad'=8] {'row'}, dimensions={0} | all-to-all | bytes 524288 | tf_op jit(solution)/shard_map/all_to_all | solution.py:421
  189.8 3.3 %last.1 = f32[5,16,8,128]{3,2,1,0:T(8,128)} custom-call(s32[6]{0:T(128)S(1)} %stack.15.ids, s32[32]{0:T(128)S(1)} %convert_bitcast_fusion.1.donors, f32[5]{0:T(128)S(1)} %copy-done.22, f32[5]{0:T(128)S(1)} %copy-done.23, f32[5,16,16,128]{3,2,1,0:T(8,128)S(1)} %copy-done.3, f32[13,16,16,128]{3,2,1,0:T(8,128)S(1)} %coef.1, ...), custom_call_target="tpu_custom_call" | custom-call | flops 9830400 | bytes 2990080 | tf_op jit(solution)/shard_map/last/pallas_call | solution.py:32
  (91 shorter events, 44.7 us)
Async XLA Ops:
  6.6 39.3 %copy-start.1 = (f32[5,1,16,8,128]{4,3,2,1,0:T(8,128)S(1)}, f32[5,1,16,8,128]{4,3,2,1,0:T(8,128)}, u32[]{:S(2)}) copy-start(f32[5,1,16,8,128]{4,3,2,1,0:T(8,128)} %param.13) | copy-start | bytes 983044
  6.6 39.3 %copy-start.7 = (f32[1,16,8,128]{3,2,1,0:T(8,128)S(1)}, f32[1,16,8,128]{3,2,1,0:T(8,128)}, u32[]{:S(2)}) copy-start(f32[1,16,8,128]{3,2,1,0:T(8,128)} %param.14) | copy-start | bytes 196612
  6.6 39.3 %copy-start.9 = (f32[1,16,8,128]{3,2,1,0:T(8,128)S(1)}, f32[1,16,8,128]{3,2,1,0:T(8,128)}, u32[]{:S(2)}) copy-start(f32[1,16,8,128]{3,2,1,0:T(8,128)} %param.15) | copy-start | bytes 196612
  6.6 39.3 %copy-start.11 = (f32[1,16,8,128]{3,2,1,0:T(8,128)S(1)}, f32[1,16,8,128]{3,2,1,0:T(8,128)}, u32[]{:S(2)}) copy-start(f32[1,16,8,128]{3,2,1,0:T(8,128)} %param.16) | copy-start | bytes 196612
  6.6 39.3 %copy-start.13 = (f32[1,16,8,128]{3,2,1,0:T(8,128)S(1)}, f32[1,16,8,128]{3,2,1,0:T(8,128)}, u32[]{:S(2)}) copy-start(f32[1,16,8,128]{3,2,1,0:T(8,128)} %param.17) | copy-start | bytes 196612
  6.6 39.3 %copy-start.15 = (f32[1,16,8,128]{3,2,1,0:T(8,128)S(1)}, f32[1,16,8,128]{3,2,1,0:T(8,128)}, u32[]{:S(2)}) copy-start(f32[1,16,8,128]{3,2,1,0:T(8,128)} %param.18) | copy-start | bytes 196612
  7.3 7.1 %collective-permute-start.1 = (f32[8,128]{1,0:T(8,128)S(1)}, f32[8,128]{1,0:T(8,128)S(1)}, u32[]{:S(2)}, u32[]{:S(2)}) collective-permute-start(f32[8,128]{1,0:T(8,128)S(1)} %get-tuple-element.31), channel_id=1, source_target_pairs={{64,0},{128,64},{192,128},{65,1},{129,65},{193,129},{66,2},{130,66... | collective-permute-start | bytes 12296 | tf_op jit(solution)/shard_map/ppermute | solution.py:395
  8.6 5.9 %collective-permute-start = (f32[5,8,128]{2,1,0:T(8,128)S(1)}, f32[5,8,128]{2,1,0:T(8,128)S(1)}, u32[]{:S(2)}, u32[]{:S(2)}) collective-permute-start(f32[5,8,128]{2,1,0:T(8,128)S(1)} %get-tuple-element.30), channel_id=1, source_target_pairs={{0,64},{64,128},{128,192},{1,65},{65,129},{129,193},{2,66},{66,130... | collective-permute-start | bytes 61448 | tf_op jit(solution)/shard_map/ppermute | solution.py:394
  16.4 40.4 %copy-start.24 = (f32[1,3,5,5]{3,0,2,1:T(1,128)S(1)}, f32[1,3,5,5]{3,0,2,1:T(1,128)}, u32[]{:S(2)}) copy-start(f32[1,3,5,5]{3,0,2,1:T(1,128)} %param.19) | copy-start | bytes 904
  16.4 20.5 %all-to-all-start = ((f32[8,56,128]{2,1,0:T(8,128)}), f32[8,56,128]{2,1,0:T(8,128)S(1)}, u32[]{:S(2)}, u32[]{:S(2)}) async-start(f32[8,56,128]{2,1,0:T(8,128)} %gather.4), calls=%async_computation | async-start | bytes 458752 | tf_op jit(solution)/shard_map/all_to_all | solution.py:406
  27.0 18.8 %collective-permute-start.2 = (f32[80,8,128]{2,1,0:T(8,128)S(1)}, f32[80,8,128]{2,1,0:T(8,128)S(1)}, u32[]{:S(2)}, u32[]{:S(2)}) collective-permute-start(f32[80,8,128]{2,1,0:T(8,128)S(1)} %get-tuple-element.34), channel_id=1, source_target_pairs={{0,1},{1,2},{2,3},{3,4},{4,5},{5,6},{6,7},{8,9},{9,10},{10,11},{11... | collective-permute-start | bytes 983048 | tf_op jit(solution)/shard_map/ppermute | solution.py:397
  30.4 15.4 %collective-permute-start.3 = (f32[80,8,128]{2,1,0:T(8,128)S(1)}, f32[80,8,128]{2,1,0:T(8,128)S(1)}, u32[]{:S(2)}, u32[]{:S(2)}) collective-permute-start(f32[80,8,128]{2,1,0:T(8,128)S(1)} %get-tuple-element.35), channel_id=1, source_target_pairs={{1,0},{2,1},{3,2},{4,3},{5,4},{6,5},{7,6},{9,8},{10,9},{11,10},{12... | collective-permute-start | bytes 983048 | tf_op jit(solution)/shard_map/ppermute | solution.py:398
  38.2 12.4 %all-to-all-start.1 = ((f32[8,8,128]{2,1,0:T(8,128)}), f32[8,8,128]{2,1,0:T(8,128)S(1)}, u32[]{:S(2)}, u32[]{:S(2)}) async-start(f32[8,8,128]{2,1,0:T(8,128)} %get-tuple-element.38), calls=%async_computation.1 | async-start | bytes 65536 | tf_op jit(solution)/shard_map/all_to_all | solution.py:409
  52.6 14.3 %copy-start.23 = (f32[5]{0:T(128)S(1)}, f32[5]{0:T(128)}, u32[]{:S(2)}) copy-start(f32[5]{0:T(128)} %coupling.7) | copy-start | bytes 64
  52.6 12.3 %all-to-all-start.2 = ((f32[8,104,128]{2,1,0:T(8,128)}), f32[8,104,128]{2,1,0:T(8,128)S(1)}, u32[]{:S(2)}, u32[]{:S(2)}) async-start(f32[8,104,128]{2,1,0:T(8,128)} %select.6), calls=%async_computation.2 | async-start | bytes 851968 | tf_op jit(solution)/shard_map/all_to_all | solution.py:421
  68.3 8.5 %collective-permute-start.4 = (f32[5,8,128]{2,1,0:T(8,128)S(1)}, f32[5,8,128]{2,1,0:T(8,128)S(1)}, u32[]{:S(2)}, u32[]{:S(2)}) collective-permute-start(f32[5,8,128]{2,1,0:T(8,128)S(1)} %get-tuple-element.42), channel_id=1, source_target_pairs={{0,64},{64,128},{128,192},{1,65},{65,129},{129,193},{2,66},{66,130... | collective-permute-start | bytes 61448 | tf_op jit(solution)/shard_map/ppermute | solution.py:394
  72.3 4.5 %collective-permute-start.5 = (f32[8,128]{1,0:T(8,128)S(1)}, f32[8,128]{1,0:T(8,128)S(1)}, u32[]{:S(2)}, u32[]{:S(2)}) collective-permute-start(f32[8,128]{1,0:T(8,128)S(1)} %get-tuple-element.43), channel_id=1, source_target_pairs={{64,0},{128,64},{192,128},{65,1},{129,65},{193,129},{66,2},{130,66... | collective-permute-start | bytes 12296 | tf_op jit(solution)/shard_map/ppermute | solution.py:395
  78.0 23.3 %all-to-all-start.3 = ((f32[8,48,128]{2,1,0:T(8,128)}), f32[8,48,128]{2,1,0:T(8,128)}, u32[]{:S(2)}, u32[]{:S(2)}) async-start(f32[8,48,128]{2,1,0:T(8,128)} %gather.5), calls=%async_computation.3 | async-start | bytes 393216 | tf_op jit(solution)/shard_map/all_to_all | solution.py:406
  117.9 6.9 %collective-permute-start.6 = (f32[5,8,128]{2,1,0:T(8,128)S(1)}, f32[5,8,128]{2,1,0:T(8,128)S(1)}, u32[]{:S(2)}, u32[]{:S(2)}) collective-permute-start(f32[5,8,128]{2,1,0:T(8,128)S(1)} %get-tuple-element.47), channel_id=1, source_target_pairs={{0,64},{64,128},{128,192},{1,65},{65,129},{129,193},{2,66},{66,130... | collective-permute-start | bytes 61448 | tf_op jit(solution)/shard_map/ppermute | solution.py:394
  120.5 4.4 %collective-permute-start.7 = (f32[8,128]{1,0:T(8,128)S(1)}, f32[8,128]{1,0:T(8,128)S(1)}, u32[]{:S(2)}, u32[]{:S(2)}) collective-permute-start(f32[8,128]{1,0:T(8,128)S(1)} %get-tuple-element.48), channel_id=1, source_target_pairs={{64,0},{128,64},{192,128},{65,1},{129,65},{193,129},{66,2},{130,66... | collective-permute-start | bytes 12296 | tf_op jit(solution)/shard_map/ppermute | solution.py:395
  126.1 13.9 %all-to-all-start.5 = ((f32[8,48,128]{2,1,0:T(8,128)}), f32[8,48,128]{2,1,0:T(8,128)}, u32[]{:S(2)}, u32[]{:S(2)}) async-start(f32[8,48,128]{2,1,0:T(8,128)} %gather.6), calls=%async_computation.5 | async-start | bytes 393216 | tf_op jit(solution)/shard_map/all_to_all | solution.py:406
  155.3 6.0 %collective-permute-start.8 = (f32[5,8,128]{2,1,0:T(8,128)S(1)}, f32[5,8,128]{2,1,0:T(8,128)S(1)}, u32[]{:S(2)}, u32[]{:S(2)}) collective-permute-start(f32[5,8,128]{2,1,0:T(8,128)S(1)} %get-tuple-element.52), channel_id=1, source_target_pairs={{0,64},{64,128},{128,192},{1,65},{65,129},{129,193},{2,66},{66,130... | collective-permute-start | bytes 61448 | tf_op jit(solution)/shard_map/ppermute | solution.py:394
  156.9 4.4 %collective-permute-start.9 = (f32[8,128]{1,0:T(8,128)S(1)}, f32[8,128]{1,0:T(8,128)S(1)}, u32[]{:S(2)}, u32[]{:S(2)}) collective-permute-start(f32[8,128]{1,0:T(8,128)S(1)} %get-tuple-element.53), channel_id=1, source_target_pairs={{64,0},{128,64},{192,128},{65,1},{129,65},{193,129},{66,2},{130,66... | collective-permute-start | bytes 12296 | tf_op jit(solution)/shard_map/ppermute | solution.py:395
  162.5 13.0 %all-to-all-start.7 = ((f32[8,48,128]{2,1,0:T(8,128)}), f32[8,48,128]{2,1,0:T(8,128)S(1)}, u32[]{:S(2)}, u32[]{:S(2)}) async-start(f32[8,48,128]{2,1,0:T(8,128)} %gather.7), calls=%async_computation.7 | async-start | bytes 393216 | tf_op jit(solution)/shard_map/all_to_all | solution.py:406
  (17 other events, 48.1 us)

commit v4 on v3

--- a/solution.py
+++ b/solution.py
@@ -7,6 +7,7 @@
 from jax.experimental.pallas import tpu as pltpu
 from jax.sharding import PartitionSpec as P
 
+
 STEPS = 4
 time_step = 0.08
 INTERPRET = False
@@ -27,7 +28,7 @@
     return pl.BlockSpec(memory_space=pltpu.SMEM)
 
 
-def call(kernel, outs, scalars, arrays, name, flops=0, scratch=()):
+def call(kernel, outs, scalars, arrays, flops=0, scratch=(), limit=VMEM_LIMIT):
     moved = sum(a.size * 4 for a in arrays) + sum(4 * functools.reduce(lambda x, y: x * y, o) for o in outs)
     return pl.pallas_call(
         kernel,
@@ -35,8 +36,7 @@
         in_specs=[smem() for _ in scalars] + [vmem() for _ in arrays],
         out_specs=[vmem() for _ in outs],
         scratch_shapes=list(scratch),
-        name=name,
-        compiler_params=pltpu.CompilerParams(vmem_limit_bytes=VMEM_LIMIT),
+        compiler_params=pltpu.CompilerParams(vmem_limit_bytes=limit),
         cost_estimate=pl.CostEstimate(flops=flops, bytes_accessed=moved, transcendentals=0),
         interpret=INTERPRET,
     )(*scalars, *arrays)
@@ -92,10 +92,7 @@
 
 
 def gather_kernel(first_step, ids, down, up, inflow, out_pressure, *refs):
-    if first_step:
-        donors, send = refs
-    else:
-        (send,) = refs
+    others, send = refs
     section = ids[0]
     size = send.shape[0]
     for v in range(NV):
@@ -106,10 +103,11 @@
     for j in range(size):
         send[j, 40:48, :] = value
         if first_step:
-            send[j, 48:56, :] = donors[...]
-
-
-def wanted_kernel(ids, got, send, mine):
+            for w in range(others.shape[0]):
+                send[j, 48 + w : 49 + w, :] = others[w, 0:1, :]
+
+
+def wanted_kernel(ids, got, lists):
     rad, rad_size = ids[2], ids[3]
     lanes = lanes_of((8, 128))
     below = got[jnp.maximum(rad - 1, 0), 48:56, :]
@@ -117,10 +115,7 @@
     own = got[rad, 48:56, :]
     down = jnp.where(lanes < 4, roll(below, -4, 1), jnp.where(lanes < 12, roll(own, 4, 1), roll(above, 12, 1)))
     up = jnp.where(lanes < 20, roll(below, 4, 1), jnp.where(lanes < 28, roll(own, 12, 1), roll(above, 20, 1)))
-    both = jnp.where(lanes < 16, down, up)
-    mine[...] = both
-    for j in range(send.shape[0]):
-        send[j] = both
+    lists[...] = jnp.where(lanes < 16, down, up)
 
 
 def extend_kernel(state, volume, axial, radial, circ, mu, from_below, from_above, field, raw, edges):
@@ -257,25 +252,25 @@
     return total
 
 
-def ghosts_of(step, donors, weight, coupling, field, across, ghost):
+def ghosts_of(step, ids, wanted, weight, coupling, field, across, ghost):
     rows, _ = picked(step)
     count = len(rows)
     ghost[...] = jnp.zeros(ghost.shape, jnp.float32)
     for n, i in enumerate(rows):
-        d = donors[i] >> 6
+        d = wanted[ids[1], i] >> 6
         for v in range(NV):
             ghost[v, i : i + 1, :] = across[d, v * count + n : v * count + n + 1, :]
-        e = donors[16 + i] >> 6
+        e = wanted[ids[1], 16 + i] >> 6
         ghost[NV, i : i + 1, :] = across[e, NV * count + n : NV * count + n + 1, :]
     outlet = [field[v, PLANES - 1] for v in range(NV)]
     jump = ghost[NV] - pressure(weight, outlet)
     return [ghost[v] for v in range(NV)], [outlet[v] + coupling[v] * jump for v in range(NV)]
 
 
-def ends_of(step, ids, donors, weight, coupling, field, coef, matrix, across, ghost):
+def ends_of(step, ids, wanted, weight, coupling, field, coef, matrix, across, ghost):
     lanes = lanes_of((ROWS, 128))
     left, right = sides(ids, across, picked(step)[1])
-    inlet_ghost, outlet_ghost = ghosts_of(step, donors, weight, coupling, field, across, ghost)
+    inlet_ghost, outlet_ghost = ghosts_of(step, ids, wanted, weight, coupling, field, across, ghost)
     plane = lambda k: [field[v, k] for v in range(NV)]
     new_inlet = advance(0, inlet_ghost, plane(0), plane(1), coef, matrix, left, right, lanes)
     last = PLANES - 1
@@ -283,8 +278,8 @@
     return new_inlet, new_outlet
 
 
-def ends_kernel(step, ids, donors, weight, coupling, field, coef, matrix, across, ends, down, up, ghost):
-    new_inlet, new_outlet = ends_of(step, ids, donors, weight, coupling, field, coef, matrix, across, ghost)
+def ends_kernel(step, ids, wanted, weight, coupling, field, coef, matrix, across, ends, down, up, ghost):
+    new_inlet, new_outlet = ends_of(step, ids, wanted, weight, coupling, field, coef, matrix, across, ghost)
     for v in range(NV):
         ends[0, v] = new_inlet[v]
         ends[1, v] = new_outlet[v]
@@ -321,10 +316,10 @@
     edges[1] = first
 
 
-def last_kernel(step, ids, donors, weight, coupling, field, coef, matrix, across, new, ghost):
+def last_kernel(step, ids, wanted, weight, coupling, field, coef, matrix, across, new, ghost):
     lanes = lanes_of((ROWS, 128))
     left, right = sides(ids, across, picked(step)[1])
-    new_inlet, new_outlet = ends_of(step, ids, donors, weight, coupling, field, coef, matrix, across, ghost)
+    new_inlet, new_outlet = ends_of(step, ids, wanted, weight, coupling, field, coef, matrix, across, ghost)
     for v in range(NV):
         new[v, 0] = new_inlet[v][WIDE : WIDE + 8]
         new[v, PLANES - 1] = new_outlet[v][WIDE : WIDE + 8]
@@ -369,7 +364,7 @@
     ).astype(jnp.int32)
     own = [state[:, 0], volume[0], face_axial[0], face_radial[0], face_circum[0], viscosity[0]]
     donors = jnp.concatenate([down_donors[0], up_donors[0]]).astype(jnp.float32)
-    donors = jnp.broadcast_to(jnp.pad(donors, (0, 112))[None], (8, 128))
+    donors = jnp.broadcast_to(jnp.pad(donors, (0, 112))[None, None], (row_size, 8, 128))
     matrix = jnp.broadcast_to(jnp.pad(flux_matrix[0].reshape(75), (0, 5))[:, None], (80, 128))
     extended = (NV, PLANES, ROWS, 128)
     strips = (2, ROWS, 128)
@@ -381,54 +376,45 @@
         [sent, sent, (NV, 8, 128), (8, 128), (8, 128)],
         [pressure_weight],
         own + [outflow_plane],
-        "first",
+        limit=60 * 1024 * 1024,
     )
     forward = [(i, i + 1) for i in range(sections - 1)]
     backward = [(i + 1, i) for i in range(sections - 1)]
     outward = [(i, i + 1) for i in range(rad_size - 1)]
     inward = [(i + 1, i) for i in range(rad_size - 1)]
-    field = coef = edges = wanted = mine = None
+    from_below = lax.ppermute(to_above, "rad", outward)
+    from_above = lax.ppermute(to_below, "rad", inward)
+    table = lax.all_to_all(donors, "row", 0, 0)
+    field = coef = edges = wanted = None
     for step in range(STEPS):
         last_step = step == STEPS - 1
-        rows, base = picked(step)
+        _, base = picked(step)
         down = lax.ppermute(down, "sec", forward)
         up = lax.ppermute(up, "sec", backward)
-        if step == 0:
-            from_below = lax.ppermute(to_above, "rad", outward)
-            from_above = lax.ppermute(to_below, "rad", inward)
         (send,) = call(
             functools.partial(gather_kernel, step == 0),
             [(rad_size, TILE_ROWS + (8 if step == 0 else 0), 128)],
             [ids],
-            [down, up, inflow_plane, out_pressure] + ([donors] if step == 0 else []),
-            "gather",
+            [down, up, inflow_plane, out_pressure, table if step == 0 else edges],
         )
         got = lax.all_to_all(send, "rad", 0, 0)
         if step == 0:
-            lists, mine = call(wanted_kernel, [(row_size, 8, 128), (8, 128)], [ids], [got], "wanted")
-            wanted = lax.all_to_all(lists, "row", 0, 0)[:, 0, :32].astype(jnp.int32)
-            mine = mine[0, :32].astype(jnp.int32)
-            field, raw, edges = call(
-                extend_kernel, [extended, extended, strips], [], own + [from_below, from_above], "extend"
-            )
+            (lists,) = call(wanted_kernel, [(8, 128)], [ids], [got])
+            wanted = lists[:, :32].astype(jnp.int32)
+            field, raw, edges = call(extend_kernel, [extended, extended, strips], [], own + [from_below, from_above])
         (send,) = call(
-            functools.partial(select_kernel, step),
-            [(row_size, base + ROWS, 128)],
-            [ids, wanted],
-            [got, edges],
-            "select",
+            functools.partial(select_kernel, step), [(row_size, base + ROWS, 128)], [ids, wanted], [got, edges]
         )
         across = lax.all_to_all(send, "row", 0, 0)
         if step == 0:
-            (coef,) = call(coef_kernel, [(13, PLANES, ROWS, 128)], [ids], [raw, across], "coef")
+            (coef,) = call(coef_kernel, [(13, PLANES, ROWS, 128)], [ids], [raw, across])
         ghost = [pltpu.VMEM((NV + 1, ROWS, 128), jnp.float32)]
         if last_step:
             (field,) = call(
                 functools.partial(last_kernel, step),
                 [(NV, PLANES, 8, 128)],
-                [ids, mine] + scalars,
+                [ids, wanted] + scalars,
                 [field, coef, matrix, across],
-                "last",
                 flops=PLANES * ROWS * 128 * 300,
                 scratch=ghost,
             )
@@ -436,9 +422,8 @@
             ends, down, up = call(
                 functools.partial(ends_kernel, step),
                 [(2, NV, ROWS, 128), (NV, 8, 128), (8, 128)],
-                [ids, mine] + scalars,
+                [ids, wanted] + scalars,
                 [field, coef, matrix, across],
-                "ends",
                 flops=2 * ROWS * 128 * 300,
                 scratch=ghost,
             )
@@ -447,7 +432,6 @@
                 [extended, strips],
                 [ids],
                 [field, coef, matrix, across, ends],
-                "bulk",
                 flops=PLANES * ROWS * 128 * 300,
             )
     return field[:, None]
@@ -470,4 +454,5 @@
         P(),
     )
     out_specs = P(None, "sec", None, "rad", "row")
+
     return jax.shard_map(body, mesh=mesh, in_specs=in_specs, out_specs=out_specs, check_vma=False)

time: 195 us -> 200 us (1.026)
  blocking collectives: 39.5 us -> 91.4 us
  waiting for transfers between devices: 42.1 us -> 20.8 us
  starting transfers between devices: 66.4 us -> 48.3 us
  local copies, waits for them, and re-layouts: 11.9 us -> 6.5 us
    all_to_all x0 -> x3, blocking collectives: none -> 53.1 us  [body(): got = lax.all_to_all(send, 'rad', 0, 0)]
    all_to_all x4 -> x1, starting transfers between devices: 31.5 us -> 9.69 us  [body(): got = lax.all_to_all(send, 'rad', 0, 0)]
    all_to_all x4 -> x1, waiting for transfers between devices: 21.3 us -> 0.01 us  [body(): got = lax.all_to_all(send, 'rad', 0, 0)]
    unnamed x50 -> x26, local copies, waits for them, and re-layouts: 11.6 us -> 5.63 us
    ppermute x4, waiting for transfers between devices: 9.31 us -> 3.37 us  [body(): up = lax.ppermute(up, 'sec', backward)]
    ppermute x1, waiting for transfers between devices: 0.01 us -> 5.31 us  [body(): from_below = lax.ppermute(to_above, 'rad', outward)]
    ppermute x1, waiting for transfers between devices: 0.01 us -> 4.2 us  [body(): from_above = lax.ppermute(to_below, 'rad', inward)]
    all_to_all x1, waiting for transfers between devices: 3.49 us -> 0.01 us  [body(): table = lax.all_to_all(donors, 'row', 0, 0)]
  transfers between devices with their start and end apart: 16 -> 13, of which waited for: 9 -> 4; matrix products, arithmetic and copies ran while one was open for 0% -> 0% of each run, Pallas kernels for 7% -> 7%
where the time goes in v4:
time: 200 us; the launch traced here: 199 us
  blocking collectives  91.4 us (46%)
  starting transfers between devices  48.3 us (24%)
  Pallas kernels  30.5 us (15%)
  waiting for transfers between devices  20.8 us (10%)
  local copies, waits for them, and re-layouts  6.5 us (3%)
    all_to_all x3, blocking collectives, body(): got = lax.all_to_all(send, 'rad', 0, 0)  53.1 us
    all_to_all x3, blocking collectives, body(): across = lax.all_to_all(send, 'row', 0, 0)  38.3 us
    pallas_call x19, Pallas kernels, call(): pl.pallas_call(kernel, out_shape=[jax.ShapeDtypeStruct(o, jnp.float32) fo...  30.5 us
    ppermute x4, starting transfers between devices, body(): down = lax.ppermute(down, 'sec', forward)  15.5 us
    all_to_all x1, starting transfers between devices, body(): got = lax.all_to_all(send, 'rad', 0, 0)  9.69 us
    all_to_all x1, waiting for transfers between devices, body(): across = lax.all_to_all(send, 'row', 0, 0)  7.88 us
    all_to_all x1, starting transfers between devices, body(): across = lax.all_to_all(send, 'row', 0, 0)  6.82 us
    all_to_all x1, starting transfers between devices, body(): table = lax.all_to_all(donors, 'row', 0, 0)  6.43 us
  transfers between devices with their start and end apart: 13, of which 4 were waited for; matrix products, arithmetic and copies ran while one was open for 0% of the time, Pallas kernels for 7%

profile of v4, /device:TPU:1, one launch (start us, length us, event | category | flops | bytes accessed | tf_op | source)
XLA Modules:
  0.0 198.6 jit_solution(14425409352118678422)
XLA Ops:
  1.4 6.4 %all-to-all-start = ((f32[8,8,128]{2,1,0:T(8,128)}), f32[8,8,128]{2,1,0:T(8,128)S(1)}, u32[]{:S(2)}, u32[]{:S(2)}) async-start(f32[8,8,128]{2,1,0:T(8,128)} %broadcast_in_dim.6), calls=%async_computation | async-start | bytes 65536 | tf_op jit(solution)/shard_map/all_to_all | solution.py:387
  7.8 2.1 %shard_map.127 = (f32[80,8,128]{2,1,0:T(8,128)}, f32[80,8,128]{2,1,0:T(8,128)}, f32[5,8,128]{2,1,0:T(8,128)}, f32[8,128]{1,0:T(8,128)}, f32[8,128]{1,0:T(8,128)}) custom-call(f32[5]{0:T(128)} %weight.9, f32[5,16,8,128]{3,2,1,0:T(8,128)} %bitcast.14, f32[16,8,128]{2,1,0:T(8,128)} %bitcast.16, f32[16,8,128]{2,1,0:T(8,128)} %bitcast.18, ...), custom_call_target="tpu_custom_call" | custom-call | bytes 1359872 | tf_op jit(solution)/shard_map/pallas_call | solution.py:33
  9.9 3.1 %collective-permute-start = (f32[5,8,128]{2,1,0:T(8,128)}, f32[5,8,128]{2,1,0:T(8,128)S(1)}, u32[]{:S(2)}, u32[]{:S(2)}) collective-permute-start(f32[5,8,128]{2,1,0:T(8,128)} %get-tuple-element.28), channel_id=1, source_target_pairs={{0,64},{64,128},{128,192},{1,65},{65,129},{129,193},{2,66},{66,130... | collective-permute-start | bytes 61448 | tf_op jit(solution)/shard_map/ppermute | solution.py:392
  14.4 3.4 %collective-permute-done.1.up = f32[8,128]{1,0:T(8,128)S(1)} collective-permute-done((f32[8,128]{1,0:T(8,128)}, f32[8,128]{1,0:T(8,128)S(1)}, u32[]{:S(2)}, u32[]{:S(2)}) %collective-permute-start.1) | collective-permute-done | bytes 4128 | tf_op jit(solution)/shard_map/ppermute | solution.py:393
  20.4 9.7 %all-to-all-start.1 = ((f32[8,56,128]{2,1,0:T(8,128)}), f32[8,56,128]{2,1,0:T(8,128)S(1)}, u32[]{:S(2)}, u32[]{:S(2)}) async-start(f32[8,56,128]{2,1,0:T(8,128)} %shard_map.128), calls=%async_computation.1 | async-start | bytes 458752 | tf_op jit(solution)/shard_map/all_to_all | solution.py:400
  30.1 3.4 %collective-permute-start.2 = (f32[80,8,128]{2,1,0:T(8,128)}, f32[80,8,128]{2,1,0:T(8,128)S(1)}, u32[]{:S(2)}, u32[]{:S(2)}) collective-permute-start(f32[80,8,128]{2,1,0:T(8,128)} %get-tuple-element.31), channel_id=1, source_target_pairs={{0,1},{1,2},{2,3},{3,4},{4,5},{5,6},{6,7},{8,9},{9,10},{10,11},{11... | collective-permute-start | bytes 983048 | tf_op jit(solution)/shard_map/ppermute | solution.py:385
  34.8 5.3 %collective-permute-done.2.from_below = f32[80,8,128]{2,1,0:T(8,128)S(1)} collective-permute-done((f32[80,8,128]{2,1,0:T(8,128)}, f32[80,8,128]{2,1,0:T(8,128)S(1)}, u32[]{:S(2)}, u32[]{:S(2)}) %collective-permute-start.2) | collective-permute-done | bytes 327712 | tf_op jit(solution)/shard_map/ppermute | solution.py:385
  40.1 4.2 %collective-permute-done.3.from_above = f32[80,8,128]{2,1,0:T(8,128)S(1)} collective-permute-done((f32[80,8,128]{2,1,0:T(8,128)}, f32[80,8,128]{2,1,0:T(8,128)S(1)}, u32[]{:S(2)}, u32[]{:S(2)}) %collective-permute-start.3) | collective-permute-done | bytes 327712 | tf_op jit(solution)/shard_map/ppermute | solution.py:386
  50.3 2.0 shard_map.131
  52.3 6.8 %all-to-all-start.2 = ((f32[8,104,128]{2,1,0:T(8,128)}), f32[8,104,128]{2,1,0:T(8,128)S(1)}, u32[]{:S(2)}, u32[]{:S(2)}) async-start(f32[8,104,128]{2,1,0:T(8,128)} %shard_map.131), calls=%async_computation.2 | async-start | bytes 851968 | tf_op jit(solution)/shard_map/all_to_all | solution.py:408
  59.2 7.9 %all-to-all-done.2.across = f32[8,104,128]{2,1,0:T(8,128)S(1)} async-done(((f32[8,104,128]{2,1,0:T(8,128)}), f32[8,104,128]{2,1,0:T(8,128)S(1)}, u32[]{:S(2)}, u32[]{:S(2)}) %all-to-all-start.2) | async-done | bytes 426016 | tf_op jit(solution)/shard_map/all_to_all | solution.py:408
  70.1 3.0 %collective-permute-start.4 = (f32[5,8,128]{2,1,0:T(8,128)S(1)}, f32[5,8,128]{2,1,0:T(8,128)S(1)}, u32[]{:S(2)}, u32[]{:S(2)}) collective-permute-start(f32[5,8,128]{2,1,0:T(8,128)S(1)} %get-tuple-element.38), channel_id=1, source_target_pairs={{0,64},{64,128},{128,192},{1,65},{65,129},{129,193},{2,66},{66,130... | collective-permute-start | bytes 61448 | tf_op jit(solution)/shard_map/ppermute | solution.py:392
  74.4 3.5 %shard_map.134 = (f32[5,16,16,128]{3,2,1,0:T(8,128)S(1)}, f32[2,16,128]{2,1,0:T(8,128)S(1)}) custom-call(s32[6]{0:T(128)S(1)} %stack.15.ids, f32[5,16,16,128]{3,2,1,0:T(8,128)S(1)} %get-tuple-element.33.field, f32[13,16,16,128]{3,2,1,0:T(8,128)S(1)} %shard_map.132.coef, f32[80,128]{1,0:T(8,128)S(1)} %broadcast_in_dim.7.matrix, ...), custom_call_target="tpu_custom_call" | custom-call | flops 9830400 | bytes 3579904 | tf_op jit(solution)/shard_map/pallas_call | solution.py:33
  78.5 28.8 %all_to_all.45.got = f32[8,48,128]{2,1,0:T(8,128)S(1)} all-to-all(f32[8,48,128]{2,1,0:T(8,128)S(1)} %shard_map.135), channel_id=1, replica_groups=mesh['sec'=4,'row'=8,'rad'=8] {'rad'}, dimensions={0} | all-to-all | bytes 393216 | tf_op jit(solution)/shard_map/all_to_all | solution.py:400
  108.5 13.7 %all_to_all.46.across = f32[8,88,128]{2,1,0:T(8,128)S(1)} all-to-all(f32[8,88,128]{2,1,0:T(8,128)S(1)} %shard_map.136), channel_id=1, replica_groups=mesh['sec'=4,'row'=8,'rad'=8] {'row'}, dimensions={0} | all-to-all | bytes 720896 | tf_op jit(solution)/shard_map/all_to_all | solution.py:408
  123.2 4.6 %collective-permute-start.6 = (f32[5,8,128]{2,1,0:T(8,128)S(1)}, f32[5,8,128]{2,1,0:T(8,128)S(1)}, u32[]{:S(2)}, u32[]{:S(2)}) collective-permute-start(f32[5,8,128]{2,1,0:T(8,128)S(1)} %get-tuple-element.43), channel_id=1, source_target_pairs={{0,64},{64,128},{128,192},{1,65},{65,129},{129,193},{2,66},{66,130... | collective-permute-start | bytes 61448 | tf_op jit(solution)/shard_map/ppermute | solution.py:392
  129.1 3.6 %shard_map.138 = (f32[5,16,16,128]{3,2,1,0:T(8,128)S(1)}, f32[2,16,128]{2,1,0:T(8,128)S(1)}) custom-call(s32[6]{0:T(128)S(1)} %stack.15.ids, f32[5,16,16,128]{3,2,1,0:T(8,128)S(1)} %get-tuple-element.37.field, f32[13,16,16,128]{3,2,1,0:T(8,128)S(1)} %shard_map.132.coef, f32[80,128]{1,0:T(8,128)S(1)} %broadcast_in_dim.7.matrix, ...), custom_call_target="tpu_custom_call" | custom-call | flops 9830400 | bytes 3514368 | tf_op jit(solution)/shard_map/pallas_call | solution.py:33
  133.2 12.1 %all_to_all.47.got = f32[8,48,128]{2,1,0:T(8,128)S(1)} all-to-all(f32[8,48,128]{2,1,0:T(8,128)S(1)} %shard_map.139), channel_id=1, replica_groups=mesh['sec'=4,'row'=8,'rad'=8] {'rad'}, dimensions={0} | all-to-all | bytes 393216 | tf_op jit(solution)/shard_map/all_to_all | solution.py:400
  146.4 12.8 %all_to_all.48.across = f32[8,80,128]{2,1,0:T(8,128)S(1)} all-to-all(f32[8,80,128]{2,1,0:T(8,128)S(1)} %shard_map.140), channel_id=1, replica_groups=mesh['sec'=4,'row'=8,'rad'=8] {'row'}, dimensions={0} | all-to-all | bytes 655360 | tf_op jit(solution)/shard_map/all_to_all | solution.py:408
  160.1 4.8 %collective-permute-start.8 = (f32[5,8,128]{2,1,0:T(8,128)S(1)}, f32[5,8,128]{2,1,0:T(8,128)S(1)}, u32[]{:S(2)}, u32[]{:S(2)}) collective-permute-start(f32[5,8,128]{2,1,0:T(8,128)S(1)} %get-tuple-element.48), channel_id=1, source_target_pairs={{0,64},{64,128},{128,192},{1,65},{65,129},{129,193},{2,66},{66,130... | collective-permute-start | bytes 61448 | tf_op jit(solution)/shard_map/ppermute | solution.py:392
  166.2 3.5 %shard_map.142 = (f32[5,16,16,128]{3,2,1,0:T(8,128)S(1)}, f32[2,16,128]{2,1,0:T(8,128)S(1)}) custom-call(s32[6]{0:T(128)S(1)} %stack.15.ids, f32[5,16,16,128]{3,2,1,0:T(8,128)S(1)} %get-tuple-element.42.field, f32[13,16,16,128]{3,2,1,0:T(8,128)S(1)} %shard_map.132.coef, f32[80,128]{1,0:T(8,128)S(1)} %broadcast_in_dim.7.matrix, ...), custom_call_target="tpu_custom_call" | custom-call | flops 9830400 | bytes 3481600 | tf_op jit(solution)/shard_map/pallas_call | solution.py:33
  170.3 12.1 %all_to_all.49.got = f32[8,48,128]{2,1,0:T(8,128)S(1)} all-to-all(f32[8,48,128]{2,1,0:T(8,128)S(1)} %shard_map.143), channel_id=1, replica_groups=mesh['sec'=4,'row'=8,'rad'=8] {'rad'}, dimensions={0} | all-to-all | bytes 393216 | tf_op jit(solution)/shard_map/all_to_all | solution.py:400
  183.4 11.8 %all_to_all.50.across = f32[8,64,128]{2,1,0:T(8,128)S(1)} all-to-all(f32[8,64,128]{2,1,0:T(8,128)S(1)} %shard_map.144), channel_id=1, replica_groups=mesh['sec'=4,'row'=8,'rad'=8] {'row'}, dimensions={0} | all-to-all | bytes 524288 | tf_op jit(solution)/shard_map/all_to_all | solution.py:408
  195.3 3.3 %shard_map.145 = f32[5,16,8,128]{3,2,1,0:T(8,128)} custom-call(s32[6]{0:T(128)S(1)} %stack.15.ids, s32[8,32]{1,0:T(8,128)S(1)} %slice_convert_fusion.wanted, f32[5]{0:T(128)S(1)} %copy-done.10, f32[5]{0:T(128)S(1)} %copy-done.11, f32[5,16,16,128]{3,2,1,0:T(8,128)S(1)} %get-tuple-element.47.field, f32[13,16,16,128]{3,2,1,0:T(8,128)S(1)} %shard_map.132.coef, ...), custom_call_target="tpu_custom_call" | custom-call | flops 9830400 | bytes 2990080 | tf_op jit(solution)/shard_map/pallas_call | solution.py:33
  (62 shorter events, 26.3 us)
Async XLA Ops:
  0.0 44.3 %copy-start = (f32[5,1,16,8,128]{4,3,2,1,0:T(8,128)S(1)}, f32[5,1,16,8,128]{4,3,2,1,0:T(8,128)}, u32[]{:S(2)}) copy-start(f32[5,1,16,8,128]{4,3,2,1,0:T(8,128)} %param.13) | copy-start | bytes 983044
  1.4 16.3 %all-to-all-start = ((f32[8,8,128]{2,1,0:T(8,128)}), f32[8,8,128]{2,1,0:T(8,128)S(1)}, u32[]{:S(2)}, u32[]{:S(2)}) async-start(f32[8,8,128]{2,1,0:T(8,128)} %broadcast_in_dim.6), calls=%async_computation | async-start | bytes 65536 | tf_op jit(solution)/shard_map/all_to_all | solution.py:387
  9.9 7.8 %collective-permute-start = (f32[5,8,128]{2,1,0:T(8,128)}, f32[5,8,128]{2,1,0:T(8,128)S(1)}, u32[]{:S(2)}, u32[]{:S(2)}) collective-permute-start(f32[5,8,128]{2,1,0:T(8,128)} %get-tuple-element.28), channel_id=1, source_target_pairs={{0,64},{64,128},{128,192},{1,65},{65,129},{129,193},{2,66},{66,130... | collective-permute-start | bytes 61448 | tf_op jit(solution)/shard_map/ppermute | solution.py:392
  13.0 4.7 %collective-permute-start.1 = (f32[8,128]{1,0:T(8,128)}, f32[8,128]{1,0:T(8,128)S(1)}, u32[]{:S(2)}, u32[]{:S(2)}) collective-permute-start(f32[8,128]{1,0:T(8,128)} %get-tuple-element.29), channel_id=1, source_target_pairs={{64,0},{128,64},{192,128},{65,1},{129,65},{193,129},{66,2},{130,66... | collective-permute-start | bytes 12296 | tf_op jit(solution)/shard_map/ppermute | solution.py:393
  20.4 38.7 %copy-start.12 = (f32[1,3,5,5]{3,0,2,1:T(1,128)S(1)}, f32[1,3,5,5]{3,0,2,1:T(1,128)}, u32[]{:S(2)}) copy-start(f32[1,3,5,5]{3,0,2,1:T(1,128)} %param.19) | copy-start | bytes 904
  20.4 29.2 %all-to-all-start.1 = ((f32[8,56,128]{2,1,0:T(8,128)}), f32[8,56,128]{2,1,0:T(8,128)S(1)}, u32[]{:S(2)}, u32[]{:S(2)}) async-start(f32[8,56,128]{2,1,0:T(8,128)} %shard_map.128), calls=%async_computation.1 | async-start | bytes 458752 | tf_op jit(solution)/shard_map/all_to_all | solution.py:400
  30.1 10.0 %collective-permute-start.2 = (f32[80,8,128]{2,1,0:T(8,128)}, f32[80,8,128]{2,1,0:T(8,128)S(1)}, u32[]{:S(2)}, u32[]{:S(2)}) collective-permute-start(f32[80,8,128]{2,1,0:T(8,128)} %get-tuple-element.31), channel_id=1, source_target_pairs={{0,1},{1,2},{2,3},{3,4},{4,5},{5,6},{6,7},{8,9},{9,10},{10,11},{11... | collective-permute-start | bytes 983048 | tf_op jit(solution)/shard_map/ppermute | solution.py:385
  33.5 10.8 %collective-permute-start.3 = (f32[80,8,128]{2,1,0:T(8,128)}, f32[80,8,128]{2,1,0:T(8,128)S(1)}, u32[]{:S(2)}, u32[]{:S(2)}) collective-permute-start(f32[80,8,128]{2,1,0:T(8,128)} %get-tuple-element.32), channel_id=1, source_target_pairs={{1,0},{2,1},{3,2},{4,3},{5,4},{6,5},{7,6},{9,8},{10,9},{11,10},{12... | collective-permute-start | bytes 983048 | tf_op jit(solution)/shard_map/ppermute | solution.py:386
  44.3 0.8 copy-start.3
  45.2 0.8 copy-start.4
  46.0 0.8 copy-start.5
  46.8 0.8 copy-start.6
  47.7 0.8 copy-start.7
  52.3 16.9 %copy-start.10 = (f32[5]{0:T(128)S(1)}, f32[5]{0:T(128)}, u32[]{:S(2)}) copy-start(f32[5]{0:T(128)} %weight.9) | copy-start | bytes 64
  52.3 16.9 %copy-start.11 = (f32[5]{0:T(128)S(1)}, f32[5]{0:T(128)}, u32[]{:S(2)}) copy-start(f32[5]{0:T(128)} %coupling.7) | copy-start | bytes 64
  52.3 14.8 %all-to-all-start.2 = ((f32[8,104,128]{2,1,0:T(8,128)}), f32[8,104,128]{2,1,0:T(8,128)S(1)}, u32[]{:S(2)}, u32[]{:S(2)}) async-start(f32[8,104,128]{2,1,0:T(8,128)} %shard_map.131), calls=%async_computation.2 | async-start | bytes 851968 | tf_op jit(solution)/shard_map/all_to_all | solution.py:408
  70.1 7.9 %copy-start.2 = (f32[5,8,128]{2,1,0:T(8,128)S(1)}, f32[5,8,128]{2,1,0:T(8,128)}, u32[]{:S(2)}) copy-start(f32[5,8,128]{2,1,0:T(8,128)} %inflow.7) | copy-start | bytes 61444
  70.1 7.9 %copy-start.9 = (f32[8,128]{1,0:T(8,128)S(1)}, f32[8,128]{1,0:T(8,128)}, u32[]{:S(2)}) copy-start(f32[8,128]{1,0:T(8,128)} %get-tuple-element.30.out_pressure) | copy-start | bytes 12292
  70.1 7.8 %collective-permute-start.4 = (f32[5,8,128]{2,1,0:T(8,128)S(1)}, f32[5,8,128]{2,1,0:T(8,128)S(1)}, u32[]{:S(2)}, u32[]{:S(2)}) collective-permute-start(f32[5,8,128]{2,1,0:T(8,128)S(1)} %get-tuple-element.38), channel_id=1, source_target_pairs={{0,64},{64,128},{128,192},{1,65},{65,129},{129,193},{2,66},{66,130... | collective-permute-start | bytes 61448 | tf_op jit(solution)/shard_map/ppermute | solution.py:392
  73.1 4.9 %collective-permute-start.5 = (f32[8,128]{1,0:T(8,128)S(1)}, f32[8,128]{1,0:T(8,128)S(1)}, u32[]{:S(2)}, u32[]{:S(2)}) collective-permute-start(f32[8,128]{1,0:T(8,128)S(1)} %get-tuple-element.39), channel_id=1, source_target_pairs={{64,0},{128,64},{192,128},{65,1},{129,65},{193,129},{66,2},{130,66... | collective-permute-start | bytes 12296 | tf_op jit(solution)/shard_map/ppermute | solution.py:393
  123.2 9.5 %collective-permute-start.6 = (f32[5,8,128]{2,1,0:T(8,128)S(1)}, f32[5,8,128]{2,1,0:T(8,128)S(1)}, u32[]{:S(2)}, u32[]{:S(2)}) collective-permute-start(f32[5,8,128]{2,1,0:T(8,128)S(1)} %get-tuple-element.43), channel_id=1, source_target_pairs={{0,64},{64,128},{128,192},{1,65},{65,129},{129,193},{2,66},{66,130... | collective-permute-start | bytes 61448 | tf_op jit(solution)/shard_map/ppermute | solution.py:392
  127.8 4.9 %collective-permute-start.7 = (f32[8,128]{1,0:T(8,128)S(1)}, f32[8,128]{1,0:T(8,128)S(1)}, u32[]{:S(2)}, u32[]{:S(2)}) collective-permute-start(f32[8,128]{1,0:T(8,128)S(1)} %get-tuple-element.44), channel_id=1, source_target_pairs={{64,0},{128,64},{192,128},{65,1},{129,65},{193,129},{66,2},{130,66... | collective-permute-start | bytes 12296 | tf_op jit(solution)/shard_map/ppermute | solution.py:393
  160.1 9.7 %collective-permute-start.8 = (f32[5,8,128]{2,1,0:T(8,128)S(1)}, f32[5,8,128]{2,1,0:T(8,128)S(1)}, u32[]{:S(2)}, u32[]{:S(2)}) collective-permute-start(f32[5,8,128]{2,1,0:T(8,128)S(1)} %get-tuple-element.48), channel_id=1, source_target_pairs={{0,64},{64,128},{128,192},{1,65},{65,129},{129,193},{2,66},{66,130... | collective-permute-start | bytes 61448 | tf_op jit(solution)/shard_map/ppermute | solution.py:392
  164.9 4.8 %collective-permute-start.9 = (f32[8,128]{1,0:T(8,128)S(1)}, f32[8,128]{1,0:T(8,128)S(1)}, u32[]{:S(2)}, u32[]{:S(2)}) collective-permute-start(f32[8,128]{1,0:T(8,128)S(1)} %get-tuple-element.49), channel_id=1, source_target_pairs={{64,0},{128,64},{192,128},{65,1},{129,65},{193,129},{66,2},{130,66... | collective-permute-start | bytes 12296 | tf_op jit(solution)/shard_map/ppermute | solution.py:393
  (2 other events, 1.4 us)

commit v5 on v4

--- a/solution.py
+++ b/solution.py
@@ -12,6 +12,7 @@
 time_step = 0.08
 INTERPRET = False
 VMEM_LIMIT = 8 * 1024 * 1024
+FAR_LIMIT = 60 * 1024 * 1024
 
 NV = 5
 WIDE = 4
@@ -28,18 +29,25 @@
     return pl.BlockSpec(memory_space=pltpu.SMEM)
 
 
-def call(kernel, outs, scalars, arrays, flops=0, scratch=(), limit=VMEM_LIMIT):
+def hbm():
+    return pl.BlockSpec(memory_space=pltpu.HBM)
+
+
+def call(kernel, outs, scalars, arrays, flops=0, scratch=(), far=()):
     moved = sum(a.size * 4 for a in arrays) + sum(4 * functools.reduce(lambda x, y: x * y, o) for o in outs)
+    scratch = list(scratch)
+    if far:
+        scratch += [pltpu.VMEM(a.shape, jnp.float32) for a in far] + [pltpu.SemaphoreType.DMA((len(far),))]
     return pl.pallas_call(
         kernel,
         out_shape=[jax.ShapeDtypeStruct(o, jnp.float32) for o in outs],
-        in_specs=[smem() for _ in scalars] + [vmem() for _ in arrays],
+        in_specs=[smem() for _ in scalars] + [vmem() for _ in arrays] + [hbm() for _ in far],
         out_specs=[vmem() for _ in outs],
-        scratch_shapes=list(scratch),
-        compiler_params=pltpu.CompilerParams(vmem_limit_bytes=limit),
+        scratch_shapes=scratch,
+        compiler_params=pltpu.CompilerParams(vmem_limit_bytes=FAR_LIMIT if far else VMEM_LIMIT),
         cost_estimate=pl.CostEstimate(flops=flops, bytes_accessed=moved, transcendentals=0),
         interpret=INTERPRET,
-    )(*scalars, *arrays)
+    )(*scalars, *arrays, *far)
 
 
 def lanes_of(shape):
@@ -70,7 +78,56 @@
     return range(step + 1, step + 1 + count), -(-6 * count // 8) * 8
 
 
-def first_kernel(weight, state, volume, axial, radial, circ, mu, outflow, to_above, to_below, down, up, out_pressure):
+def fetch(sources, targets, sems):
+    copies = [pltpu.make_async_copy(a, b, sems.at[i]) for i, (a, b) in enumerate(zip(sources, targets))]
+    for copy in copies:
+        copy.start()
+    for copy in copies:
+        copy.wait()
+
+
+def first_kernel(ids, weight, down_donors, up_donors, state_hbm, circ_hbm, mu_hbm, outflow_hbm, down, up, out_pressure, send, state, circ, mu, outflow, sems):
+    fetch((state_hbm, circ_hbm, mu_hbm, outflow_hbm), (state, circ, mu, outflow), sems)
+    lanes = lanes_of((8, 128))
+    row, size = ids[1], send.shape[0]
+    for v in range(NV):
+        down[v] = state[v, PLANES - 1]
+    up[...] = pressure(weight, [state[v, 0] for v in range(NV)])
+    out_pressure[...] = pressure(weight, [outflow[v] for v in range(NV)])
+    listed = jnp.zeros((8, 128), jnp.int32)
+    for a in range(8):
+        listed = jnp.where(lanes == a, down_donors[a], listed)
+        listed = jnp.where(lanes == 8 + a, up_donors[a], listed)
+    listed = listed.astype(jnp.float32)
+    for j in range(size):
+        send[j, 0:8, :] = listed
+
+    def one(k, carry):
+        last, first = carry
+        for v in range(NV):
+            cell = state[v, k]
+            at = v * 16 + k
+            here = lanes == at
+            last = jnp.where(here, roll(cell, at + 1, 1), last)
+            first = jnp.where(here, roll(cell, at, 1), first)
+        here = lanes == 80 + k
+        last = jnp.where(here, roll(mu[k], 81 + k, 1), last)
+        first = jnp.where(here, roll(mu[k], 80 + k, 1), first)
+        last = jnp.where(lanes == 96 + k, roll(circ[k], 97 + k, 1), last)
+        return last, first
+
+    zero = jnp.zeros((8, 128), jnp.float32)
+    last, first = lax.fori_loop(0, PLANES, one, (zero, zero))
+    send[lax.rem(row + 1, size), 8:16, :] = last
+    send[lax.rem(row + size - 1, size), 8:16, :] = first
+
+
+def pack_kernel(ids, table, *refs):
+    sources, (to_above, to_below, field, raw), targets, sems = refs[:6], refs[6:10], refs[10:16], refs[16]
+    fetch(sources, targets, sems)
+    state, arrays = targets[0], targets[1:]
+    row, size = ids[1], table.shape[0]
+
     def put(at, half, cell):
         to_above[at, half : half + 4, :] = cell[4:8]
         to_below[at, half : half + 4, :] = cell[0:4]
@@ -79,16 +136,18 @@
         for half in (0, 1):
             plane = 2 * k + half
             for v in range(NV):
-                put(v * 8 + k, 4 * half, state[v, plane])
-            for at, array in enumerate((volume, axial, radial, circ, mu)):
-                put((NV + at) * 8 + k, 4 * half, array[plane])
+                cell = state[v, plane]
+                put(v * 8 + k, 4 * half, cell)
+                field[v, plane, 4:12, :] = cell
+            for at, array in enumerate(arrays):
+                cell = array[plane]
+                put((NV + at) * 8 + k, 4 * half, cell)
+                raw[at, plane, 4:12, :] = cell
         return carry
 
-    for v in range(NV):
-        down[v] = state[v, PLANES - 1]
-    up[...] = pressure(weight, [state[v, 0] for v in range(NV)])
-    out_pressure[...] = pressure(weight, [outflow[v] for v in range(NV)])
     lax.fori_loop(0, PLANES // 2, one, 0)
+    put(2 * NV * 8, 0, table[lax.rem(row + size - 1, size), 8:16, :])
+    put(2 * NV * 8, 4, table[lax.rem(row + 1, size), 8:16, :])
 
 
 def gather_kernel(first_step, ids, down, up, inflow, out_pressure, *refs):
@@ -118,42 +177,31 @@
     lists[...] = jnp.where(lanes < 16, down, up)
 
 
-def extend_kernel(state, volume, axial, radial, circ, mu, from_below, from_above, field, raw, edges):
-    lanes = lanes_of((ROWS, 128))
+def extend_kernel(ids, field_in, raw_in, table, from_below, from_above, field, raw, around):
+    row, size = ids[1], table.shape[0]
 
     def one(k, carry):
-        last, first = carry
         for half in (0, 1):
             plane = 2 * k + half
             rows = slice(4 * half, 4 * half + 4)
-
-            def put(at, target, index, cell):
-                target[index, plane, 0:4, :] = from_below[at, rows, :]
-                target[index, plane, 4:12, :] = cell
-                target[index, plane, 12:16, :] = from_above[at, rows, :]
-                return target[index, plane]
-
-            for v in range(NV):
-                cell = put(v * 8 + k, field, v, state[v, plane])
-                at = v * 16 + plane
-                last = jnp.where(lanes == at, roll(cell, at + 1, 1), last)
-                first = jnp.where(lanes == at, roll(cell, at, 1), first)
-            for at, array in enumerate((volume, axial, radial, circ, mu)):
-                cell = put((NV + at) * 8 + k, raw, at, array[plane])
-                if at == 3:
-                    last = jnp.where(lanes == 96 + plane, roll(cell, 97 + plane, 1), last)
-                if at == 4:
-                    last = jnp.where(lanes == 80 + plane, roll(cell, 81 + plane, 1), last)
-                    first = jnp.where(lanes == 80 + plane, roll(cell, 80 + plane, 1), first)
-        return last, first
-
-    zero = jnp.zeros((ROWS, 128), jnp.float32)
-    last, first = lax.fori_loop(0, PLANES // 2, one, (zero, zero))
-    edges[0] = last
-    edges[1] = first
-
-
-def select_kernel(step, ids, wanted, got, edges, send):
+            for target, base in ((field, 0), (raw, NV)):
+                for v in range(NV):
+                    at = (base + v) * 8 + k
+                    target[v, plane, 0:4, :] = from_below[at, rows, :]
+                    target[v, plane, 12:16, :] = from_above[at, rows, :]
+                    target[v, plane, 4:12, :] = (field_in, raw_in)[base // NV][v, plane, 4:12, :]
+        return carry
+
+    lax.fori_loop(0, PLANES // 2, one, 0)
+    for side, source in enumerate((lax.rem(row + size - 1, size), lax.rem(row + 1, size))):
+        rows = slice(4 * side, 4 * side + 4)
+        around[side, 0:4, :] = from_below[2 * NV * 8, rows, :]
+        around[side, 4:12, :] = table[source, 8:16, :]
+        around[side, 12:16, :] = from_above[2 * NV * 8, rows, :]
+
+
+def select_kernel(step, ids, wanted, got, *refs):
+    send = refs[-1]
     size = send.shape[0]
     row = ids[1]
     rows, base = picked(step)
@@ -170,18 +218,23 @@
         return carry
 
     lax.fori_loop(0, size, one, 0)
-    send[lax.rem(row + 1, size), base : base + ROWS, :] = edges[0]
-    send[lax.rem(row + size - 1, size), base : base + ROWS, :] = edges[1]
-
-
-def sides(ids, across, base):
+    if step:
+        edges = refs[0]
+        send[lax.rem(row + 1, size), base : base + ROWS, :] = edges[0]
+        send[lax.rem(row + size - 1, size), base : base + ROWS, :] = edges[1]
+
+
+def sides(step, ids, around):
+    if step == 0:
+        return around[0], around[1]
+    base = picked(step)[1]
     row, row_size = ids[1], ids[5]
-    left = across[lax.rem(row + row_size - 1, row_size), base : base + ROWS, :]
-    right = across[lax.rem(row + 1, row_size), base : base + ROWS, :]
+    left = around[lax.rem(row + row_size - 1, row_size), base : base + ROWS, :]
+    right = around[lax.rem(row + 1, row_size), base : base + ROWS, :]
     return left, right
 
 
-def coef_kernel(ids, raw, across, coef):
+def coef_kernel(ids, raw, around_ref, coef):
     rad, rad_size = ids[2], ids[3]
     lanes = lanes_of((ROWS, 128))
     rows = rows_of((ROWS, 128))
@@ -189,7 +242,7 @@
         jnp.logical_and(rad == 0, rows < WIDE), jnp.logical_and(rad == rad_size - 1, rows >= WIDE + 8)
     )
     casing = jnp.logical_and(rad == rad_size - 1, rows >= WIDE + 7)
-    left, right = sides(ids, across, picked(0)[1])
+    left, right = sides(0, ids, around_ref)
 
     def one(k, carry):
         m = raw[4, k]
@@ -267,9 +320,9 @@
     return [ghost[v] for v in range(NV)], [outlet[v] + coupling[v] * jump for v in range(NV)]
 
 
-def ends_of(step, ids, wanted, weight, coupling, field, coef, matrix, across, ghost):
+def ends_of(step, ids, wanted, weight, coupling, field, coef, matrix, across, around, ghost):
     lanes = lanes_of((ROWS, 128))
-    left, right = sides(ids, across, picked(step)[1])
+    left, right = sides(step, ids, around)
     inlet_ghost, outlet_ghost = ghosts_of(step, ids, wanted, weight, coupling, field, across, ghost)
     plane = lambda k: [field[v, k] for v in range(NV)]
     new_inlet = advance(0, inlet_ghost, plane(0), plane(1), coef, matrix, left, right, lanes)
@@ -278,8 +331,8 @@
     return new_inlet, new_outlet
 
 
-def ends_kernel(step, ids, wanted, weight, coupling, field, coef, matrix, across, ends, down, up, ghost):
-    new_inlet, new_outlet = ends_of(step, ids, wanted, weight, coupling, field, coef, matrix, across, ghost)
+def ends_kernel(step, ids, wanted, weight, coupling, field, coef, matrix, across, around, ends, down, up, ghost):
+    new_inlet, new_outlet = ends_of(step, ids, wanted, weight, coupling, field, coef, matrix, across, around, ghost)
     for v in range(NV):
         ends[0, v] = new_inlet[v]
         ends[1, v] = new_outlet[v]
@@ -287,9 +340,9 @@
     up[...] = pressure(weight, new_inlet)[WIDE : WIDE + 8]
 
 
-def bulk_kernel(step, ids, field, coef, matrix, across, ends, new, edges):
+def bulk_kernel(step, ids, field, coef, matrix, around, ends, new, edges):
     lanes = lanes_of((ROWS, 128))
-    left, right = sides(ids, across, picked(step)[1])
+    left, right = sides(step, ids, around)
 
     def note(k, total, last, first):
         for v in range(NV):
@@ -316,10 +369,10 @@
     edges[1] = first
 
 
-def last_kernel(step, ids, wanted, weight, coupling, field, coef, matrix, across, new, ghost):
+def last_kernel(step, ids, wanted, weight, coupling, field, coef, matrix, across, around, new, ghost):
     lanes = lanes_of((ROWS, 128))
-    left, right = sides(ids, across, picked(step)[1])
-    new_inlet, new_outlet = ends_of(step, ids, wanted, weight, coupling, field, coef, matrix, across, ghost)
+    left, right = sides(step, ids, around)
+    new_inlet, new_outlet = ends_of(step, ids, wanted, weight, coupling, field, coef, matrix, across, around, ghost)
     for v in range(NV):
         new[v, 0] = new_inlet[v][WIDE : WIDE + 8]
         new[v, PLANES - 1] = new_outlet[v][WIDE : WIDE + 8]
@@ -363,29 +416,28 @@
         ]
     ).astype(jnp.int32)
     own = [state[:, 0], volume[0], face_axial[0], face_radial[0], face_circum[0], viscosity[0]]
-    donors = jnp.concatenate([down_donors[0], up_donors[0]]).astype(jnp.float32)
-    donors = jnp.broadcast_to(jnp.pad(donors, (0, 112))[None, None], (row_size, 8, 128))
     matrix = jnp.broadcast_to(jnp.pad(flux_matrix[0].reshape(75), (0, 5))[:, None], (80, 128))
     extended = (NV, PLANES, ROWS, 128)
     strips = (2, ROWS, 128)
-    sent = (2 * NV * PLANES // 2, 8, 128)
+    sent = (2 * NV * PLANES // 2 + 1, 8, 128)
     scalars = [pressure_weight, boundary_coupling]
 
-    to_above, to_below, down, up, out_pressure = call(
+    down, up, out_pressure, lists = call(
         first_kernel,
-        [sent, sent, (NV, 8, 128), (8, 128), (8, 128)],
-        [pressure_weight],
-        own + [outflow_plane],
-        limit=60 * 1024 * 1024,
+        [(NV, 8, 128), (8, 128), (8, 128), (row_size, 16, 128)],
+        [ids, pressure_weight, down_donors[0], up_donors[0]],
+        [],
+        far=[own[0], own[4], own[5], outflow_plane],
     )
     forward = [(i, i + 1) for i in range(sections - 1)]
     backward = [(i + 1, i) for i in range(sections - 1)]
     outward = [(i, i + 1) for i in range(rad_size - 1)]
     inward = [(i + 1, i) for i in range(rad_size - 1)]
+    table = lax.all_to_all(lists, "row", 0, 0)
+    to_above, to_below, field, raw = call(pack_kernel, [sent, sent, extended, extended], [ids], [table], far=own)
     from_below = lax.ppermute(to_above, "rad", outward)
     from_above = lax.ppermute(to_below, "rad", inward)
-    table = lax.all_to_all(donors, "row", 0, 0)
-    field = coef = edges = wanted = None
+    coef = edges = wanted = None
     for step in range(STEPS):
         last_step = step == STEPS - 1
         _, base = picked(step)
@@ -401,20 +453,26 @@
         if step == 0:
             (lists,) = call(wanted_kernel, [(8, 128)], [ids], [got])
             wanted = lists[:, :32].astype(jnp.int32)
-            field, raw, edges = call(extend_kernel, [extended, extended, strips], [], own + [from_below, from_above])
+            field, raw, around = call(
+                extend_kernel, [extended, extended, strips], [ids], [field, raw, table, from_below, from_above]
+            )
+            (coef,) = call(coef_kernel, [(13, PLANES, ROWS, 128)], [ids], [raw, around])
         (send,) = call(
-            functools.partial(select_kernel, step), [(row_size, base + ROWS, 128)], [ids, wanted], [got, edges]
+            functools.partial(select_kernel, step),
+            [(row_size, base + (ROWS if step else 0), 128)],
+            [ids, wanted],
+            [got, edges] if step else [got],
         )
         across = lax.all_to_all(send, "row", 0, 0)
-        if step == 0:
-            (coef,) = call(coef_kernel, [(13, PLANES, ROWS, 128)], [ids], [raw, across])
+        if step:
+            around = across
         ghost = [pltpu.VMEM((NV + 1, ROWS, 128), jnp.float32)]
         if last_step:
             (field,) = call(
                 functools.partial(last_kernel, step),
                 [(NV, PLANES, 8, 128)],
                 [ids, wanted] + scalars,
-                [field, coef, matrix, across],
+                [field, coef, matrix, across, around],
                 flops=PLANES * ROWS * 128 * 300,
                 scratch=ghost,
             )
@@ -423,7 +481,7 @@
                 functools.partial(ends_kernel, step),
                 [(2, NV, ROWS, 128), (NV, 8, 128), (8, 128)],
                 [ids, wanted] + scalars,
-                [field, coef, matrix, across],
+                [field, coef, matrix, across, around],
                 flops=2 * ROWS * 128 * 300,
                 scratch=ghost,
             )
@@ -431,7 +489,7 @@
                 functools.partial(bulk_kernel, step),
                 [extended, strips],
                 [ids],
-                [field, coef, matrix, across, ends],
+                [field, coef, matrix, around, ends],
                 flops=PLANES * ROWS * 128 * 300,
             )
     return field[:, None]

time: 200 us -> 187 us (0.935)
  waiting for transfers between devices: 20.8 us -> 8.84 us
  Pallas kernels: 30.5 us -> 35.3 us
  blocking collectives: 91.4 us -> 87.6 us
  local copies, waits for them, and re-layouts: 6.5 us -> 3.76 us
    ppermute x1, waiting for transfers between devices: 5.31 us -> 0.01 us  [body(): from_below = lax.ppermute(to_above, 'rad', outward)]
    all_to_all x3, blocking collectives: 53.1 us -> 48.3 us  [body(): got = lax.all_to_all(send, 'rad', 0, 0)]
    pallas_call x19 -> x20, Pallas kernels: 30.5 us -> 35.3 us  [call(): pl.pallas_call(kernel, out_shape=[jax.ShapeDtypeStruct(o, jnp.float32) fo...]
    all_to_all x1, waiting for transfers between devices: 7.88 us -> 3.67 us  [body(): across = lax.all_to_all(send, 'row', 0, 0)]
    ppermute x1, waiting for transfers between devices: 4.2 us -> 0.01 us  [body(): from_above = lax.ppermute(to_below, 'rad', inward)]
    unnamed x26, local copies, waits for them, and re-layouts: 5.63 us -> 2.93 us
  transfers between devices with their start and end apart: 13 -> 13, of which waited for: 4 -> 3; matrix products, arithmetic and copies ran while one was open for 0% -> 0% of each run, Pallas kernels for 7% -> 10%
where the time goes in v5:
time: 187 us; the launch traced here: 186 us
  blocking collectives  87.6 us (47%)
  starting transfers between devices  49.8 us (27%)
  Pallas kernels  35.3 us (19%)
  waiting for transfers between devices  8.84 us (5%)
  local copies, waits for them, and re-layouts  3.76 us (2%)
    all_to_all x3, blocking collectives, body(): got = lax.all_to_all(send, 'rad', 0, 0)  48.3 us
    all_to_all x3, blocking collectives, body(): across = lax.all_to_all(send, 'row', 0, 0)  39.4 us
    pallas_call x20, Pallas kernels, call(): pl.pallas_call(kernel, out_shape=[jax.ShapeDtypeStruct(o, jnp.float32) fo...  35.3 us
    ppermute x4, starting transfers between devices, body(): down = lax.ppermute(down, 'sec', forward)  16.1 us
    all_to_all x1, starting transfers between devices, body(): got = lax.all_to_all(send, 'rad', 0, 0)  9.56 us
    all_to_all x1, starting transfers between devices, body(): across = lax.all_to_all(send, 'row', 0, 0)  7.67 us
    all_to_all x1, starting transfers between devices, body(): table = lax.all_to_all(lists, 'row', 0, 0)  6.47 us
    ppermute x4, starting transfers between devices, body(): up = lax.ppermute(up, 'sec', backward)  5.17 us
  transfers between devices with their start and end apart: 13, of which 3 were waited for; matrix products, arithmetic and copies ran while one was open for 0% of the time, Pallas kernels for 10%

profile of v5, /device:TPU:1, one launch (start us, length us, event | category | flops | bytes accessed | tf_op | source)
XLA Modules:
  0.0 185.7 jit_solution(7910696314621609834)
XLA Ops:
  0.7 3.8 %shard_map.127 = (f32[5,8,128]{2,1,0:T(8,128)}, f32[8,128]{1,0:T(8,128)}, f32[8,128]{1,0:T(8,128)}, f32[8,16,128]{2,1,0:T(8,128)}) custom-call(s32[6]{0:T(128)} %stack.15.ids, f32[5]{0:T(128)} %weight.9, s32[8]{0:T(128)} %bitcast.23, s32[8]{0:T(128)} %bitcast.24, f32[5,16,8,128]{3,2,1,0:T(8,128)} %bitcast.14, f32[16,8,128]{2,1,0:T(8,128)} %bitcast.16, ...), custom_call_target="tpu_custom_call" | custom-call | bytes 94208 | tf_op jit(solution)/shard_map/pallas_call | solution.py:41
  4.5 6.5 %all-to-all-start = ((f32[8,16,128]{2,1,0:T(8,128)}), f32[8,16,128]{2,1,0:T(8,128)S(1)}, u32[]{:S(2)}, u32[]{:S(2)}) async-start(f32[8,16,128]{2,1,0:T(8,128)} %get-tuple-element.34), calls=%async_computation | async-start | bytes 131072 | tf_op jit(solution)/shard_map/all_to_all | solution.py:436
  11.0 3.0 %collective-permute-start = (f32[5,8,128]{2,1,0:T(8,128)}, f32[5,8,128]{2,1,0:T(8,128)S(1)}, u32[]{:S(2)}, u32[]{:S(2)}) collective-permute-start(f32[5,8,128]{2,1,0:T(8,128)} %get-tuple-element.31), channel_id=1, source_target_pairs={{0,64},{64,128},{128,192},{1,65},{65,129},{129,193},{2,66},{66,130... | collective-permute-start | bytes 61448 | tf_op jit(solution)/shard_map/ppermute | solution.py:444
  15.3 3.4 %collective-permute-done.1.up = f32[8,128]{1,0:T(8,128)S(1)} collective-permute-done((f32[8,128]{1,0:T(8,128)}, f32[8,128]{1,0:T(8,128)S(1)}, u32[]{:S(2)}, u32[]{:S(2)}) %collective-permute-start.1) | collective-permute-done | bytes 4128 | tf_op jit(solution)/shard_map/ppermute | solution.py:445
  22.1 9.6 %all-to-all-start.1 = ((f32[8,56,128]{2,1,0:T(8,128)}), f32[8,56,128]{2,1,0:T(8,128)S(1)}, u32[]{:S(2)}, u32[]{:S(2)}) async-start(f32[8,56,128]{2,1,0:T(8,128)} %shard_map.128), calls=%async_computation.1 | async-start | bytes 458752 | tf_op jit(solution)/shard_map/all_to_all | solution.py:452
  31.7 3.4 %shard_map.130 = (f32[81,8,128]{2,1,0:T(8,128)}, f32[81,8,128]{2,1,0:T(8,128)}, f32[5,16,16,128]{3,2,1,0:T(8,128)}, f32[5,16,16,128]{3,2,1,0:T(8,128)}) custom-call(s32[6]{0:T(128)} %stack.15.ids, f32[8,16,128]{2,1,0:T(8,128)} %copy-done, f32[5,16,8,128]{3,2,1,0:T(8,128)} %bitcast.15, f32[16,8,128]{2,1,0:T(8,128)} %bitcast.20, f32[16,8,128]{2,1,0:T(8,128)} %bitcast.21, ...), custom_call_target="tpu_custom_call" | custom-call | bytes 2039808 | tf_op jit(solution)/shard_map/pallas_call | solution.py:41
  35.1 3.5 %collective-permute-start.2 = (f32[81,8,128]{2,1,0:T(8,128)}, f32[81,8,128]{2,1,0:T(8,128)S(1)}, u32[]{:S(2)}, u32[]{:S(2)}) collective-permute-start(f32[81,8,128]{2,1,0:T(8,128)} %get-tuple-element.37), channel_id=1, source_target_pairs={{0,1},{1,2},{2,3},{3,4},{4,5},{5,6},{6,7},{8,9},{9,10},{10,11},{11... | collective-permute-start | bytes 995336 | tf_op jit(solution)/shard_map/ppermute | solution.py:438
  42.3 2.0 %shard_map.133 = f32[8,88,128]{2,1,0:T(8,128)} custom-call(s32[6]{0:T(128)S(1)} %copy-done.7, s32[8,32]{1,0:T(8,128)S(1)} %slice_convert_fusion.wanted, f32[8,56,128]{2,1,0:T(8,128)S(1)} %all-to-all-done.1.got), custom_call_target="tpu_custom_call" | custom-call | bytes 589824 | tf_op jit(solution)/shard_map/pallas_call | solution.py:41
  44.2 7.7 %all-to-all-start.2 = ((f32[8,88,128]{2,1,0:T(8,128)}), f32[8,88,128]{2,1,0:T(8,128)S(1)}, u32[]{:S(2)}, u32[]{:S(2)}) async-start(f32[8,88,128]{2,1,0:T(8,128)} %shard_map.133), calls=%async_computation.2 | async-start | bytes 720896 | tf_op jit(solution)/shard_map/all_to_all | solution.py:466
  53.6 2.0 %shard_map.132.coef = f32[13,16,16,128]{3,2,1,0:T(8,128)S(1)} custom-call(s32[6]{0:T(128)S(1)} %copy-done.7, f32[5,16,16,128]{3,2,1,0:T(8,128)S(1)} %get-tuple-element.40.raw, f32[2,16,128]{2,1,0:T(8,128)S(1)} %get-tuple-element.41.around_ref.around), custom_call_target="tpu_custom_call" | custom-call | bytes 2375680 | tf_op jit(solution)/shard_map/pallas_call | solution.py:41
  55.6 3.7 %all-to-all-done.2.across = f32[8,88,128]{2,1,0:T(8,128)S(1)} async-done(((f32[8,88,128]{2,1,0:T(8,128)}), f32[8,88,128]{2,1,0:T(8,128)S(1)}, u32[]{:S(2)}, u32[]{:S(2)}) %all-to-all-start.2) | async-done | bytes 360480 | tf_op jit(solution)/shard_map/all_to_all | solution.py:466
  60.3 3.6 %collective-permute-start.4 = (f32[5,8,128]{2,1,0:T(8,128)S(1)}, f32[5,8,128]{2,1,0:T(8,128)S(1)}, u32[]{:S(2)}, u32[]{:S(2)}) collective-permute-start(f32[5,8,128]{2,1,0:T(8,128)S(1)} %get-tuple-element.44), channel_id=1, source_target_pairs={{0,64},{64,128},{128,192},{1,65},{65,129},{129,193},{2,66},{66,130... | collective-permute-start | bytes 61448 | tf_op jit(solution)/shard_map/ppermute | solution.py:444
  65.2 3.6 %shard_map.135 = (f32[5,16,16,128]{3,2,1,0:T(8,128)S(1)}, f32[2,16,128]{2,1,0:T(8,128)S(1)}) custom-call(s32[6]{0:T(128)S(1)} %copy-done.7, f32[5,16,16,128]{3,2,1,0:T(8,128)S(1)} %get-tuple-element.39.field, f32[13,16,16,128]{3,2,1,0:T(8,128)S(1)} %shard_map.132.coef, f32[80,128]{1,0:T(8,128)S(1)} %broadcast_in_dim.4.matrix, ...), custom_call_target="tpu_custom_call" | custom-call | flops 9830400 | bytes 3170304 | tf_op jit(solution)/shard_map/pallas_call | solution.py:41
  69.4 24.0 %all_to_all.45.got = f32[8,48,128]{2,1,0:T(8,128)S(1)} all-to-all(f32[8,48,128]{2,1,0:T(8,128)S(1)} %shard_map.136), channel_id=1, replica_groups=mesh['sec'=4,'row'=8,'rad'=8] {'rad'}, dimensions={0} | all-to-all | bytes 393216 | tf_op jit(solution)/shard_map/all_to_all | solution.py:452
  94.5 14.8 %all_to_all.46.across.around = f32[8,88,128]{2,1,0:T(8,128)S(1)} all-to-all(f32[8,88,128]{2,1,0:T(8,128)S(1)} %shard_map.137), channel_id=1, replica_groups=mesh['sec'=4,'row'=8,'rad'=8] {'row'}, dimensions={0} | all-to-all | bytes 720896 | tf_op jit(solution)/shard_map/all_to_all | solution.py:466
  110.2 4.6 %collective-permute-start.6 = (f32[5,8,128]{2,1,0:T(8,128)S(1)}, f32[5,8,128]{2,1,0:T(8,128)S(1)}, u32[]{:S(2)}, u32[]{:S(2)}) collective-permute-start(f32[5,8,128]{2,1,0:T(8,128)S(1)} %get-tuple-element.49), channel_id=1, source_target_pairs={{0,64},{64,128},{128,192},{1,65},{65,129},{129,193},{2,66},{66,130... | collective-permute-start | bytes 61448 | tf_op jit(solution)/shard_map/ppermute | solution.py:444
  116.2 3.6 %shard_map.139 = (f32[5,16,16,128]{3,2,1,0:T(8,128)S(1)}, f32[2,16,128]{2,1,0:T(8,128)S(1)}) custom-call(s32[6]{0:T(128)S(1)} %copy-done.7, f32[5,16,16,128]{3,2,1,0:T(8,128)S(1)} %get-tuple-element.43.field, f32[13,16,16,128]{3,2,1,0:T(8,128)S(1)} %shard_map.132.coef, f32[80,128]{1,0:T(8,128)S(1)} %broadcast_in_dim.4.matrix, ...), custom_call_target="tpu_custom_call" | custom-call | flops 9830400 | bytes 3514368 | tf_op jit(solution)/shard_map/pallas_call | solution.py:41
  120.3 12.1 %all_to_all.47.got = f32[8,48,128]{2,1,0:T(8,128)S(1)} all-to-all(f32[8,48,128]{2,1,0:T(8,128)S(1)} %shard_map.140), channel_id=1, replica_groups=mesh['sec'=4,'row'=8,'rad'=8] {'rad'}, dimensions={0} | all-to-all | bytes 393216 | tf_op jit(solution)/shard_map/all_to_all | solution.py:452
  133.5 12.7 %all_to_all.48.across.around = f32[8,80,128]{2,1,0:T(8,128)S(1)} all-to-all(f32[8,80,128]{2,1,0:T(8,128)S(1)} %shard_map.141), channel_id=1, replica_groups=mesh['sec'=4,'row'=8,'rad'=8] {'row'}, dimensions={0} | all-to-all | bytes 655360 | tf_op jit(solution)/shard_map/all_to_all | solution.py:466
  147.1 4.9 %collective-permute-start.8 = (f32[5,8,128]{2,1,0:T(8,128)S(1)}, f32[5,8,128]{2,1,0:T(8,128)S(1)}, u32[]{:S(2)}, u32[]{:S(2)}) collective-permute-start(f32[5,8,128]{2,1,0:T(8,128)S(1)} %get-tuple-element.54), channel_id=1, source_target_pairs={{0,64},{64,128},{128,192},{1,65},{65,129},{129,193},{2,66},{66,130... | collective-permute-start | bytes 61448 | tf_op jit(solution)/shard_map/ppermute | solution.py:444
  153.3 3.6 %shard_map.143 = (f32[5,16,16,128]{3,2,1,0:T(8,128)S(1)}, f32[2,16,128]{2,1,0:T(8,128)S(1)}) custom-call(s32[6]{0:T(128)S(1)} %copy-done.7, f32[5,16,16,128]{3,2,1,0:T(8,128)S(1)} %get-tuple-element.48.field, f32[13,16,16,128]{3,2,1,0:T(8,128)S(1)} %shard_map.132.coef, f32[80,128]{1,0:T(8,128)S(1)} %broadcast_in_dim.4.matrix, ...), custom_call_target="tpu_custom_call" | custom-call | flops 9830400 | bytes 3481600 | tf_op jit(solution)/shard_map/pallas_call | solution.py:41
  157.5 12.1 %all_to_all.49.got = f32[8,48,128]{2,1,0:T(8,128)S(1)} all-to-all(f32[8,48,128]{2,1,0:T(8,128)S(1)} %shard_map.144), channel_id=1, replica_groups=mesh['sec'=4,'row'=8,'rad'=8] {'rad'}, dimensions={0} | all-to-all | bytes 393216 | tf_op jit(solution)/shard_map/all_to_all | solution.py:452
  170.6 11.8 %all_to_all.50.across.around = f32[8,64,128]{2,1,0:T(8,128)S(1)} all-to-all(f32[8,64,128]{2,1,0:T(8,128)S(1)} %shard_map.145), channel_id=1, replica_groups=mesh['sec'=4,'row'=8,'rad'=8] {'row'}, dimensions={0} | all-to-all | bytes 524288 | tf_op jit(solution)/shard_map/all_to_all | solution.py:466
  182.4 3.3 %shard_map.146 = f32[5,16,8,128]{3,2,1,0:T(8,128)} custom-call(s32[6]{0:T(128)S(1)} %copy-done.7, s32[8,32]{1,0:T(8,128)S(1)} %slice_convert_fusion.wanted, f32[5]{0:T(128)S(1)} %copy-done.10, f32[5]{0:T(128)S(1)} %copy-done.11, f32[5,16,16,128]{3,2,1,0:T(8,128)S(1)} %get-tuple-element.53.field, f32[13,16,16,128]{3,2,1,0:T(8,128)S(1)} %shard_map.132.coef, ...), custom_call_target="tpu_custom_call" | custom-call | flops 9830400 | bytes 3252224 | tf_op jit(solution)/shard_map/pallas_call | solution.py:41
  (60 shorter events, 22.1 us)
Async XLA Ops:
  0.7 41.0 %copy-start.7 = (s32[6]{0:T(128)S(1)}, s32[6]{0:T(128)}, u32[]{:S(2)}) copy-start(s32[6]{0:T(128)} %stack.15.ids) | copy-start | bytes 76
  4.5 47.4 %copy-start.12 = (f32[1,3,5,5]{3,0,2,1:T(1,128)S(1)}, f32[1,3,5,5]{3,0,2,1:T(1,128)}, u32[]{:S(2)}) copy-start(f32[1,3,5,5]{3,0,2,1:T(1,128)} %param.19) | copy-start | bytes 904
  4.5 14.3 %all-to-all-start = ((f32[8,16,128]{2,1,0:T(8,128)}), f32[8,16,128]{2,1,0:T(8,128)S(1)}, u32[]{:S(2)}, u32[]{:S(2)}) async-start(f32[8,16,128]{2,1,0:T(8,128)} %get-tuple-element.34), calls=%async_computation | async-start | bytes 131072 | tf_op jit(solution)/shard_map/all_to_all | solution.py:436
  11.0 7.8 %collective-permute-start = (f32[5,8,128]{2,1,0:T(8,128)}, f32[5,8,128]{2,1,0:T(8,128)S(1)}, u32[]{:S(2)}, u32[]{:S(2)}) collective-permute-start(f32[5,8,128]{2,1,0:T(8,128)} %get-tuple-element.31), channel_id=1, source_target_pairs={{0,64},{64,128},{128,192},{1,65},{65,129},{129,193},{2,66},{66,130... | collective-permute-start | bytes 61448 | tf_op jit(solution)/shard_map/ppermute | solution.py:444
  14.0 4.7 %collective-permute-start.1 = (f32[8,128]{1,0:T(8,128)}, f32[8,128]{1,0:T(8,128)S(1)}, u32[]{:S(2)}, u32[]{:S(2)}) collective-permute-start(f32[8,128]{1,0:T(8,128)} %get-tuple-element.32), channel_id=1, source_target_pairs={{64,0},{128,64},{192,128},{65,1},{129,65},{193,129},{66,2},{130,66... | collective-permute-start | bytes 12296 | tf_op jit(solution)/shard_map/ppermute | solution.py:445
  18.8 12.9 %copy-start = (f32[8,16,128]{2,1,0:T(8,128)}, f32[8,16,128]{2,1,0:T(8,128)S(1)}, u32[]{:S(2)}) copy-start(f32[8,16,128]{2,1,0:T(8,128)S(1)} %all-to-all-done.refs_0_.table) | copy-start | bytes 196612
  18.8 0.7 copy-start.4
  22.1 19.5 %all-to-all-start.1 = ((f32[8,56,128]{2,1,0:T(8,128)}), f32[8,56,128]{2,1,0:T(8,128)S(1)}, u32[]{:S(2)}, u32[]{:S(2)}) async-start(f32[8,56,128]{2,1,0:T(8,128)} %shard_map.128), calls=%async_computation.1 | async-start | bytes 458752 | tf_op jit(solution)/shard_map/all_to_all | solution.py:452
  35.1 16.9 %copy-start.2 = (f32[5,16,16,128]{3,2,1,0:T(8,128)S(1)}, f32[5,16,16,128]{3,2,1,0:T(8,128)}, u32[]{:S(2)}) copy-start(f32[5,16,16,128]{3,2,1,0:T(8,128)} %get-tuple-element.35.field_in) | copy-start | bytes 1966084
  35.1 16.9 %copy-start.3 = (f32[5,16,16,128]{3,2,1,0:T(8,128)S(1)}, f32[5,16,16,128]{3,2,1,0:T(8,128)}, u32[]{:S(2)}) copy-start(f32[5,16,16,128]{3,2,1,0:T(8,128)} %get-tuple-element.36.raw_in) | copy-start | bytes 1966084
  35.1 16.9 %collective-permute-start.2 = (f32[81,8,128]{2,1,0:T(8,128)}, f32[81,8,128]{2,1,0:T(8,128)S(1)}, u32[]{:S(2)}, u32[]{:S(2)}) collective-permute-start(f32[81,8,128]{2,1,0:T(8,128)} %get-tuple-element.37), channel_id=1, source_target_pairs={{0,1},{1,2},{2,3},{3,4},{4,5},{5,6},{6,7},{8,9},{9,10},{10,11},{11... | collective-permute-start | bytes 995336 | tf_op jit(solution)/shard_map/ppermute | solution.py:438
  38.6 13.4 %collective-permute-start.3 = (f32[81,8,128]{2,1,0:T(8,128)}, f32[81,8,128]{2,1,0:T(8,128)S(1)}, u32[]{:S(2)}, u32[]{:S(2)}) collective-permute-start(f32[81,8,128]{2,1,0:T(8,128)} %get-tuple-element.38), channel_id=1, source_target_pairs={{1,0},{2,1},{3,2},{4,3},{5,4},{6,5},{7,6},{9,8},{10,9},{11,10},{12... | collective-permute-start | bytes 995336 | tf_op jit(solution)/shard_map/ppermute | solution.py:439
  44.2 15.1 %all-to-all-start.2 = ((f32[8,88,128]{2,1,0:T(8,128)}), f32[8,88,128]{2,1,0:T(8,128)S(1)}, u32[]{:S(2)}, u32[]{:S(2)}) async-start(f32[8,88,128]{2,1,0:T(8,128)} %shard_map.133), calls=%async_computation.2 | async-start | bytes 720896 | tf_op jit(solution)/shard_map/all_to_all | solution.py:466
  52.1 0.8 copy-start.1
  53.6 5.7 %copy-start.10 = (f32[5]{0:T(128)S(1)}, f32[5]{0:T(128)}, u32[]{:S(2)}) copy-start(f32[5]{0:T(128)} %weight.9) | copy-start | bytes 64
  53.6 5.7 %copy-start.11 = (f32[5]{0:T(128)S(1)}, f32[5]{0:T(128)}, u32[]{:S(2)}) copy-start(f32[5]{0:T(128)} %coupling.7) | copy-start | bytes 64
  60.2 8.5 %copy-start.5 = (f32[5,8,128]{2,1,0:T(8,128)S(1)}, f32[5,8,128]{2,1,0:T(8,128)}, u32[]{:S(2)}) copy-start(f32[5,8,128]{2,1,0:T(8,128)} %inflow.7) | copy-start | bytes 61444
  60.3 8.5 %copy-start.9 = (f32[8,128]{1,0:T(8,128)S(1)}, f32[8,128]{1,0:T(8,128)}, u32[]{:S(2)}) copy-start(f32[8,128]{1,0:T(8,128)} %get-tuple-element.33.out_pressure) | copy-start | bytes 12292
  60.3 8.5 %collective-permute-start.4 = (f32[5,8,128]{2,1,0:T(8,128)S(1)}, f32[5,8,128]{2,1,0:T(8,128)S(1)}, u32[]{:S(2)}, u32[]{:S(2)}) collective-permute-start(f32[5,8,128]{2,1,0:T(8,128)S(1)} %get-tuple-element.44), channel_id=1, source_target_pairs={{0,64},{64,128},{128,192},{1,65},{65,129},{129,193},{2,66},{66,130... | collective-permute-start | bytes 61448 | tf_op jit(solution)/shard_map/ppermute | solution.py:444
  63.9 4.9 %collective-permute-start.5 = (f32[8,128]{1,0:T(8,128)S(1)}, f32[8,128]{1,0:T(8,128)S(1)}, u32[]{:S(2)}, u32[]{:S(2)}) collective-permute-start(f32[8,128]{1,0:T(8,128)S(1)} %get-tuple-element.45), channel_id=1, source_target_pairs={{64,0},{128,64},{192,128},{65,1},{129,65},{193,129},{66,2},{130,66... | collective-permute-start | bytes 12296 | tf_op jit(solution)/shard_map/ppermute | solution.py:445
  110.2 9.5 %collective-permute-start.6 = (f32[5,8,128]{2,1,0:T(8,128)S(1)}, f32[5,8,128]{2,1,0:T(8,128)S(1)}, u32[]{:S(2)}, u32[]{:S(2)}) collective-permute-start(f32[5,8,128]{2,1,0:T(8,128)S(1)} %get-tuple-element.49), channel_id=1, source_target_pairs={{0,64},{64,128},{128,192},{1,65},{65,129},{129,193},{2,66},{66,130... | collective-permute-start | bytes 61448 | tf_op jit(solution)/shard_map/ppermute | solution.py:444
  114.9 4.9 %collective-permute-start.7 = (f32[8,128]{1,0:T(8,128)S(1)}, f32[8,128]{1,0:T(8,128)S(1)}, u32[]{:S(2)}, u32[]{:S(2)}) collective-permute-start(f32[8,128]{1,0:T(8,128)S(1)} %get-tuple-element.50), channel_id=1, source_target_pairs={{64,0},{128,64},{192,128},{65,1},{129,65},{193,129},{66,2},{130,66... | collective-permute-start | bytes 12296 | tf_op jit(solution)/shard_map/ppermute | solution.py:445
  147.1 9.8 %collective-permute-start.8 = (f32[5,8,128]{2,1,0:T(8,128)S(1)}, f32[5,8,128]{2,1,0:T(8,128)S(1)}, u32[]{:S(2)}, u32[]{:S(2)}) collective-permute-start(f32[5,8,128]{2,1,0:T(8,128)S(1)} %get-tuple-element.54), channel_id=1, source_target_pairs={{0,64},{64,128},{128,192},{1,65},{65,129},{129,193},{2,66},{66,130... | collective-permute-start | bytes 61448 | tf_op jit(solution)/shard_map/ppermute | solution.py:444
  152.0 4.9 %collective-permute-start.9 = (f32[8,128]{1,0:T(8,128)S(1)}, f32[8,128]{1,0:T(8,128)S(1)}, u32[]{:S(2)}, u32[]{:S(2)}) collective-permute-start(f32[8,128]{1,0:T(8,128)S(1)} %get-tuple-element.55), channel_id=1, source_target_pairs={{64,0},{128,64},{192,128},{65,1},{129,65},{193,129},{66,2},{130,66... | collective-permute-start | bytes 12296 | tf_op jit(solution)/shard_map/ppermute | solution.py:445
  (2 other events, 1.3 us)

commit v6 on v5

v6 whole, which is shorter than its diff:
```python
import functools

import jax
import jax.numpy as jnp
from jax import lax
from jax.experimental import pallas as pl
from jax.experimental.pallas import tpu as pltpu
from jax.sharding import PartitionSpec as P


STEPS = 4
time_step = 0.08
INTERPRET = False
VMEM_LIMIT = 8 * 1024 * 1024
FAR_LIMIT = 60 * 1024 * 1024

NV = 5
ROWS = 8
FIELD_ROWS = 80
PLANES = 16
TILE_ROWS = 48


def vmem():
    return pl.BlockSpec(memory_space=pltpu.VMEM)


def smem():
    return pl.BlockSpec(memory_space=pltpu.SMEM)


def hbm():
    return pl.BlockSpec(memory_space=pltpu.HBM)


def call(kernel, outs, scalars, arrays, flops=0, scratch=(), far=()):
    moved = sum(a.size * 4 for a in arrays) + sum(4 * functools.reduce(lambda x, y: x * y, o) for o in outs)
    scratch = list(scratch)
    if far:
        scratch += [pltpu.VMEM(a.shape, jnp.float32) for a in far] + [pltpu.SemaphoreType.DMA((len(far),))]
    return pl.pallas_call(
        kernel,
        out_shape=[jax.ShapeDtypeStruct(o, jnp.float32) for o in outs],
        in_specs=[smem() for _ in scalars] + [vmem() for _ in arrays] + [hbm() for _ in far],
        out_specs=[vmem() for _ in outs],
        scratch_shapes=scratch,
        compiler_params=pltpu.CompilerParams(vmem_limit_bytes=FAR_LIMIT if far else VMEM_LIMIT),
        cost_estimate=pl.CostEstimate(flops=flops, bytes_accessed=moved, transcendentals=0),
        interpret=INTERPRET,
    )(*scalars, *arrays, *far)


def lanes_of(shape):
    return lax.broadcasted_iota(jnp.int32, shape, 1)


def rows_of(shape):
    return lax.broadcasted_iota(jnp.int32, shape, 0)


def roll(x, by, axis):
    size = x.shape[axis]
    if not isinstance(by, int):
        return pltpu.roll(x, lax.rem(by + 2 * size, size), axis)
    by %= size
    return x if by == 0 else pltpu.roll(x, by, axis)


def pressure(weight_ref, values):
    total = weight_ref[0] * values[0]
    for v in range(1, NV):
        total = total + weight_ref[v] * values[v]
    return total


def fetch(sources, targets, sems):
    copies = [pltpu.make_async_copy(a, b, sems.at[i]) for i, (a, b) in enumerate(zip(sources, targets))]
    for copy in copies:
        copy.start()
    for copy in copies:
        copy.wait()


def first_kernel(ids, weight, down_donors, up_donors, *refs):
    sources, (down, up, out_pressure, send, to_above, to_below), targets, sems = refs[:5], refs[5:11], refs[11:16], refs[16]
    fetch(sources, targets, sems)
    state, radial, circ, mu, outflow = targets
    lanes = lanes_of((8, 128))
    row, size = ids[1], send.shape[0]
    for v in range(NV):
        down[v] = state[v, PLANES - 1]
    up[...] = pressure(weight, [state[v, 0] for v in range(NV)])
    out_pressure[...] = pressure(weight, [outflow[v] for v in range(NV)])
    listed = jnp.zeros((8, 128), jnp.int32)
    for a in range(8):
        listed = jnp.where(lanes == a, down_donors[a], listed)
        listed = jnp.where(lanes == 8 + a, up_donors[a], listed)
    listed = listed.astype(jnp.float32)
    for j in range(size):
        send[j, 0:8, :] = listed

    def put(at, cell):
        to_above[pl.ds(at, 1), :] = cell[7:8]
        to_below[pl.ds(at, 1), :] = cell[0:1]

    def one(k, carry):
        last, first = carry
        for v in range(NV):
            cell = state[v, k]
            at = v * 16 + k
            put(at, cell)
            here = lanes == at
            last = jnp.where(here, roll(cell, at + 1, 1), last)
            first = jnp.where(here, roll(cell, at, 1), first)
        put(FIELD_ROWS + k, mu[k])
        put(FIELD_ROWS + 16 + k, radial[k])
        here = lanes == 80 + k
        last = jnp.where(here, roll(mu[k], 81 + k, 1), last)
        first = jnp.where(here, roll(mu[k], 80 + k, 1), first)
        last = jnp.where(lanes == 96 + k, roll(circ[k], 97 + k, 1), last)
        return last, first

    zero = jnp.zeros((8, 128), jnp.float32)
    last, first = lax.fori_loop(0, PLANES, one, (zero, zero))
    send[lax.rem(row + 1, size), 8:16, :] = last
    send[lax.rem(row + size - 1, size), 8:16, :] = first


def gather_kernel(ids, down, up, inflow, out_pressure, after, send):
    section = ids[0]
    size = send.shape[0]
    for v in range(NV):
        value = jnp.where(section == 0, inflow[v], down[v])
        for j in range(size):
            send[j, v * 8 : v * 8 + 8, :] = value
    value = jnp.where(section == ids[4] - 1, out_pressure[...], up[...])
    for j in range(size):
        send[j, 40:48, :] = value


def select_kernel(step, ids, wanted, got, *refs):
    send = refs[-1]
    size = send.shape[0]
    row = ids[1]

    def one(j, carry):
        for a in range(8):
            d = wanted[j, a] & 63
            r, b = d >> 3, d & 7
            for v in range(NV):
                send[j, v * 8 + a : v * 8 + a + 1, :] = got[r, pl.ds(v * 8 + b, 1), :]
            e = wanted[j, 8 + a] & 63
            send[j, 40 + a : 41 + a, :] = got[e >> 3, pl.ds(40 + (e & 7), 1), :]
        return carry

    lax.fori_loop(0, size, one, 0)
    if step:
        edges = refs[0]
        send[lax.rem(row + 1, size), 48:56, :] = edges[0]
        send[lax.rem(row + size - 1, size), 48:56, :] = edges[1]


def sides(step, ids, around):
    base = 48 if step else 8
    row, row_size = ids[1], ids[5]
    left = around[lax.rem(row + row_size - 1, row_size), base : base + ROWS, :]
    right = around[lax.rem(row + 1, row_size), base : base + ROWS, :]
    return left, right


def beyond(ref, at):
    return jnp.broadcast_to(ref[pl.ds(at, 1), :], (ROWS, 128))


def coef_kernel(ids, volume, axial, radial, circ, mu, around, low, high, coef):
    rad, rad_size = ids[2], ids[3]
    lanes = lanes_of((ROWS, 128))
    rows = rows_of((ROWS, 128))
    casing = jnp.logical_and(rad == rad_size - 1, rows == 7)
    left, right = sides(0, ids, around)

    def one(k, carry):
        m = mu[k]
        c = time_step / volume[k]
        half = 0.5 * c
        diffused = []

        def put(at, area, viscous):
            coef[at, k] = half * area
            b = c * area * viscous
            coef[at + 1, k] = b
            diffused.append(b)

        lower, upper = jnp.maximum(k - 1, 0), jnp.minimum(k + 1, PLANES - 1)
        put(0, axial[lower], 0.5 * (m + mu[lower]))
        put(2, axial[k], 0.5 * (m + mu[upper]))
        face = jnp.where(casing, 0.0, radial[k])
        face_below = jnp.where(rows == 0, beyond(low, FIELD_ROWS + 16 + k), roll(face, 1, 0))
        mu_below = jnp.where(rows == 0, beyond(low, FIELD_ROWS + k), roll(m, 1, 0))
        mu_above = jnp.where(rows == 7, beyond(high, FIELD_ROWS + k), roll(m, 7, 0))
        put(4, face_below, 0.5 * (m + mu_below))
        put(6, face, 0.5 * (m + mu_above))
        ring = circ[k]
        at = 80 + k
        mu_left = jnp.where(lanes == 0, roll(left, -at, 1), roll(m, 1, 1))
        mu_right = jnp.where(lanes == 127, roll(right, 127 - at, 1), roll(m, 127, 1))
        circ_left = jnp.where(lanes == 0, roll(left, -(at + 16), 1), roll(ring, 1, 1))
        put(8, circ_left, 0.5 * (mu_left + m))
        put(10, ring, 0.5 * (m + mu_right))
        total = diffused[0]
        for b in diffused[1:]:
            total = total + b
        coef[12, k] = 1.0 - total
        return carry

    lax.fori_loop(0, PLANES, one, 0)


def advance(k, before, here, after, coef, matrix, left, right, low, high):
    lanes = lanes_of((ROWS, 128))
    rows = rows_of((ROWS, 128))
    rest = coef[12, k]
    total = [rest * here[v] for v in range(NV)]
    for d in range(3):
        low_a, low_b = coef[4 * d, k], coef[4 * d + 1, k]
        high_a, high_b = coef[4 * d + 2, k], coef[4 * d + 3, k]
        own_a = high_a - low_a
        mixed = []
        for v in range(NV):
            cell = here[v]
            at = v * 16 + k
            if d == 0:
                lower, upper = before[v], after[v]
            elif d == 1:
                lower = jnp.where(rows == 0, beyond(low, at), roll(cell, 1, 0))
                upper = jnp.where(rows == 7, beyond(high, at), roll(cell, 7, 0))
            else:
                lower = jnp.where(lanes == 0, roll(left, -at, 1), roll(cell, 1, 1))
                upper = jnp.where(lanes == 127, roll(right, 127 - at, 1), roll(cell, 127, 1))
            mixed.append(high_a * upper - low_a * lower + own_a * cell)
            total[v] = total[v] + (high_b * upper + low_b * lower)
        for u in range(NV):
            for v in range(NV):
                at = 25 * d + 5 * u + v
                total[u] = total[u] - jnp.broadcast_to(matrix[at : at + 1, :], (ROWS, 128)) * mixed[v]
    return total


def ghosts_of(ids, wanted, weight, coupling, field, across, ghost):
    for a in range(8):
        d = wanted[ids[1], a] >> 6
        for v in range(NV):
            ghost[v, a : a + 1, :] = across[d, v * 8 + a : v * 8 + a + 1, :]
        e = wanted[ids[1], 8 + a] >> 6
        ghost[NV, a : a + 1, :] = across[e, 40 + a : 41 + a, :]
    outlet = [field[v, PLANES - 1] for v in range(NV)]
    jump = ghost[NV] - pressure(weight, outlet)
    return [ghost[v] for v in range(NV)], [outlet[v] + coupling[v] * jump for v in range(NV)]


def ends_of(step, ids, wanted, weight, coupling, field, coef, matrix, across, around, low, high, ghost):
    lanes = lanes_of((ROWS, 128))
    left, right = sides(step, ids, around)
    inlet_ghost, outlet_ghost = ghosts_of(ids, wanted, weight, coupling, field, across, ghost)
    plane = lambda k: [field[v, k] for v in range(NV)]
    new_inlet = advance(0, inlet_ghost, plane(0), plane(1), coef, matrix, left, right, low, high)
    last = PLANES - 1
    new_outlet = advance(last, plane(last - 1), plane(last), outlet_ghost, coef, matrix, left, right, low, high)
    return new_inlet, new_outlet


def ends_kernel(step, ids, wanted, weight, coupling, field, coef, matrix, across, around, low, high, ends, down, up, ghost):
    new_inlet, new_outlet = ends_of(step, ids, wanted, weight, coupling, field, coef, matrix, across, around, low, high, ghost)
    for v in range(NV):
        ends[0, v] = new_inlet[v]
        ends[1, v] = new_outlet[v]
        down[v] = new_outlet[v]
    up[...] = pressure(weight, new_inlet)


def bulk_kernel(step, ids, field, coef, matrix, around, low, high, ends, new, edges, to_above, to_below):
    lanes = lanes_of((ROWS, 128))
    left, right = sides(step, ids, around)

    def note(k, total, last, first):
        for v in range(NV):
            new[v, k] = total[v]
            at = v * 16 + k
            to_above[pl.ds(at, 1), :] = total[v][7:8]
            to_below[pl.ds(at, 1), :] = total[v][0:1]
            spot = lanes == at
            last = jnp.where(spot, roll(total[v], at + 1, 1), last)
            first = jnp.where(spot, roll(total[v], at, 1), first)
        return last, first

    def one(k, carry):
        before, here, last, first = carry
        after = [field[v, k + 1] for v in range(NV)]
        total = advance(k, before, here, after, coef, matrix, left, right, low, high)
        last, first = note(k, total, last, first)
        return here, after, last, first

    zero = jnp.zeros((ROWS, 128), jnp.float32)
    last, first = note(0, [ends[0, v] for v in range(NV)], zero, zero)
    last, first = note(PLANES - 1, [ends[1, v] for v in range(NV)], last, first)
    carry = ([field[v, 0] for v in range(NV)], [field[v, 1] for v in range(NV)], last, first)
    _, _, last, first = lax.fori_loop(1, PLANES - 1, one, carry)
    edges[0] = last
    edges[1] = first


def last_kernel(step, ids, wanted, weight, coupling, field, coef, matrix, across, around, low, high, new, ghost):
    lanes = lanes_of((ROWS, 128))
    left, right = sides(step, ids, around)
    new_inlet, new_outlet = ends_of(step, ids, wanted, weight, coupling, field, coef, matrix, across, around, low, high, ghost)
    for v in range(NV):
        new[v, 0] = new_inlet[v]
        new[v, PLANES - 1] = new_outlet[v]

    def one(k, carry):
        before, here = carry
        after = [field[v, k + 1] for v in range(NV)]
        total = advance(k, before, here, after, coef, matrix, left, right, low, high)
        for v in range(NV):
            new[v, k] = total[v]
        return here, after

    carry = ([field[v, 0] for v in range(NV)], [field[v, 1] for v in range(NV)])
    lax.fori_loop(1, PLANES - 1, one, carry)


def body(
    state,
    volume,
    face_axial,
    face_radial,
    face_circum,
    viscosity,
    flux_matrix,
    inflow_plane,
    outflow_plane,
    down_donors,
    up_donors,
    pressure_weight,
    boundary_coupling,
):
    sections, row_size, rad_size = lax.axis_size("sec"), lax.axis_size("row"), lax.axis_size("rad")
    ids = jnp.stack(
        [
            lax.axis_index("sec"),
            lax.axis_index("row"),
            lax.axis_index("rad"),
            jnp.int32(rad_size),
            jnp.int32(sections),
            jnp.int32(row_size),
        ]
    ).astype(jnp.int32)
    own = [state[:, 0], volume[0], face_axial[0], face_radial[0], face_circum[0], viscosity[0]]
    matrix = jnp.broadcast_to(jnp.pad(flux_matrix[0].reshape(75), (0, 5))[:, None], (80, 128))
    extended = (NV, PLANES, ROWS, 128)
    strips = (2, ROWS, 128)
    sent = (FIELD_ROWS + 32, 128)
    scalars = [pressure_weight, boundary_coupling]

    down, up, out_pressure, lists, to_above, to_below = call(
        first_kernel,
        [(NV, 8, 128), (8, 128), (8, 128), (row_size, 16, 128), sent, sent],
        [ids, pressure_weight, down_donors[0], up_donors[0]],
        [],
        far=[own[0], own[3], own[4], own[5], outflow_plane],
    )
    forward = [(i, i + 1) for i in range(sections - 1)]
    backward = [(i + 1, i) for i in range(sections - 1)]
    outward = [(i, i + 1) for i in range(rad_size - 1)]
    inward = [(i + 1, i) for i in range(rad_size - 1)]
    table = lax.all_to_all(lists, "row", 0, 0)
    wanted = table[:, 0, :16].astype(jnp.int32)
    field = own[0]
    coef = edges = None
    for step in range(STEPS):
        last_step = step == STEPS - 1
        down = lax.ppermute(down, "sec", forward)
        up = lax.ppermute(up, "sec", backward)
        (send,) = call(
            gather_kernel,
            [(rad_size, TILE_ROWS, 128)],
            [ids],
            [down, up, inflow_plane, out_pressure, edges if step else table],
        )
        got = lax.all_to_all(send, "rad", 0, 0)
        low = lax.ppermute(to_above, "rad", outward)
        high = lax.ppermute(to_below, "rad", inward)
        if step == 0:
            (coef,) = call(coef_kernel, [(13, PLANES, ROWS, 128)], [ids], own[1:] + [table, low, high])
        (send,) = call(
            functools.partial(select_kernel, step),
            [(row_size, TILE_ROWS + (ROWS if step else 0), 128)],
            [ids, wanted],
            [got, edges] if step else [got],
        )
        across = lax.all_to_all(send, "row", 0, 0)
        around = across if step else table
        ghost = [pltpu.VMEM((NV + 1, ROWS, 128), jnp.float32)]
        if last_step:
            (field,) = call(
                functools.partial(last_kernel, step),
                [(NV, PLANES, 8, 128)],
                [ids, wanted] + scalars,
                [field, coef, matrix, across, around, low, high],
                flops=PLANES * ROWS * 128 * 300,
                scratch=ghost,
            )
        else:
            ends, down, up = call(
                functools.partial(ends_kernel, step),
                [(2, NV, ROWS, 128), (NV, 8, 128), (8, 128)],
                [ids, wanted] + scalars,
                [field, coef, matrix, across, around, low, high],
                flops=2 * ROWS * 128 * 300,
                scratch=ghost,
            )
            field, edges, to_above, to_below = call(
                functools.partial(bulk_kernel, step),
                [extended, strips, (FIELD_ROWS, 128), (FIELD_ROWS, 128)],
                [ids],
                [field, coef, matrix, around, low, high, ends],
                flops=PLANES * ROWS * 128 * 300,
            )
    return field[:, None]


def solution(mesh):
    in_specs = (
        P(None, "sec", None, "rad", "row"),
        P("sec", None, "rad", "row"),
        P("sec", None, "rad", "row"),
        P("sec", None, "rad", "row"),
        P("sec", None, "rad", "row"),
        P("sec", None, "rad", "row"),
        P("sec", None, None, None),
        P(None, "rad", "row"),
        P(None, "rad", "row"),
        P("sec", ("row", "rad")),
        P("sec", ("row", "rad")),
        P(),
        P(),
    )
    out_specs = P(None, "sec", None, "rad", "row")

    return jax.shard_map(body, mesh=mesh, in_specs=in_specs, out_specs=out_specs, check_vma=False)
```

time: 187 us -> 209 us (1.12)
  the two profiles are of different devices: /device:TPU:1 before, /device:TPU:46 now
where the time goes in v6:
time: 209 us; the launch traced here: 207 us
  starting transfers between devices  81.7 us (39%)
  waiting for transfers between devices  52.8 us (25%)
  blocking collectives  41.3 us (20%)
  Pallas kernels  29.8 us (14%)
    all_to_all x3, blocking collectives, body(): got = lax.all_to_all(send, 'rad', 0, 0)  41.3 us
    ppermute x4, waiting for transfers between devices, body(): high = lax.ppermute(to_below, 'rad', inward)  40 us
    pallas_call x17, Pallas kernels, call(): pl.pallas_call(kernel, out_shape=[jax.ShapeDtypeStruct(o, jnp.float32) fo...  29.8 us
    all_to_all x4, starting transfers between devices, body(): across = lax.all_to_all(send, 'row', 0, 0)  19.4 us
    ppermute x4, starting transfers between devices, body(): low = lax.ppermute(to_above, 'rad', outward)  16.8 us
    ppermute x4, starting transfers between devices, body(): down = lax.ppermute(down, 'sec', forward)  12.8 us
    ppermute x4, starting transfers between devices, body(): up = lax.ppermute(up, 'sec', backward)  10.6 us
    all_to_all x1, starting transfers between devices, body(): got = lax.all_to_all(send, 'rad', 0, 0)  9.6 us
  transfers between devices with their start and end apart: 22, of which 6 were waited for; matrix products, arithmetic and copies ran while one was open for 0% of the time, Pallas kernels for 5%

profile of v6, /device:TPU:46, one launch (start us, length us, event | category | flops | bytes accessed | tf_op | source)
XLA Modules:
  0.0 207.5 jit_solution(11496648312198139835)
XLA Ops:
  0.6 3.9 %shard_map.127 = (f32[5,8,128]{2,1,0:T(8,128)}, f32[8,128]{1,0:T(8,128)}, f32[8,128]{1,0:T(8,128)}, f32[8,16,128]{2,1,0:T(8,128)}, f32[112,128]{1,0:T(8,128)}, /*index=5*/f32[112,128]{1,0:T(8,128)}) custom-call(s32[6]{0:T(128)} %stack.15.ids, f32[5]{0:T(128)} %weight.9, s32[8]{0:T(128)} %bitcast.34, s32[8]{0:T(128)} %bitcast.35, f32[5,16,8,128]{3,2,1,0:T(8,128)} %bitcast.15, ...), custom_call_target="tpu_custom_call" | custom-call | bytes 208896 | tf_op jit(solution)/shard_map/pallas_call | solution.py:41
  4.5 4.9 %all-to-all-start = ((f32[8,16,128]{2,1,0:T(8,128)}), f32[8,16,128]{2,1,0:T(8,128)S(1)}, u32[]{:S(2)}, u32[]{:S(2)}) async-start(f32[8,16,128]{2,1,0:T(8,128)} %get-tuple-element.32), calls=%async_computation | async-start | bytes 131072 | tf_op jit(solution)/shard_map/all_to_all | solution.py:376
  9.5 3.8 %collective-permute-start.2 = (f32[5,8,128]{2,1,0:T(8,128)S(1)}, f32[5,8,128]{2,1,0:T(8,128)S(1)}, u32[]{:S(2)}, u32[]{:S(2)}) collective-permute-start(f32[5,8,128]{2,1,0:T(8,128)S(1)} %copy-done.14), channel_id=1, source_target_pairs={{0,64},{64,128},{128,192},{1,65},{65,129},{129,193},{2,66},{66,130... | collective-permute-start | bytes 61448 | tf_op jit(solution)/shard_map/ppermute | solution.py:382
  15.3 3.5 %collective-permute-done.3.up = f32[8,128]{1,0:T(8,128)S(1)} collective-permute-done((f32[8,128]{1,0:T(8,128)S(1)}, f32[8,128]{1,0:T(8,128)S(1)}, u32[]{:S(2)}, u32[]{:S(2)}) %collective-permute-start.3) | collective-permute-done | bytes 4128 | tf_op jit(solution)/shard_map/ppermute | solution.py:383
  20.1 9.6 %all-to-all-start.1 = ((f32[8,48,128]{2,1,0:T(8,128)}), f32[8,48,128]{2,1,0:T(8,128)S(1)}, u32[]{:S(2)}, u32[]{:S(2)}) async-start(f32[8,48,128]{2,1,0:T(8,128)} %shard_map.129), calls=%async_computation.1 | async-start | bytes 393216 | tf_op jit(solution)/shard_map/all_to_all | solution.py:390
  29.7 9.2 %all-to-all-done.1.got = f32[8,48,128]{2,1,0:T(8,128)S(1)} async-done(((f32[8,48,128]{2,1,0:T(8,128)}), f32[8,48,128]{2,1,0:T(8,128)S(1)}, u32[]{:S(2)}, u32[]{:S(2)}) %all-to-all-start.1) | async-done | bytes 196640 | tf_op jit(solution)/shard_map/all_to_all | solution.py:390
  40.6 4.9 %all-to-all-start.2 = ((f32[8,48,128]{2,1,0:T(8,128)}), f32[8,48,128]{2,1,0:T(8,128)S(1)}, u32[]{:S(2)}, u32[]{:S(2)}) async-start(f32[8,48,128]{2,1,0:T(8,128)} %shard_map.130), calls=%async_computation.2 | async-start | bytes 393216 | tf_op jit(solution)/shard_map/all_to_all | solution.py:401
  45.6 4.2 %collective-permute-start = (f32[112,128]{1,0:T(8,128)S(1)}, f32[112,128]{1,0:T(8,128)S(1)}, u32[]{:S(2)}, u32[]{:S(2)}) collective-permute-start(f32[112,128]{1,0:T(8,128)S(1)} %copy-done.13), channel_id=1, source_target_pairs={{0,1},{1,2},{2,3},{3,4},{4,5},{5,6},{6,7},{8,9},{9,10},{10,11},{11... | collective-permute-start | bytes 172040 | tf_op jit(solution)/shard_map/ppermute | solution.py:391
  51.9 10.1 %collective-permute-done.1.high = f32[112,128]{1,0:T(8,128)S(1)} collective-permute-done((f32[112,128]{1,0:T(8,128)S(1)}, f32[112,128]{1,0:T(8,128)S(1)}, u32[]{:S(2)}, u32[]{:S(2)}) %collective-permute-start.1) | collective-permute-done | bytes 57376 | tf_op jit(solution)/shard_map/ppermute | solution.py:392
  67.9 3.2 %collective-permute-start.5 = (f32[8,128]{1,0:T(8,128)S(1)}, f32[8,128]{1,0:T(8,128)S(1)}, u32[]{:S(2)}, u32[]{:S(2)}) collective-permute-start(f32[8,128]{1,0:T(8,128)S(1)} %get-tuple-element.41), channel_id=1, source_target_pairs={{64,0},{128,64},{192,128},{65,1},{129,65},{193,129},{66,2},{130,66... | collective-permute-start | bytes 12296 | tf_op jit(solution)/shard_map/ppermute | solution.py:383
  74.8 13.5 %all_to_all.45.got = f32[8,48,128]{2,1,0:T(8,128)S(1)} all-to-all(f32[8,48,128]{2,1,0:T(8,128)S(1)} %shard_map.133), channel_id=1, replica_groups=mesh['sec'=4,'row'=8,'rad'=8] {'rad'}, dimensions={0} | all-to-all | bytes 393216 | tf_op jit(solution)/shard_map/all_to_all | solution.py:390
  90.0 4.8 %all-to-all-start.4 = ((f32[8,56,128]{2,1,0:T(8,128)}), f32[8,56,128]{2,1,0:T(8,128)S(1)}, u32[]{:S(2)}, u32[]{:S(2)}) async-start(f32[8,56,128]{2,1,0:T(8,128)} %shard_map.134), calls=%async_computation.4 | async-start | bytes 458752 | tf_op jit(solution)/shard_map/all_to_all | solution.py:401
  94.8 4.2 %collective-permute-start.6 = (f32[80,128]{1,0:T(8,128)S(1)}, f32[80,128]{1,0:T(8,128)S(1)}, u32[]{:S(2)}, u32[]{:S(2)}) collective-permute-start(f32[80,128]{1,0:T(8,128)S(1)} %get-tuple-element.43), channel_id=1, source_target_pairs={{0,1},{1,2},{2,3},{3,4},{4,5},{5,6},{6,7},{8,9},{9,10},{10,11},{11... | collective-permute-start | bytes 122888 | tf_op jit(solution)/shard_map/ppermute | solution.py:391
  101.0 10.0 %collective-permute-done.7.high = f32[80,128]{1,0:T(8,128)S(1)} collective-permute-done((f32[80,128]{1,0:T(8,128)S(1)}, f32[80,128]{1,0:T(8,128)S(1)}, u32[]{:S(2)}, u32[]{:S(2)}) %collective-permute-start.7) | collective-permute-done | bytes 40992 | tf_op jit(solution)/shard_map/ppermute | solution.py:392
  111.7 3.2 %collective-permute-start.8 = (f32[5,8,128]{2,1,0:T(8,128)S(1)}, f32[5,8,128]{2,1,0:T(8,128)S(1)}, u32[]{:S(2)}, u32[]{:S(2)}) collective-permute-start(f32[5,8,128]{2,1,0:T(8,128)S(1)} %get-tuple-element.47), channel_id=1, source_target_pairs={{0,64},{64,128},{128,192},{1,65},{65,129},{129,193},{2,66},{66,130... | collective-permute-start | bytes 61448 | tf_op jit(solution)/shard_map/ppermute | solution.py:382
  121.3 13.9 %all_to_all.46.got = f32[8,48,128]{2,1,0:T(8,128)S(1)} all-to-all(f32[8,48,128]{2,1,0:T(8,128)S(1)} %shard_map.137), channel_id=1, replica_groups=mesh['sec'=4,'row'=8,'rad'=8] {'rad'}, dimensions={0} | all-to-all | bytes 393216 | tf_op jit(solution)/shard_map/all_to_all | solution.py:390
  136.8 4.8 %all-to-all-start.6 = ((f32[8,56,128]{2,1,0:T(8,128)}), f32[8,56,128]{2,1,0:T(8,128)S(1)}, u32[]{:S(2)}, u32[]{:S(2)}) async-start(f32[8,56,128]{2,1,0:T(8,128)} %shard_map.138), calls=%async_computation.6 | async-start | bytes 458752 | tf_op jit(solution)/shard_map/all_to_all | solution.py:401
  141.6 4.2 %collective-permute-start.10 = (f32[80,128]{1,0:T(8,128)S(1)}, f32[80,128]{1,0:T(8,128)S(1)}, u32[]{:S(2)}, u32[]{:S(2)}) collective-permute-start(f32[80,128]{1,0:T(8,128)S(1)} %get-tuple-element.50), channel_id=1, source_target_pairs={{0,1},{1,2},{2,3},{3,4},{4,5},{5,6},{6,7},{8,9},{9,10},{10,11},{11... | collective-permute-start | bytes 122888 | tf_op jit(solution)/shard_map/ppermute | solution.py:391
  147.8 10.0 %collective-permute-done.11.high = f32[80,128]{1,0:T(8,128)S(1)} collective-permute-done((f32[80,128]{1,0:T(8,128)S(1)}, f32[80,128]{1,0:T(8,128)S(1)}, u32[]{:S(2)}, u32[]{:S(2)}) %collective-permute-start.11) | collective-permute-done | bytes 40992 | tf_op jit(solution)/shard_map/ppermute | solution.py:392
  158.5 3.2 %collective-permute-start.12 = (f32[5,8,128]{2,1,0:T(8,128)S(1)}, f32[5,8,128]{2,1,0:T(8,128)S(1)}, u32[]{:S(2)}, u32[]{:S(2)}) collective-permute-start(f32[5,8,128]{2,1,0:T(8,128)S(1)} %get-tuple-element.54), channel_id=1, source_target_pairs={{0,64},{64,128},{128,192},{1,65},{65,129},{129,193},{2,66},{66,130... | collective-permute-start | bytes 61448 | tf_op jit(solution)/shard_map/ppermute | solution.py:382
  168.1 13.9 %all_to_all.47.got = f32[8,48,128]{2,1,0:T(8,128)S(1)} all-to-all(f32[8,48,128]{2,1,0:T(8,128)S(1)} %shard_map.141), channel_id=1, replica_groups=mesh['sec'=4,'row'=8,'rad'=8] {'rad'}, dimensions={0} | all-to-all | bytes 393216 | tf_op jit(solution)/shard_map/all_to_all | solution.py:390
  183.6 4.8 %all-to-all-start.8 = ((f32[8,56,128]{2,1,0:T(8,128)}), f32[8,56,128]{2,1,0:T(8,128)S(1)}, u32[]{:S(2)}, u32[]{:S(2)}) async-start(f32[8,56,128]{2,1,0:T(8,128)} %shard_map.142), calls=%async_computation.8 | async-start | bytes 458752 | tf_op jit(solution)/shard_map/all_to_all | solution.py:401
  188.4 4.2 %collective-permute-start.14 = (f32[80,128]{1,0:T(8,128)S(1)}, f32[80,128]{1,0:T(8,128)S(1)}, u32[]{:S(2)}, u32[]{:S(2)}) collective-permute-start(f32[80,128]{1,0:T(8,128)S(1)} %get-tuple-element.57), channel_id=1, source_target_pairs={{0,1},{1,2},{2,3},{3,4},{4,5},{5,6},{6,7},{8,9},{9,10},{10,11},{11... | collective-permute-start | bytes 122888 | tf_op jit(solution)/shard_map/ppermute | solution.py:391
  194.6 10.0 %collective-permute-done.15.high = f32[80,128]{1,0:T(8,128)S(1)} collective-permute-done((f32[80,128]{1,0:T(8,128)S(1)}, f32[80,128]{1,0:T(8,128)S(1)}, u32[]{:S(2)}, u32[]{:S(2)}) %collective-permute-start.15) | collective-permute-done | bytes 40992 | tf_op jit(solution)/shard_map/ppermute | solution.py:392
  (78 shorter events, 45.1 us)
Async XLA Ops:
  4.5 14.3 %all-to-all-start = ((f32[8,16,128]{2,1,0:T(8,128)}), f32[8,16,128]{2,1,0:T(8,128)S(1)}, u32[]{:S(2)}, u32[]{:S(2)}) async-start(f32[8,16,128]{2,1,0:T(8,128)} %get-tuple-element.32), calls=%async_computation | async-start | bytes 131072 | tf_op jit(solution)/shard_map/all_to_all | solution.py:376
  9.5 9.4 %collective-permute-start.2 = (f32[5,8,128]{2,1,0:T(8,128)S(1)}, f32[5,8,128]{2,1,0:T(8,128)S(1)}, u32[]{:S(2)}, u32[]{:S(2)}) collective-permute-start(f32[5,8,128]{2,1,0:T(8,128)S(1)} %copy-done.14), channel_id=1, source_target_pairs={{0,64},{64,128},{128,192},{1,65},{65,129},{129,193},{2,66},{66,130... | collective-permute-start | bytes 61448 | tf_op jit(solution)/shard_map/ppermute | solution.py:382
  13.3 5.5 %collective-permute-start.3 = (f32[8,128]{1,0:T(8,128)S(1)}, f32[8,128]{1,0:T(8,128)S(1)}, u32[]{:S(2)}, u32[]{:S(2)}) collective-permute-start(f32[8,128]{1,0:T(8,128)S(1)} %copy-done.15), channel_id=1, source_target_pairs={{64,0},{128,64},{192,128},{65,1},{129,65},{193,129},{66,2},{130,66... | collective-permute-start | bytes 12296 | tf_op jit(solution)/shard_map/ppermute | solution.py:383
  20.1 18.8 %all-to-all-start.1 = ((f32[8,48,128]{2,1,0:T(8,128)}), f32[8,48,128]{2,1,0:T(8,128)S(1)}, u32[]{:S(2)}, u32[]{:S(2)}) async-start(f32[8,48,128]{2,1,0:T(8,128)} %shard_map.129), calls=%async_computation.1 | async-start | bytes 393216 | tf_op jit(solution)/shard_map/all_to_all | solution.py:390
  40.6 21.4 %copy-start.2 = (f32[1,16,8,128]{3,2,1,0:T(8,128)S(1)}, f32[1,16,8,128]{3,2,1,0:T(8,128)}, u32[]{:S(2)}) copy-start(f32[1,16,8,128]{3,2,1,0:T(8,128)} %param.16) | copy-start | bytes 196612
  40.6 21.4 %copy-start.3 = (f32[1,16,8,128]{3,2,1,0:T(8,128)S(1)}, f32[1,16,8,128]{3,2,1,0:T(8,128)}, u32[]{:S(2)}) copy-start(f32[1,16,8,128]{3,2,1,0:T(8,128)} %param.17) | copy-start | bytes 196612
  40.6 23.3 %all-to-all-start.2 = ((f32[8,48,128]{2,1,0:T(8,128)}), f32[8,48,128]{2,1,0:T(8,128)S(1)}, u32[]{:S(2)}, u32[]{:S(2)}) async-start(f32[8,48,128]{2,1,0:T(8,128)} %shard_map.130), calls=%async_computation.2 | async-start | bytes 393216 | tf_op jit(solution)/shard_map/all_to_all | solution.py:401
  45.6 6.3 %collective-permute-start = (f32[112,128]{1,0:T(8,128)S(1)}, f32[112,128]{1,0:T(8,128)S(1)}, u32[]{:S(2)}, u32[]{:S(2)}) collective-permute-start(f32[112,128]{1,0:T(8,128)S(1)} %copy-done.13), channel_id=1, source_target_pairs={{0,1},{1,2},{2,3},{3,4},{4,5},{5,6},{6,7},{8,9},{9,10},{10,11},{11... | collective-permute-start | bytes 172040 | tf_op jit(solution)/shard_map/ppermute | solution.py:391
  49.8 12.2 %collective-permute-start.1 = (f32[112,128]{1,0:T(8,128)S(1)}, f32[112,128]{1,0:T(8,128)S(1)}, u32[]{:S(2)}, u32[]{:S(2)}) collective-permute-start(f32[112,128]{1,0:T(8,128)S(1)} %copy-done.12), channel_id=1, source_target_pairs={{1,0},{2,1},{3,2},{4,3},{5,4},{6,5},{7,6},{9,8},{10,9},{11,10},{12... | collective-permute-start | bytes 172040 | tf_op jit(solution)/shard_map/ppermute | solution.py:392
  65.3 9.0 %collective-permute-start.4 = (f32[5,8,128]{2,1,0:T(8,128)S(1)}, f32[5,8,128]{2,1,0:T(8,128)S(1)}, u32[]{:S(2)}, u32[]{:S(2)}) collective-permute-start(f32[5,8,128]{2,1,0:T(8,128)S(1)} %get-tuple-element.40), channel_id=1, source_target_pairs={{0,64},{64,128},{128,192},{1,65},{65,129},{129,193},{2,66},{66,130... | collective-permute-start | bytes 61448 | tf_op jit(solution)/shard_map/ppermute | solution.py:382
  67.9 6.3 %collective-permute-start.5 = (f32[8,128]{1,0:T(8,128)S(1)}, f32[8,128]{1,0:T(8,128)S(1)}, u32[]{:S(2)}, u32[]{:S(2)}) collective-permute-start(f32[8,128]{1,0:T(8,128)S(1)} %get-tuple-element.41), channel_id=1, source_target_pairs={{64,0},{128,64},{192,128},{65,1},{129,65},{193,129},{66,2},{130,66... | collective-permute-start | bytes 12296 | tf_op jit(solution)/shard_map/ppermute | solution.py:383
  90.0 20.9 %all-to-all-start.4 = ((f32[8,56,128]{2,1,0:T(8,128)}), f32[8,56,128]{2,1,0:T(8,128)S(1)}, u32[]{:S(2)}, u32[]{:S(2)}) async-start(f32[8,56,128]{2,1,0:T(8,128)} %shard_map.134), calls=%async_computation.4 | async-start | bytes 458752 | tf_op jit(solution)/shard_map/all_to_all | solution.py:401
  94.8 6.1 %collective-permute-start.6 = (f32[80,128]{1,0:T(8,128)S(1)}, f32[80,128]{1,0:T(8,128)S(1)}, u32[]{:S(2)}, u32[]{:S(2)}) collective-permute-start(f32[80,128]{1,0:T(8,128)S(1)} %get-tuple-element.43), channel_id=1, source_target_pairs={{0,1},{1,2},{2,3},{3,4},{4,5},{5,6},{6,7},{8,9},{9,10},{10,11},{11... | collective-permute-start | bytes 122888 | tf_op jit(solution)/shard_map/ppermute | solution.py:391
  99.0 11.9 %collective-permute-start.7 = (f32[80,128]{1,0:T(8,128)S(1)}, f32[80,128]{1,0:T(8,128)S(1)}, u32[]{:S(2)}, u32[]{:S(2)}) collective-permute-start(f32[80,128]{1,0:T(8,128)S(1)} %get-tuple-element.44), channel_id=1, source_target_pairs={{1,0},{2,1},{3,2},{4,3},{5,4},{6,5},{7,6},{9,8},{10,9},{11,10},{12... | collective-permute-start | bytes 122888 | tf_op jit(solution)/shard_map/ppermute | solution.py:392
  111.7 9.0 %collective-permute-start.8 = (f32[5,8,128]{2,1,0:T(8,128)S(1)}, f32[5,8,128]{2,1,0:T(8,128)S(1)}, u32[]{:S(2)}, u32[]{:S(2)}) collective-permute-start(f32[5,8,128]{2,1,0:T(8,128)S(1)} %get-tuple-element.47), channel_id=1, source_target_pairs={{0,64},{64,128},{128,192},{1,65},{65,129},{129,193},{2,66},{66,130... | collective-permute-start | bytes 61448 | tf_op jit(solution)/shard_map/ppermute | solution.py:382
  114.9 5.8 %collective-permute-start.9 = (f32[8,128]{1,0:T(8,128)S(1)}, f32[8,128]{1,0:T(8,128)S(1)}, u32[]{:S(2)}, u32[]{:S(2)}) collective-permute-start(f32[8,128]{1,0:T(8,128)S(1)} %get-tuple-element.48), channel_id=1, source_target_pairs={{64,0},{128,64},{192,128},{65,1},{129,65},{193,129},{66,2},{130,66... | collective-permute-start | bytes 12296 | tf_op jit(solution)/shard_map/ppermute | solution.py:383
  136.8 20.9 %all-to-all-start.6 = ((f32[8,56,128]{2,1,0:T(8,128)}), f32[8,56,128]{2,1,0:T(8,128)S(1)}, u32[]{:S(2)}, u32[]{:S(2)}) async-start(f32[8,56,128]{2,1,0:T(8,128)} %shard_map.138), calls=%async_computation.6 | async-start | bytes 458752 | tf_op jit(solution)/shard_map/all_to_all | solution.py:401
  141.6 6.1 %collective-permute-start.10 = (f32[80,128]{1,0:T(8,128)S(1)}, f32[80,128]{1,0:T(8,128)S(1)}, u32[]{:S(2)}, u32[]{:S(2)}) collective-permute-start(f32[80,128]{1,0:T(8,128)S(1)} %get-tuple-element.50), channel_id=1, source_target_pairs={{0,1},{1,2},{2,3},{3,4},{4,5},{5,6},{6,7},{8,9},{9,10},{10,11},{11... | collective-permute-start | bytes 122888 | tf_op jit(solution)/shard_map/ppermute | solution.py:391
  145.8 11.9 %collective-permute-start.11 = (f32[80,128]{1,0:T(8,128)S(1)}, f32[80,128]{1,0:T(8,128)S(1)}, u32[]{:S(2)}, u32[]{:S(2)}) collective-permute-start(f32[80,128]{1,0:T(8,128)S(1)} %get-tuple-element.51), channel_id=1, source_target_pairs={{1,0},{2,1},{3,2},{4,3},{5,4},{6,5},{7,6},{9,8},{10,9},{11,10},{12... | collective-permute-start | bytes 122888 | tf_op jit(solution)/shard_map/ppermute | solution.py:392
  158.5 9.0 %collective-permute-start.12 = (f32[5,8,128]{2,1,0:T(8,128)S(1)}, f32[5,8,128]{2,1,0:T(8,128)S(1)}, u32[]{:S(2)}, u32[]{:S(2)}) collective-permute-start(f32[5,8,128]{2,1,0:T(8,128)S(1)} %get-tuple-element.54), channel_id=1, source_target_pairs={{0,64},{64,128},{128,192},{1,65},{65,129},{129,193},{2,66},{66,130... | collective-permute-start | bytes 61448 | tf_op jit(solution)/shard_map/ppermute | solution.py:382
  161.7 5.8 %collective-permute-start.13 = (f32[8,128]{1,0:T(8,128)S(1)}, f32[8,128]{1,0:T(8,128)S(1)}, u32[]{:S(2)}, u32[]{:S(2)}) collective-permute-start(f32[8,128]{1,0:T(8,128)S(1)} %get-tuple-element.55), channel_id=1, source_target_pairs={{64,0},{128,64},{192,128},{65,1},{129,65},{193,129},{66,2},{130,66... | collective-permute-start | bytes 12296 | tf_op jit(solution)/shard_map/ppermute | solution.py:383
  183.6 20.9 %all-to-all-start.8 = ((f32[8,56,128]{2,1,0:T(8,128)}), f32[8,56,128]{2,1,0:T(8,128)S(1)}, u32[]{:S(2)}, u32[]{:S(2)}) async-start(f32[8,56,128]{2,1,0:T(8,128)} %shard_map.142), calls=%async_computation.8 | async-start | bytes 458752 | tf_op jit(solution)/shard_map/all_to_all | solution.py:401
  188.4 6.1 %collective-permute-start.14 = (f32[80,128]{1,0:T(8,128)S(1)}, f32[80,128]{1,0:T(8,128)S(1)}, u32[]{:S(2)}, u32[]{:S(2)}) collective-permute-start(f32[80,128]{1,0:T(8,128)S(1)} %get-tuple-element.57), channel_id=1, source_target_pairs={{0,1},{1,2},{2,3},{3,4},{4,5},{5,6},{6,7},{8,9},{9,10},{10,11},{11... | collective-permute-start | bytes 122888 | tf_op jit(solution)/shard_map/ppermute | solution.py:391
  192.6 11.9 %collective-permute-start.15 = (f32[80,128]{1,0:T(8,128)S(1)}, f32[80,128]{1,0:T(8,128)S(1)}, u32[]{:S(2)}, u32[]{:S(2)}) collective-permute-start(f32[80,128]{1,0:T(8,128)S(1)} %get-tuple-element.58), channel_id=1, source_target_pairs={{1,0},{2,1},{3,2},{4,3},{5,4},{6,5},{7,6},{9,8},{10,9},{11,10},{12... | collective-permute-start | bytes 122888 | tf_op jit(solution)/shard_map/ppermute | solution.py:392
  (14 other events, 137.4 us)

commit v7 on v6

--- a/solution.py
+++ b/solution.py
@@ -82,14 +82,14 @@
 
 
 def first_kernel(ids, weight, down_donors, up_donors, *refs):
-    sources, (down, up, out_pressure, send, to_above, to_below), targets, sems = refs[:5], refs[5:11], refs[11:16], refs[16]
+    sources, (beside, out_pressure, send, first_swap, second_swap), targets, sems = refs[:5], refs[5:10], refs[10:15], refs[15]
     fetch(sources, targets, sems)
     state, radial, circ, mu, outflow = targets
     lanes = lanes_of((8, 128))
     row, size = ids[1], send.shape[0]
     for v in range(NV):
-        down[v] = state[v, PLANES - 1]
-    up[...] = pressure(weight, [state[v, 0] for v in range(NV)])
+        beside[v] = state[v, PLANES - 1]
+    beside[NV] = pressure(weight, [state[v, 0] for v in range(NV)])
     out_pressure[...] = pressure(weight, [outflow[v] for v in range(NV)])
     listed = jnp.zeros((8, 128), jnp.int32)
     for a in range(8):
@@ -99,9 +99,11 @@
     for j in range(size):
         send[j, 0:8, :] = listed
 
+    even = lax.rem(ids[2], 2) == 0
+
     def put(at, cell):
-        to_above[pl.ds(at, 1), :] = cell[7:8]
-        to_below[pl.ds(at, 1), :] = cell[0:1]
+        first_swap[pl.ds(at, 1), :] = jnp.where(even, cell[7:8], cell[0:1])
+        second_swap[pl.ds(at, 1), :] = jnp.where(even, cell[0:1], cell[7:8])
 
     def one(k, carry):
         last, first = carry
@@ -126,14 +128,15 @@
     send[lax.rem(row + size - 1, size), 8:16, :] = first
 
 
-def gather_kernel(ids, down, up, inflow, out_pressure, after, send):
+def gather_kernel(ids, one_way, other_way, inflow, out_pressure, after, send):
     section = ids[0]
+    odd = lax.rem(section, 2) == 1
     size = send.shape[0]
     for v in range(NV):
-        value = jnp.where(section == 0, inflow[v], down[v])
+        value = jnp.where(section == 0, inflow[v], jnp.where(odd, one_way[v], other_way[v]))
         for j in range(size):
             send[j, v * 8 : v * 8 + 8, :] = value
-    value = jnp.where(section == ids[4] - 1, out_pressure[...], up[...])
+    value = jnp.where(section == ids[4] - 1, out_pressure[...], jnp.where(odd, other_way[NV], one_way[NV]))
     for j in range(size):
         send[j, 40:48, :] = value
 
@@ -168,11 +171,18 @@
     return left, right
 
 
+def settle(ids, first_swap, second_swap, low, high):
+    even = lax.rem(ids[2], 2) == 0
+    low[...] = jnp.where(even, second_swap[...], first_swap[...])
+    high[...] = jnp.where(even, first_swap[...], second_swap[...])
+
+
 def beyond(ref, at):
     return jnp.broadcast_to(ref[pl.ds(at, 1), :], (ROWS, 128))
 
 
-def coef_kernel(ids, volume, axial, radial, circ, mu, around, low, high, coef):
+def coef_kernel(ids, volume, axial, radial, circ, mu, around, first_swap, second_swap, coef, low, high):
+    settle(ids, first_swap, second_swap, low, high)
     rad, rad_size = ids[2], ids[3]
     lanes = lanes_of((ROWS, 128))
     rows = rows_of((ROWS, 128))
@@ -269,16 +279,19 @@
     return new_inlet, new_outlet
 
 
-def ends_kernel(step, ids, wanted, weight, coupling, field, coef, matrix, across, around, low, high, ends, down, up, ghost):
+def ends_kernel(step, ids, wanted, weight, coupling, field, coef, matrix, across, around, first_swap, second_swap, ends, beside, ghost, low, high):
+    settle(ids, first_swap, second_swap, low, high)
     new_inlet, new_outlet = ends_of(step, ids, wanted, weight, coupling, field, coef, matrix, across, around, low, high, ghost)
     for v in range(NV):
         ends[0, v] = new_inlet[v]
         ends[1, v] = new_outlet[v]
-        down[v] = new_outlet[v]
-    up[...] = pressure(weight, new_inlet)
-
-
-def bulk_kernel(step, ids, field, coef, matrix, around, low, high, ends, new, edges, to_above, to_below):
+        beside[v] = new_outlet[v]
+    beside[NV] = pressure(weight, new_inlet)
+
+
+def bulk_kernel(step, ids, field, coef, matrix, around, from_first, from_second, ends, new, edges, first_swap, second_swap, low, high):
+    settle(ids, from_first, from_second, low, high)
+    even = lax.rem(ids[2], 2) == 0
     lanes = lanes_of((ROWS, 128))
     left, right = sides(step, ids, around)
 
@@ -286,8 +299,8 @@
         for v in range(NV):
             new[v, k] = total[v]
             at = v * 16 + k
-            to_above[pl.ds(at, 1), :] = total[v][7:8]
-            to_below[pl.ds(at, 1), :] = total[v][0:1]
+            first_swap[pl.ds(at, 1), :] = jnp.where(even, total[v][7:8], total[v][0:1])
+            second_swap[pl.ds(at, 1), :] = jnp.where(even, total[v][0:1], total[v][7:8])
             spot = lanes == at
             last = jnp.where(spot, roll(total[v], at + 1, 1), last)
             first = jnp.where(spot, roll(total[v], at, 1), first)
@@ -309,7 +322,8 @@
     edges[1] = first
 
 
-def last_kernel(step, ids, wanted, weight, coupling, field, coef, matrix, across, around, low, high, new, ghost):
+def last_kernel(step, ids, wanted, weight, coupling, field, coef, matrix, across, around, first_swap, second_swap, new, ghost, low, high):
+    settle(ids, first_swap, second_swap, low, high)
     lanes = lanes_of((ROWS, 128))
     left, right = sides(step, ids, around)
     new_inlet, new_outlet = ends_of(step, ids, wanted, weight, coupling, field, coef, matrix, across, around, low, high, ghost)
@@ -362,36 +376,37 @@
     sent = (FIELD_ROWS + 32, 128)
     scalars = [pressure_weight, boundary_coupling]
 
-    down, up, out_pressure, lists, to_above, to_below = call(
+    beside, out_pressure, lists, first_swap, second_swap = call(
         first_kernel,
-        [(NV, 8, 128), (8, 128), (8, 128), (row_size, 16, 128), sent, sent],
+        [(NV + 1, 8, 128), (8, 128), (row_size, 16, 128), sent, sent],
         [ids, pressure_weight, down_donors[0], up_donors[0]],
         [],
         far=[own[0], own[3], own[4], own[5], outflow_plane],
     )
-    forward = [(i, i + 1) for i in range(sections - 1)]
-    backward = [(i + 1, i) for i in range(sections - 1)]
-    outward = [(i, i + 1) for i in range(rad_size - 1)]
-    inward = [(i + 1, i) for i in range(rad_size - 1)]
+
+    def swaps(size, begin):
+        return [pair for i in range(begin, size - 1, 2) for pair in ((i, i + 1), (i + 1, i))]
+
     table = lax.all_to_all(lists, "row", 0, 0)
     wanted = table[:, 0, :16].astype(jnp.int32)
     field = own[0]
     coef = edges = None
     for step in range(STEPS):
         last_step = step == STEPS - 1
-        down = lax.ppermute(down, "sec", forward)
-        up = lax.ppermute(up, "sec", backward)
+        one_way = lax.ppermute(beside, "sec", swaps(sections, 0))
+        other_way = lax.ppermute(beside, "sec", swaps(sections, 1))
         (send,) = call(
             gather_kernel,
             [(rad_size, TILE_ROWS, 128)],
             [ids],
-            [down, up, inflow_plane, out_pressure, edges if step else table],
+            [one_way, other_way, inflow_plane, out_pressure, edges if step else table],
         )
         got = lax.all_to_all(send, "rad", 0, 0)
-        low = lax.ppermute(to_above, "rad", outward)
-        high = lax.ppermute(to_below, "rad", inward)
+        low = lax.ppermute(first_swap, "rad", swaps(rad_size, 0))
+        high = lax.ppermute(second_swap, "rad", swaps(rad_size, 1))
+        strip = [pltpu.VMEM(low.shape, jnp.float32)] * 2
         if step == 0:
-            (coef,) = call(coef_kernel, [(13, PLANES, ROWS, 128)], [ids], own[1:] + [table, low, high])
+            (coef,) = call(coef_kernel, [(13, PLANES, ROWS, 128)], [ids], own[1:] + [table, low, high], scratch=strip)
         (send,) = call(
             functools.partial(select_kernel, step),
             [(row_size, TILE_ROWS + (ROWS if step else 0), 128)],
@@ -408,22 +423,23 @@
                 [ids, wanted] + scalars,
                 [field, coef, matrix, across, around, low, high],
                 flops=PLANES * ROWS * 128 * 300,
-                scratch=ghost,
+                scratch=ghost + strip,
             )
         else:
-            ends, down, up = call(
+            ends, beside = call(
                 functools.partial(ends_kernel, step),
-                [(2, NV, ROWS, 128), (NV, 8, 128), (8, 128)],
+                [(2, NV, ROWS, 128), (NV + 1, 8, 128)],
                 [ids, wanted] + scalars,
                 [field, coef, matrix, across, around, low, high],
                 flops=2 * ROWS * 128 * 300,
-                scratch=ghost,
+                scratch=ghost + strip,
             )
-            field, edges, to_above, to_below = call(
+            field, edges, first_swap, second_swap = call(
                 functools.partial(bulk_kernel, step),
                 [extended, strips, (FIELD_ROWS, 128), (FIELD_ROWS, 128)],
                 [ids],
                 [field, coef, matrix, around, low, high, ends],
+                scratch=strip,
                 flops=PLANES * ROWS * 128 * 300,
             )
     return field[:, None]

time: 209 us -> 185 us (0.89)
  the two profiles are of different devices: /device:TPU:46 before, /device:TPU:14 now
where the time goes in v7:
time: 185 us; the launch traced here: 184 us
  starting transfers between devices  74.3 us (40%)
  waiting for transfers between devices  39.7 us (21%)
  blocking collectives  38.7 us (21%)
  Pallas kernels  29.8 us (16%)
    all_to_all x3, blocking collectives, body(): got = lax.all_to_all(send, 'rad', 0, 0)  38.7 us
    pallas_call x17, Pallas kernels, call(): pl.pallas_call(kernel, out_shape=[jax.ShapeDtypeStruct(o, jnp.float32) fo...  29.8 us
    ppermute x4, waiting for transfers between devices, body(): high = lax.ppermute(second_swap, 'rad', swaps(rad_size, 1))  29.3 us
    all_to_all x4, starting transfers between devices, body(): across = lax.all_to_all(send, 'row', 0, 0)  19.3 us
    ppermute x4, starting transfers between devices, body(): high = lax.ppermute(second_swap, 'rad', swaps(rad_size, 1))  18.4 us
    ppermute x4, starting transfers between devices, body(): one_way = lax.ppermute(beside, 'sec', swaps(sections, 0))  17.4 us
    all_to_all x1, starting transfers between devices, body(): got = lax.all_to_all(send, 'rad', 0, 0)  9.6 us
    all_to_all x1, waiting for transfers between devices, body(): got = lax.all_to_all(send, 'rad', 0, 0)  8.58 us
  transfers between devices with their start and end apart: 22, of which 6 were waited for; matrix products, arithmetic and copies ran while one was open for 0% of the time, Pallas kernels for 6%

profile of v7, /device:TPU:14, one launch (start us, length us, event | category | flops | bytes accessed | tf_op | source)
XLA Modules:
  0.0 184.4 jit_solution(11370417088897467408)
XLA Ops:
  0.6 3.9 %shard_map.127 = (f32[6,8,128]{2,1,0:T(8,128)}, f32[8,128]{1,0:T(8,128)}, f32[8,16,128]{2,1,0:T(8,128)}, f32[112,128]{1,0:T(8,128)}, f32[112,128]{1,0:T(8,128)}) custom-call(s32[6]{0:T(128)} %stack.15.ids, f32[5]{0:T(128)} %weight.9, s32[8]{0:T(128)} %bitcast.34, s32[8]{0:T(128)} %bitcast.35, f32[5,16,8,128]{3,2,1,0:T(8,128)} %bitcast.15, ...), custom_call_target="tpu_custom_call" | custom-call | bytes 208896 | tf_op jit(solution)/shard_map/pallas_call | solution.py:41
  4.6 4.9 %all-to-all-start = ((f32[8,16,128]{2,1,0:T(8,128)}), f32[8,16,128]{2,1,0:T(8,128)S(1)}, u32[]{:S(2)}, u32[]{:S(2)}) async-start(f32[8,16,128]{2,1,0:T(8,128)} %get-tuple-element.28), calls=%async_computation | async-start | bytes 131072 | tf_op jit(solution)/shard_map/all_to_all | solution.py:390
  10.2 5.2 %collective-permute-start.2 = (f32[6,8,128]{2,1,0:T(8,128)S(1)}, f32[6,8,128]{2,1,0:T(8,128)S(1)}, u32[]{:S(2)}, u32[]{:S(2)}) collective-permute-start(f32[6,8,128]{2,1,0:T(8,128)S(1)} %copy-done.14), channel_id=1, source_target_pairs={{0,64},{64,0},{128,192},{192,128},{1,65},{65,1},{129,193},{193,129... | collective-permute-start | bytes 73736 | tf_op jit(solution)/shard_map/ppermute | solution.py:396
  18.4 9.6 %all-to-all-start.1 = ((f32[8,48,128]{2,1,0:T(8,128)}), f32[8,48,128]{2,1,0:T(8,128)S(1)}, u32[]{:S(2)}, u32[]{:S(2)}) async-start(f32[8,48,128]{2,1,0:T(8,128)} %shard_map.129), calls=%async_computation.1 | async-start | bytes 393216 | tf_op jit(solution)/shard_map/all_to_all | solution.py:404
  28.0 8.6 %all-to-all-done.1.got = f32[8,48,128]{2,1,0:T(8,128)S(1)} async-done(((f32[8,48,128]{2,1,0:T(8,128)}), f32[8,48,128]{2,1,0:T(8,128)S(1)}, u32[]{:S(2)}, u32[]{:S(2)}) %all-to-all-start.1) | async-done | bytes 196640 | tf_op jit(solution)/shard_map/all_to_all | solution.py:404
  38.3 4.9 %all-to-all-start.2 = ((f32[8,48,128]{2,1,0:T(8,128)}), f32[8,48,128]{2,1,0:T(8,128)S(1)}, u32[]{:S(2)}, u32[]{:S(2)}) async-start(f32[8,48,128]{2,1,0:T(8,128)} %shard_map.130), calls=%async_computation.2 | async-start | bytes 393216 | tf_op jit(solution)/shard_map/all_to_all | solution.py:416
  43.8 4.5 %collective-permute-start.1 = (f32[112,128]{1,0:T(8,128)S(1)}, f32[112,128]{1,0:T(8,128)S(1)}, u32[]{:S(2)}, u32[]{:S(2)}) collective-permute-start(f32[112,128]{1,0:T(8,128)S(1)} %copy-done.12), channel_id=1, source_target_pairs={{1,2},{2,1},{3,4},{4,3},{5,6},{6,5},{9,10},{10,9},{11,12},{12,11},... | collective-permute-start | bytes 172040 | tf_op jit(solution)/shard_map/ppermute | solution.py:406
  48.4 7.5 %collective-permute-done.1.second_swap.from_second = f32[112,128]{1,0:T(8,128)S(1)} collective-permute-done((f32[112,128]{1,0:T(8,128)S(1)}, f32[112,128]{1,0:T(8,128)S(1)}, u32[]{:S(2)}, u32[]{:S(2)}) %collective-permute-start.1) | collective-permute-done | bytes 57376 | tf_op jit(solution)/shard_map/ppermute | solution.py:406
  60.0 5.2 %collective-permute-start.4 = (f32[6,8,128]{2,1,0:T(8,128)S(1)}, f32[6,8,128]{2,1,0:T(8,128)S(1)}, u32[]{:S(2)}, u32[]{:S(2)}) collective-permute-start(f32[6,8,128]{2,1,0:T(8,128)S(1)} %get-tuple-element.35), channel_id=1, source_target_pairs={{0,64},{64,0},{128,192},{192,128},{1,65},{65,1},{129,193},{193,129... | collective-permute-start | bytes 73736 | tf_op jit(solution)/shard_map/ppermute | solution.py:396
  65.2 3.1 %shard_map.132 = (f32[5,16,8,128]{3,2,1,0:T(8,128)S(1)}, f32[2,8,128]{2,1,0:T(8,128)S(1)}, f32[80,128]{1,0:T(8,128)S(1)}, f32[80,128]{1,0:T(8,128)S(1)}) custom-call(s32[6]{0:T(128)S(1)} %copy-done.5, f32[5,16,8,128]{3,2,1,0:T(8,128)S(1)} %bitcast.17, f32[13,16,8,128]{3,2,1,0:T(8,128)S(1)} %shard_map.128.coef, f32[80,128]{1,0:T(8,128)S(1)} %broadcast_in_dim.4.matrix, ...), custom_call_target="tpu_custom_call" | custom-call | flops 4915200 | bytes 1859584 | tf_op jit(solution)/shard_map/pallas_call | solution.py:41
  68.9 12.8 %all_to_all.45.got = f32[8,48,128]{2,1,0:T(8,128)S(1)} all-to-all(f32[8,48,128]{2,1,0:T(8,128)S(1)} %shard_map.133), channel_id=1, replica_groups=mesh['sec'=4,'row'=8,'rad'=8] {'rad'}, dimensions={0} | all-to-all | bytes 393216 | tf_op jit(solution)/shard_map/all_to_all | solution.py:404
  83.4 4.8 %all-to-all-start.4 = ((f32[8,56,128]{2,1,0:T(8,128)}), f32[8,56,128]{2,1,0:T(8,128)S(1)}, u32[]{:S(2)}, u32[]{:S(2)}) async-start(f32[8,56,128]{2,1,0:T(8,128)} %shard_map.134), calls=%async_computation.4 | async-start | bytes 458752 | tf_op jit(solution)/shard_map/all_to_all | solution.py:416
  88.7 4.6 %collective-permute-start.7 = (f32[80,128]{1,0:T(8,128)S(1)}, f32[80,128]{1,0:T(8,128)S(1)}, u32[]{:S(2)}, u32[]{:S(2)}) collective-permute-start(f32[80,128]{1,0:T(8,128)S(1)} %get-tuple-element.38), channel_id=1, source_target_pairs={{1,2},{2,1},{3,4},{4,3},{5,6},{6,5},{9,10},{10,9},{11,12},{12,11},... | collective-permute-start | bytes 122888 | tf_op jit(solution)/shard_map/ppermute | solution.py:406
  93.3 7.3 %collective-permute-done.7.second_swap.from_second = f32[80,128]{1,0:T(8,128)S(1)} collective-permute-done((f32[80,128]{1,0:T(8,128)S(1)}, f32[80,128]{1,0:T(8,128)S(1)}, u32[]{:S(2)}, u32[]{:S(2)}) %collective-permute-start.7) | collective-permute-done | bytes 40992 | tf_op jit(solution)/shard_map/ppermute | solution.py:406
  102.0 3.5 %collective-permute-start.8 = (f32[6,8,128]{2,1,0:T(8,128)S(1)}, f32[6,8,128]{2,1,0:T(8,128)S(1)}, u32[]{:S(2)}, u32[]{:S(2)}) collective-permute-start(f32[6,8,128]{2,1,0:T(8,128)S(1)} %get-tuple-element.41), channel_id=1, source_target_pairs={{0,64},{64,0},{128,192},{192,128},{1,65},{65,1},{129,193},{193,129... | collective-permute-start | bytes 73736 | tf_op jit(solution)/shard_map/ppermute | solution.py:396
  109.2 12.9 %all_to_all.46.got = f32[8,48,128]{2,1,0:T(8,128)S(1)} all-to-all(f32[8,48,128]{2,1,0:T(8,128)S(1)} %shard_map.137), channel_id=1, replica_groups=mesh['sec'=4,'row'=8,'rad'=8] {'rad'}, dimensions={0} | all-to-all | bytes 393216 | tf_op jit(solution)/shard_map/all_to_all | solution.py:404
  123.8 4.8 %all-to-all-start.6 = ((f32[8,56,128]{2,1,0:T(8,128)}), f32[8,56,128]{2,1,0:T(8,128)S(1)}, u32[]{:S(2)}, u32[]{:S(2)}) async-start(f32[8,56,128]{2,1,0:T(8,128)} %shard_map.138), calls=%async_computation.6 | async-start | bytes 458752 | tf_op jit(solution)/shard_map/all_to_all | solution.py:416
  129.1 4.7 %collective-permute-start.11 = (f32[80,128]{1,0:T(8,128)S(1)}, f32[80,128]{1,0:T(8,128)S(1)}, u32[]{:S(2)}, u32[]{:S(2)}) collective-permute-start(f32[80,128]{1,0:T(8,128)S(1)} %get-tuple-element.44), channel_id=1, source_target_pairs={{1,2},{2,1},{3,4},{4,3},{5,6},{6,5},{9,10},{10,9},{11,12},{12,11},... | collective-permute-start | bytes 122888 | tf_op jit(solution)/shard_map/ppermute | solution.py:406
  133.8 7.2 %collective-permute-done.11.second_swap.from_second = f32[80,128]{1,0:T(8,128)S(1)} collective-permute-done((f32[80,128]{1,0:T(8,128)S(1)}, f32[80,128]{1,0:T(8,128)S(1)}, u32[]{:S(2)}, u32[]{:S(2)}) %collective-permute-start.11) | collective-permute-done | bytes 40992 | tf_op jit(solution)/shard_map/ppermute | solution.py:406
  142.4 3.5 %collective-permute-start.12 = (f32[6,8,128]{2,1,0:T(8,128)S(1)}, f32[6,8,128]{2,1,0:T(8,128)S(1)}, u32[]{:S(2)}, u32[]{:S(2)}) collective-permute-start(f32[6,8,128]{2,1,0:T(8,128)S(1)} %get-tuple-element.47), channel_id=1, source_target_pairs={{0,64},{64,0},{128,192},{192,128},{1,65},{65,1},{129,193},{193,129... | collective-permute-start | bytes 73736 | tf_op jit(solution)/shard_map/ppermute | solution.py:396
  149.6 12.9 %all_to_all.47.got = f32[8,48,128]{2,1,0:T(8,128)S(1)} all-to-all(f32[8,48,128]{2,1,0:T(8,128)S(1)} %shard_map.141), channel_id=1, replica_groups=mesh['sec'=4,'row'=8,'rad'=8] {'rad'}, dimensions={0} | all-to-all | bytes 393216 | tf_op jit(solution)/shard_map/all_to_all | solution.py:404
  164.3 4.8 %all-to-all-start.8 = ((f32[8,56,128]{2,1,0:T(8,128)}), f32[8,56,128]{2,1,0:T(8,128)S(1)}, u32[]{:S(2)}, u32[]{:S(2)}) async-start(f32[8,56,128]{2,1,0:T(8,128)} %shard_map.142), calls=%async_computation.8 | async-start | bytes 458752 | tf_op jit(solution)/shard_map/all_to_all | solution.py:416
  169.5 4.7 %collective-permute-start.15 = (f32[80,128]{1,0:T(8,128)S(1)}, f32[80,128]{1,0:T(8,128)S(1)}, u32[]{:S(2)}, u32[]{:S(2)}) collective-permute-start(f32[80,128]{1,0:T(8,128)S(1)} %get-tuple-element.50), channel_id=1, source_target_pairs={{1,2},{2,1},{3,4},{4,3},{5,6},{6,5},{9,10},{10,9},{11,12},{12,11},... | collective-permute-start | bytes 122888 | tf_op jit(solution)/shard_map/ppermute | solution.py:406
  174.2 7.2 %collective-permute-done.15.second_swap = f32[80,128]{1,0:T(8,128)S(1)} collective-permute-done((f32[80,128]{1,0:T(8,128)S(1)}, f32[80,128]{1,0:T(8,128)S(1)}, u32[]{:S(2)}, u32[]{:S(2)}) %collective-permute-start.15) | collective-permute-done | bytes 40992 | tf_op jit(solution)/shard_map/ppermute | solution.py:406
  (76 shorter events, 30.8 us)
Async XLA Ops:
  4.6 12.6 %all-to-all-start = ((f32[8,16,128]{2,1,0:T(8,128)}), f32[8,16,128]{2,1,0:T(8,128)S(1)}, u32[]{:S(2)}, u32[]{:S(2)}) async-start(f32[8,16,128]{2,1,0:T(8,128)} %get-tuple-element.28), calls=%async_computation | async-start | bytes 131072 | tf_op jit(solution)/shard_map/all_to_all | solution.py:390
  9.5 5.8 %collective-permute-start.3 = (f32[6,8,128]{2,1,0:T(8,128)S(1)}, f32[6,8,128]{2,1,0:T(8,128)S(1)}, u32[]{:S(2)}, u32[]{:S(2)}) collective-permute-start(f32[6,8,128]{2,1,0:T(8,128)S(1)} %copy-done.14), channel_id=1, source_target_pairs={{64,128},{128,64},{65,129},{129,65},{66,130},{130,66},{67,131},{13... | collective-permute-start | bytes 73736 | tf_op jit(solution)/shard_map/ppermute | solution.py:397
  10.2 7.0 %collective-permute-start.2 = (f32[6,8,128]{2,1,0:T(8,128)S(1)}, f32[6,8,128]{2,1,0:T(8,128)S(1)}, u32[]{:S(2)}, u32[]{:S(2)}) collective-permute-start(f32[6,8,128]{2,1,0:T(8,128)S(1)} %copy-done.14), channel_id=1, source_target_pairs={{0,64},{64,0},{128,192},{192,128},{1,65},{65,1},{129,193},{193,129... | collective-permute-start | bytes 73736 | tf_op jit(solution)/shard_map/ppermute | solution.py:396
  18.4 18.2 %all-to-all-start.1 = ((f32[8,48,128]{2,1,0:T(8,128)}), f32[8,48,128]{2,1,0:T(8,128)S(1)}, u32[]{:S(2)}, u32[]{:S(2)}) async-start(f32[8,48,128]{2,1,0:T(8,128)} %shard_map.129), calls=%async_computation.1 | async-start | bytes 393216 | tf_op jit(solution)/shard_map/all_to_all | solution.py:404
  38.2 17.7 %copy-start.2 = (f32[1,16,8,128]{3,2,1,0:T(8,128)S(1)}, f32[1,16,8,128]{3,2,1,0:T(8,128)}, u32[]{:S(2)}) copy-start(f32[1,16,8,128]{3,2,1,0:T(8,128)} %param.16) | copy-start | bytes 196612
  38.3 17.7 %copy-start.3 = (f32[1,16,8,128]{3,2,1,0:T(8,128)S(1)}, f32[1,16,8,128]{3,2,1,0:T(8,128)}, u32[]{:S(2)}) copy-start(f32[1,16,8,128]{3,2,1,0:T(8,128)} %param.17) | copy-start | bytes 196612
  38.3 19.6 %all-to-all-start.2 = ((f32[8,48,128]{2,1,0:T(8,128)}), f32[8,48,128]{2,1,0:T(8,128)S(1)}, u32[]{:S(2)}, u32[]{:S(2)}) async-start(f32[8,48,128]{2,1,0:T(8,128)} %shard_map.130), calls=%async_computation.2 | async-start | bytes 393216 | tf_op jit(solution)/shard_map/all_to_all | solution.py:416
  43.2 5.2 %collective-permute-start = (f32[112,128]{1,0:T(8,128)S(1)}, f32[112,128]{1,0:T(8,128)S(1)}, u32[]{:S(2)}, u32[]{:S(2)}) collective-permute-start(f32[112,128]{1,0:T(8,128)S(1)} %copy-done.13), channel_id=1, source_target_pairs={{0,1},{1,0},{2,3},{3,2},{4,5},{5,4},{6,7},{7,6},{8,9},{9,8},{10,11... | collective-permute-start | bytes 172040 | tf_op jit(solution)/shard_map/ppermute | solution.py:405
  43.8 12.2 %collective-permute-start.1 = (f32[112,128]{1,0:T(8,128)S(1)}, f32[112,128]{1,0:T(8,128)S(1)}, u32[]{:S(2)}, u32[]{:S(2)}) collective-permute-start(f32[112,128]{1,0:T(8,128)S(1)} %copy-done.12), channel_id=1, source_target_pairs={{1,2},{2,1},{3,4},{4,3},{5,6},{6,5},{9,10},{10,9},{11,12},{12,11},... | collective-permute-start | bytes 172040 | tf_op jit(solution)/shard_map/ppermute | solution.py:406
  59.3 9.0 %collective-permute-start.5 = (f32[6,8,128]{2,1,0:T(8,128)S(1)}, f32[6,8,128]{2,1,0:T(8,128)S(1)}, u32[]{:S(2)}, u32[]{:S(2)}) collective-permute-start(f32[6,8,128]{2,1,0:T(8,128)S(1)} %get-tuple-element.35), channel_id=1, source_target_pairs={{64,128},{128,64},{65,129},{129,65},{66,130},{130,66},{67,131},{13... | collective-permute-start | bytes 73736 | tf_op jit(solution)/shard_map/ppermute | solution.py:397
  60.0 8.3 %collective-permute-start.4 = (f32[6,8,128]{2,1,0:T(8,128)S(1)}, f32[6,8,128]{2,1,0:T(8,128)S(1)}, u32[]{:S(2)}, u32[]{:S(2)}) collective-permute-start(f32[6,8,128]{2,1,0:T(8,128)S(1)} %get-tuple-element.35), channel_id=1, source_target_pairs={{0,64},{64,0},{128,192},{192,128},{1,65},{65,1},{129,193},{193,129... | collective-permute-start | bytes 73736 | tf_op jit(solution)/shard_map/ppermute | solution.py:396
  83.4 17.2 %all-to-all-start.4 = ((f32[8,56,128]{2,1,0:T(8,128)}), f32[8,56,128]{2,1,0:T(8,128)S(1)}, u32[]{:S(2)}, u32[]{:S(2)}) async-start(f32[8,56,128]{2,1,0:T(8,128)} %shard_map.134), calls=%async_computation.4 | async-start | bytes 458752 | tf_op jit(solution)/shard_map/all_to_all | solution.py:416
  88.2 5.1 %collective-permute-start.6 = (f32[80,128]{1,0:T(8,128)S(1)}, f32[80,128]{1,0:T(8,128)S(1)}, u32[]{:S(2)}, u32[]{:S(2)}) collective-permute-start(f32[80,128]{1,0:T(8,128)S(1)} %get-tuple-element.37), channel_id=1, source_target_pairs={{0,1},{1,0},{2,3},{3,2},{4,5},{5,4},{6,7},{7,6},{8,9},{9,8},{10,11... | collective-permute-start | bytes 122888 | tf_op jit(solution)/shard_map/ppermute | solution.py:405
  88.7 11.9 %collective-permute-start.7 = (f32[80,128]{1,0:T(8,128)S(1)}, f32[80,128]{1,0:T(8,128)S(1)}, u32[]{:S(2)}, u32[]{:S(2)}) collective-permute-start(f32[80,128]{1,0:T(8,128)S(1)} %get-tuple-element.38), channel_id=1, source_target_pairs={{1,2},{2,1},{3,4},{4,3},{5,6},{6,5},{9,10},{10,9},{11,12},{12,11},... | collective-permute-start | bytes 122888 | tf_op jit(solution)/shard_map/ppermute | solution.py:406
  101.4 7.3 %collective-permute-start.9 = (f32[6,8,128]{2,1,0:T(8,128)S(1)}, f32[6,8,128]{2,1,0:T(8,128)S(1)}, u32[]{:S(2)}, u32[]{:S(2)}) collective-permute-start(f32[6,8,128]{2,1,0:T(8,128)S(1)} %get-tuple-element.41), channel_id=1, source_target_pairs={{64,128},{128,64},{65,129},{129,65},{66,130},{130,66},{67,131},{13... | collective-permute-start | bytes 73736 | tf_op jit(solution)/shard_map/ppermute | solution.py:397
  102.0 6.6 %collective-permute-start.8 = (f32[6,8,128]{2,1,0:T(8,128)S(1)}, f32[6,8,128]{2,1,0:T(8,128)S(1)}, u32[]{:S(2)}, u32[]{:S(2)}) collective-permute-start(f32[6,8,128]{2,1,0:T(8,128)S(1)} %get-tuple-element.41), channel_id=1, source_target_pairs={{0,64},{64,0},{128,192},{192,128},{1,65},{65,1},{129,193},{193,129... | collective-permute-start | bytes 73736 | tf_op jit(solution)/shard_map/ppermute | solution.py:396
  123.8 17.2 %all-to-all-start.6 = ((f32[8,56,128]{2,1,0:T(8,128)}), f32[8,56,128]{2,1,0:T(8,128)S(1)}, u32[]{:S(2)}, u32[]{:S(2)}) async-start(f32[8,56,128]{2,1,0:T(8,128)} %shard_map.138), calls=%async_computation.6 | async-start | bytes 458752 | tf_op jit(solution)/shard_map/all_to_all | solution.py:416
  128.6 5.2 %collective-permute-start.10 = (f32[80,128]{1,0:T(8,128)S(1)}, f32[80,128]{1,0:T(8,128)S(1)}, u32[]{:S(2)}, u32[]{:S(2)}) collective-permute-start(f32[80,128]{1,0:T(8,128)S(1)} %get-tuple-element.43), channel_id=1, source_target_pairs={{0,1},{1,0},{2,3},{3,2},{4,5},{5,4},{6,7},{7,6},{8,9},{9,8},{10,11... | collective-permute-start | bytes 122888 | tf_op jit(solution)/shard_map/ppermute | solution.py:405
  129.1 11.9 %collective-permute-start.11 = (f32[80,128]{1,0:T(8,128)S(1)}, f32[80,128]{1,0:T(8,128)S(1)}, u32[]{:S(2)}, u32[]{:S(2)}) collective-permute-start(f32[80,128]{1,0:T(8,128)S(1)} %get-tuple-element.44), channel_id=1, source_target_pairs={{1,2},{2,1},{3,4},{4,3},{5,6},{6,5},{9,10},{10,9},{11,12},{12,11},... | collective-permute-start | bytes 122888 | tf_op jit(solution)/shard_map/ppermute | solution.py:406
  141.8 7.3 %collective-permute-start.13 = (f32[6,8,128]{2,1,0:T(8,128)S(1)}, f32[6,8,128]{2,1,0:T(8,128)S(1)}, u32[]{:S(2)}, u32[]{:S(2)}) collective-permute-start(f32[6,8,128]{2,1,0:T(8,128)S(1)} %get-tuple-element.47), channel_id=1, source_target_pairs={{64,128},{128,64},{65,129},{129,65},{66,130},{130,66},{67,131},{13... | collective-permute-start | bytes 73736 | tf_op jit(solution)/shard_map/ppermute | solution.py:397
  142.4 6.6 %collective-permute-start.12 = (f32[6,8,128]{2,1,0:T(8,128)S(1)}, f32[6,8,128]{2,1,0:T(8,128)S(1)}, u32[]{:S(2)}, u32[]{:S(2)}) collective-permute-start(f32[6,8,128]{2,1,0:T(8,128)S(1)} %get-tuple-element.47), channel_id=1, source_target_pairs={{0,64},{64,0},{128,192},{192,128},{1,65},{65,1},{129,193},{193,129... | collective-permute-start | bytes 73736 | tf_op jit(solution)/shard_map/ppermute | solution.py:396
  164.3 17.2 %all-to-all-start.8 = ((f32[8,56,128]{2,1,0:T(8,128)}), f32[8,56,128]{2,1,0:T(8,128)S(1)}, u32[]{:S(2)}, u32[]{:S(2)}) async-start(f32[8,56,128]{2,1,0:T(8,128)} %shard_map.142), calls=%async_computation.8 | async-start | bytes 458752 | tf_op jit(solution)/shard_map/all_to_all | solution.py:416
  169.1 5.2 %collective-permute-start.14 = (f32[80,128]{1,0:T(8,128)S(1)}, f32[80,128]{1,0:T(8,128)S(1)}, u32[]{:S(2)}, u32[]{:S(2)}) collective-permute-start(f32[80,128]{1,0:T(8,128)S(1)} %get-tuple-element.49), channel_id=1, source_target_pairs={{0,1},{1,0},{2,3},{3,2},{4,5},{5,4},{6,7},{7,6},{8,9},{9,8},{10,11... | collective-permute-start | bytes 122888 | tf_op jit(solution)/shard_map/ppermute | solution.py:405
  169.5 11.9 %collective-permute-start.15 = (f32[80,128]{1,0:T(8,128)S(1)}, f32[80,128]{1,0:T(8,128)S(1)}, u32[]{:S(2)}, u32[]{:S(2)}) collective-permute-start(f32[80,128]{1,0:T(8,128)S(1)} %get-tuple-element.50), channel_id=1, source_target_pairs={{1,2},{2,1},{3,4},{4,3},{5,6},{6,5},{9,10},{10,9},{11,12},{12,11},... | collective-permute-start | bytes 122888 | tf_op jit(solution)/shard_map/ppermute | solution.py:406
  (13 other events, 116.5 us)

commit v8 on v7

--- a/solution.py
+++ b/solution.py
@@ -81,15 +81,24 @@
         copy.wait()
 
 
+def beside_kernel(weight, state_hbm, beside, inlet, sem):
+    copies = [
+        pltpu.make_async_copy(state_hbm.at[:, PLANES - 1], beside.at[pl.ds(0, NV)], sem.at[0]),
+        pltpu.make_async_copy(state_hbm.at[:, 0], inlet, sem.at[1]),
+    ]
+    for copy in copies:
+        copy.start()
+    for copy in copies:
+        copy.wait()
+    beside[NV] = pressure(weight, [inlet[v] for v in range(NV)])
+
+
 def first_kernel(ids, weight, down_donors, up_donors, *refs):
-    sources, (beside, out_pressure, send, first_swap, second_swap), targets, sems = refs[:5], refs[5:10], refs[10:15], refs[15]
+    sources, (out_pressure, send, first_swap, second_swap), targets, sems = refs[:5], refs[5:9], refs[9:14], refs[14]
     fetch(sources, targets, sems)
     state, radial, circ, mu, outflow = targets
     lanes = lanes_of((8, 128))
     row, size = ids[1], send.shape[0]
-    for v in range(NV):
-        beside[v] = state[v, PLANES - 1]
-    beside[NV] = pressure(weight, [state[v, 0] for v in range(NV)])
     out_pressure[...] = pressure(weight, [outflow[v] for v in range(NV)])
     listed = jnp.zeros((8, 128), jnp.int32)
     for a in range(8):
@@ -376,9 +385,19 @@
     sent = (FIELD_ROWS + 32, 128)
     scalars = [pressure_weight, boundary_coupling]
 
-    beside, out_pressure, lists, first_swap, second_swap = call(
+    beside = pl.pallas_call(
+        beside_kernel,
+        out_shape=jax.ShapeDtypeStruct((NV + 1, 8, 128), jnp.float32),
+        in_specs=[smem(), hbm()],
+        out_specs=vmem(),
+        scratch_shapes=[pltpu.VMEM((NV, 8, 128), jnp.float32), pltpu.SemaphoreType.DMA((2,))],
+        name="beside",
+        compiler_params=pltpu.CompilerParams(vmem_limit_bytes=FAR_LIMIT),
+        interpret=INTERPRET,
+    )(pressure_weight, own[0])
+    out_pressure, lists, first_swap, second_swap = call(
         first_kernel,
-        [(NV + 1, 8, 128), (8, 128), (row_size, 16, 128), sent, sent],
+        [(8, 128), (row_size, 16, 128), sent, sent],
         [ids, pressure_weight, down_donors[0], up_donors[0]],
         [],
         far=[own[0], own[3], own[4], own[5], outflow_plane],
@@ -402,8 +421,8 @@
             [one_way, other_way, inflow_plane, out_pressure, edges if step else table],
         )
         got = lax.all_to_all(send, "rad", 0, 0)
+        high = lax.ppermute(second_swap, "rad", swaps(rad_size, 1))
         low = lax.ppermute(first_swap, "rad", swaps(rad_size, 0))
-        high = lax.ppermute(second_swap, "rad", swaps(rad_size, 1))
         strip = [pltpu.VMEM(low.shape, jnp.float32)] * 2
         if step == 0:
             (coef,) = call(coef_kernel, [(13, PLANES, ROWS, 128)], [ids], own[1:] + [table, low, high], scratch=strip)

time: 185 us -> 188 us (1.016)
  Pallas kernels: 29.8 us -> 32 us
    pallas_call x0 -> x1, Pallas kernels: none -> 2.17 us  [body(): pl.pallas_call(beside_kernel, out_shape=jax.ShapeDtypeStruct((NV + 1, 8,...]
  transfers between devices with their start and end apart: 22 -> 22, of which waited for: 6 -> 6; matrix products, arithmetic and copies ran while one was open for 0% -> 0% of each run, Pallas kernels for 6% -> 7%
where the time goes in v8:
time: 188 us; the launch traced here: 187 us
  starting transfers between devices  74.3 us (40%)
  waiting for transfers between devices  39.9 us (21%)
  blocking collectives  38.7 us (21%)
  Pallas kernels  32 us (17%)
    all_to_all x3, blocking collectives, body(): got = lax.all_to_all(send, 'rad', 0, 0)  38.7 us
    pallas_call x17, Pallas kernels, call(): pl.pallas_call(kernel, out_shape=[jax.ShapeDtypeStruct(o, jnp.float32) fo...  29.8 us
    ppermute x4, waiting for transfers between devices, body(): high = lax.ppermute(second_swap, 'rad', swaps(rad_size, 1))  29.3 us
    all_to_all x4, starting transfers between devices, body(): across = lax.all_to_all(send, 'row', 0, 0)  19.3 us
    ppermute x4, starting transfers between devices, body(): high = lax.ppermute(second_swap, 'rad', swaps(rad_size, 1))  18.4 us
    ppermute x4, starting transfers between devices, body(): one_way = lax.ppermute(beside, 'sec', swaps(sections, 0))  17.4 us
    all_to_all x1, starting transfers between devices, body(): got = lax.all_to_all(send, 'rad', 0, 0)  9.6 us
    all_to_all x1, waiting for transfers between devices, body(): got = lax.all_to_all(send, 'rad', 0, 0)  8.58 us
  transfers between devices with their start and end apart: 22, of which 6 were waited for; matrix products, arithmetic and copies ran while one was open for 0% of the time, Pallas kernels for 7%

profile of v8, /device:TPU:14, one launch (start us, length us, event | category | flops | bytes accessed | tf_op | source)
XLA Modules:
  0.0 186.8 jit_solution(12336891392050480046)
XLA Ops:
  0.7 3.9 %shard_map.127 = (f32[8,128]{1,0:T(8,128)}, f32[8,16,128]{2,1,0:T(8,128)}, f32[112,128]{1,0:T(8,128)}, f32[112,128]{1,0:T(8,128)}) custom-call(s32[6]{0:T(128)} %stack.15.ids, f32[5]{0:T(128)} %weight.11, s32[8]{0:T(128)} %bitcast.35, s32[8]{0:T(128)} %bitcast.36, f32[5,16,8,128]{3,2,1,0:T(8,128)} %bitcast.15, f32[16,8,128]{2,1,0:T(8,128)} %bitcast.27, ...), custom_call_target="tpu_custom_call" | custom-call | bytes 184320 | tf_op jit(solution)/shard_map/pallas_call | solution.py:41
  4.6 4.9 %all-to-all-start = ((f32[8,16,128]{2,1,0:T(8,128)}), f32[8,16,128]{2,1,0:T(8,128)S(1)}, u32[]{:S(2)}, u32[]{:S(2)}) async-start(f32[8,16,128]{2,1,0:T(8,128)} %get-tuple-element.27), calls=%async_computation | async-start | bytes 131072 | tf_op jit(solution)/shard_map/all_to_all | solution.py:409
  12.4 5.2 %collective-permute-start.2 = (f32[6,8,128]{2,1,0:T(8,128)}, f32[6,8,128]{2,1,0:T(8,128)S(1)}, u32[]{:S(2)}, u32[]{:S(2)}) collective-permute-start(f32[6,8,128]{2,1,0:T(8,128)} %beside.1), channel_id=1, source_target_pairs={{0,64},{64,0},{128,192},{192,128},{1,65},{65,1},{129,193},{193,129... | collective-permute-start | bytes 73736 | tf_op jit(solution)/shard_map/ppermute | solution.py:415
  20.8 9.6 %all-to-all-start.1 = ((f32[8,48,128]{2,1,0:T(8,128)}), f32[8,48,128]{2,1,0:T(8,128)S(1)}, u32[]{:S(2)}, u32[]{:S(2)}) async-start(f32[8,48,128]{2,1,0:T(8,128)} %shard_map.129), calls=%async_computation.1 | async-start | bytes 393216 | tf_op jit(solution)/shard_map/all_to_all | solution.py:423
  30.4 8.6 %all-to-all-done.1.got = f32[8,48,128]{2,1,0:T(8,128)S(1)} async-done(((f32[8,48,128]{2,1,0:T(8,128)}), f32[8,48,128]{2,1,0:T(8,128)S(1)}, u32[]{:S(2)}, u32[]{:S(2)}) %all-to-all-start.1) | async-done | bytes 196640 | tf_op jit(solution)/shard_map/all_to_all | solution.py:423
  40.7 4.9 %all-to-all-start.2 = ((f32[8,48,128]{2,1,0:T(8,128)}), f32[8,48,128]{2,1,0:T(8,128)S(1)}, u32[]{:S(2)}, u32[]{:S(2)}) async-start(f32[8,48,128]{2,1,0:T(8,128)} %shard_map.130), calls=%async_computation.2 | async-start | bytes 393216 | tf_op jit(solution)/shard_map/all_to_all | solution.py:435
  46.2 4.5 %collective-permute-start.1 = (f32[112,128]{1,0:T(8,128)S(1)}, f32[112,128]{1,0:T(8,128)S(1)}, u32[]{:S(2)}, u32[]{:S(2)}) collective-permute-start(f32[112,128]{1,0:T(8,128)S(1)} %copy-done.12), channel_id=1, source_target_pairs={{1,2},{2,1},{3,4},{4,3},{5,6},{6,5},{9,10},{10,9},{11,12},{12,11},... | collective-permute-start | bytes 172040 | tf_op jit(solution)/shard_map/ppermute | solution.py:424
  50.8 7.5 %collective-permute-done.1.second_swap.from_second = f32[112,128]{1,0:T(8,128)S(1)} collective-permute-done((f32[112,128]{1,0:T(8,128)S(1)}, f32[112,128]{1,0:T(8,128)S(1)}, u32[]{:S(2)}, u32[]{:S(2)}) %collective-permute-start.1) | collective-permute-done | bytes 57376 | tf_op jit(solution)/shard_map/ppermute | solution.py:424
  62.4 5.2 %collective-permute-start.4 = (f32[6,8,128]{2,1,0:T(8,128)S(1)}, f32[6,8,128]{2,1,0:T(8,128)S(1)}, u32[]{:S(2)}, u32[]{:S(2)}) collective-permute-start(f32[6,8,128]{2,1,0:T(8,128)S(1)} %get-tuple-element.33), channel_id=1, source_target_pairs={{0,64},{64,0},{128,192},{192,128},{1,65},{65,1},{129,193},{193,129... | collective-permute-start | bytes 73736 | tf_op jit(solution)/shard_map/ppermute | solution.py:415
  67.6 3.1 %shard_map.132 = (f32[5,16,8,128]{3,2,1,0:T(8,128)S(1)}, f32[2,8,128]{2,1,0:T(8,128)S(1)}, f32[80,128]{1,0:T(8,128)S(1)}, f32[80,128]{1,0:T(8,128)S(1)}) custom-call(s32[6]{0:T(128)S(1)} %copy-done.5, f32[5,16,8,128]{3,2,1,0:T(8,128)S(1)} %bitcast.18, f32[13,16,8,128]{3,2,1,0:T(8,128)S(1)} %shard_map.128.coef, f32[80,128]{1,0:T(8,128)S(1)} %broadcast_in_dim.4.matrix, ...), custom_call_target="tpu_custom_call" | custom-call | flops 4915200 | bytes 1859584 | tf_op jit(solution)/shard_map/pallas_call | solution.py:41
  71.3 12.8 %all_to_all.45.got = f32[8,48,128]{2,1,0:T(8,128)S(1)} all-to-all(f32[8,48,128]{2,1,0:T(8,128)S(1)} %shard_map.133), channel_id=1, replica_groups=mesh['sec'=4,'row'=8,'rad'=8] {'rad'}, dimensions={0} | all-to-all | bytes 393216 | tf_op jit(solution)/shard_map/all_to_all | solution.py:423
  85.8 4.8 %all-to-all-start.4 = ((f32[8,56,128]{2,1,0:T(8,128)}), f32[8,56,128]{2,1,0:T(8,128)S(1)}, u32[]{:S(2)}, u32[]{:S(2)}) async-start(f32[8,56,128]{2,1,0:T(8,128)} %shard_map.134), calls=%async_computation.4 | async-start | bytes 458752 | tf_op jit(solution)/shard_map/all_to_all | solution.py:435
  91.1 4.6 %collective-permute-start.7 = (f32[80,128]{1,0:T(8,128)S(1)}, f32[80,128]{1,0:T(8,128)S(1)}, u32[]{:S(2)}, u32[]{:S(2)}) collective-permute-start(f32[80,128]{1,0:T(8,128)S(1)} %get-tuple-element.36), channel_id=1, source_target_pairs={{1,2},{2,1},{3,4},{4,3},{5,6},{6,5},{9,10},{10,9},{11,12},{12,11},... | collective-permute-start | bytes 122888 | tf_op jit(solution)/shard_map/ppermute | solution.py:424
  95.7 7.3 %collective-permute-done.7.second_swap.from_second = f32[80,128]{1,0:T(8,128)S(1)} collective-permute-done((f32[80,128]{1,0:T(8,128)S(1)}, f32[80,128]{1,0:T(8,128)S(1)}, u32[]{:S(2)}, u32[]{:S(2)}) %collective-permute-start.7) | collective-permute-done | bytes 40992 | tf_op jit(solution)/shard_map/ppermute | solution.py:424
  104.4 3.5 %collective-permute-start.8 = (f32[6,8,128]{2,1,0:T(8,128)S(1)}, f32[6,8,128]{2,1,0:T(8,128)S(1)}, u32[]{:S(2)}, u32[]{:S(2)}) collective-permute-start(f32[6,8,128]{2,1,0:T(8,128)S(1)} %get-tuple-element.39), channel_id=1, source_target_pairs={{0,64},{64,0},{128,192},{192,128},{1,65},{65,1},{129,193},{193,129... | collective-permute-start | bytes 73736 | tf_op jit(solution)/shard_map/ppermute | solution.py:415
  111.6 12.9 %all_to_all.46.got = f32[8,48,128]{2,1,0:T(8,128)S(1)} all-to-all(f32[8,48,128]{2,1,0:T(8,128)S(1)} %shard_map.137), channel_id=1, replica_groups=mesh['sec'=4,'row'=8,'rad'=8] {'rad'}, dimensions={0} | all-to-all | bytes 393216 | tf_op jit(solution)/shard_map/all_to_all | solution.py:423
  126.2 4.8 %all-to-all-start.6 = ((f32[8,56,128]{2,1,0:T(8,128)}), f32[8,56,128]{2,1,0:T(8,128)S(1)}, u32[]{:S(2)}, u32[]{:S(2)}) async-start(f32[8,56,128]{2,1,0:T(8,128)} %shard_map.138), calls=%async_computation.6 | async-start | bytes 458752 | tf_op jit(solution)/shard_map/all_to_all | solution.py:435
  131.5 4.7 %collective-permute-start.11 = (f32[80,128]{1,0:T(8,128)S(1)}, f32[80,128]{1,0:T(8,128)S(1)}, u32[]{:S(2)}, u32[]{:S(2)}) collective-permute-start(f32[80,128]{1,0:T(8,128)S(1)} %get-tuple-element.42), channel_id=1, source_target_pairs={{1,2},{2,1},{3,4},{4,3},{5,6},{6,5},{9,10},{10,9},{11,12},{12,11},... | collective-permute-start | bytes 122888 | tf_op jit(solution)/shard_map/ppermute | solution.py:424
  136.2 7.2 %collective-permute-done.11.second_swap.from_second = f32[80,128]{1,0:T(8,128)S(1)} collective-permute-done((f32[80,128]{1,0:T(8,128)S(1)}, f32[80,128]{1,0:T(8,128)S(1)}, u32[]{:S(2)}, u32[]{:S(2)}) %collective-permute-start.11) | collective-permute-done | bytes 40992 | tf_op jit(solution)/shard_map/ppermute | solution.py:424
  144.9 3.5 %collective-permute-start.12 = (f32[6,8,128]{2,1,0:T(8,128)S(1)}, f32[6,8,128]{2,1,0:T(8,128)S(1)}, u32[]{:S(2)}, u32[]{:S(2)}) collective-permute-start(f32[6,8,128]{2,1,0:T(8,128)S(1)} %get-tuple-element.45), channel_id=1, source_target_pairs={{0,64},{64,0},{128,192},{192,128},{1,65},{65,1},{129,193},{193,129... | collective-permute-start | bytes 73736 | tf_op jit(solution)/shard_map/ppermute | solution.py:415
  152.0 12.9 %all_to_all.47.got = f32[8,48,128]{2,1,0:T(8,128)S(1)} all-to-all(f32[8,48,128]{2,1,0:T(8,128)S(1)} %shard_map.141), channel_id=1, replica_groups=mesh['sec'=4,'row'=8,'rad'=8] {'rad'}, dimensions={0} | all-to-all | bytes 393216 | tf_op jit(solution)/shard_map/all_to_all | solution.py:423
  166.7 4.8 %all-to-all-start.8 = ((f32[8,56,128]{2,1,0:T(8,128)}), f32[8,56,128]{2,1,0:T(8,128)S(1)}, u32[]{:S(2)}, u32[]{:S(2)}) async-start(f32[8,56,128]{2,1,0:T(8,128)} %shard_map.142), calls=%async_computation.8 | async-start | bytes 458752 | tf_op jit(solution)/shard_map/all_to_all | solution.py:435
  171.9 4.7 %collective-permute-start.15 = (f32[80,128]{1,0:T(8,128)S(1)}, f32[80,128]{1,0:T(8,128)S(1)}, u32[]{:S(2)}, u32[]{:S(2)}) collective-permute-start(f32[80,128]{1,0:T(8,128)S(1)} %get-tuple-element.48), channel_id=1, source_target_pairs={{1,2},{2,1},{3,4},{4,3},{5,6},{6,5},{9,10},{10,9},{11,12},{12,11},... | collective-permute-start | bytes 122888 | tf_op jit(solution)/shard_map/ppermute | solution.py:424
  176.6 7.2 %collective-permute-done.15.second_swap = f32[80,128]{1,0:T(8,128)S(1)} collective-permute-done((f32[80,128]{1,0:T(8,128)S(1)}, f32[80,128]{1,0:T(8,128)S(1)}, u32[]{:S(2)}, u32[]{:S(2)}) %collective-permute-start.15) | collective-permute-done | bytes 40992 | tf_op jit(solution)/shard_map/ppermute | solution.py:424
  (75 shorter events, 33.2 us)
Async XLA Ops:
  4.6 15.0 %all-to-all-start = ((f32[8,16,128]{2,1,0:T(8,128)}), f32[8,16,128]{2,1,0:T(8,128)S(1)}, u32[]{:S(2)}, u32[]{:S(2)}) async-start(f32[8,16,128]{2,1,0:T(8,128)} %get-tuple-element.27), calls=%async_computation | async-start | bytes 131072 | tf_op jit(solution)/shard_map/all_to_all | solution.py:409
  11.7 5.8 %collective-permute-start.3 = (f32[6,8,128]{2,1,0:T(8,128)}, f32[6,8,128]{2,1,0:T(8,128)S(1)}, u32[]{:S(2)}, u32[]{:S(2)}) collective-permute-start(f32[6,8,128]{2,1,0:T(8,128)} %beside.1), channel_id=1, source_target_pairs={{64,128},{128,64},{65,129},{129,65},{66,130},{130,66},{67,131},{13... | collective-permute-start | bytes 73736 | tf_op jit(solution)/shard_map/ppermute | solution.py:416
  12.4 7.2 %collective-permute-start.2 = (f32[6,8,128]{2,1,0:T(8,128)}, f32[6,8,128]{2,1,0:T(8,128)S(1)}, u32[]{:S(2)}, u32[]{:S(2)}) collective-permute-start(f32[6,8,128]{2,1,0:T(8,128)} %beside.1), channel_id=1, source_target_pairs={{0,64},{64,0},{128,192},{192,128},{1,65},{65,1},{129,193},{193,129... | collective-permute-start | bytes 73736 | tf_op jit(solution)/shard_map/ppermute | solution.py:415
  20.8 18.2 %all-to-all-start.1 = ((f32[8,48,128]{2,1,0:T(8,128)}), f32[8,48,128]{2,1,0:T(8,128)S(1)}, u32[]{:S(2)}, u32[]{:S(2)}) async-start(f32[8,48,128]{2,1,0:T(8,128)} %shard_map.129), calls=%async_computation.1 | async-start | bytes 393216 | tf_op jit(solution)/shard_map/all_to_all | solution.py:423
  40.7 17.7 %copy-start.2 = (f32[1,16,8,128]{3,2,1,0:T(8,128)S(1)}, f32[1,16,8,128]{3,2,1,0:T(8,128)}, u32[]{:S(2)}) copy-start(f32[1,16,8,128]{3,2,1,0:T(8,128)} %param.16) | copy-start | bytes 196612
  40.7 17.7 %copy-start.3 = (f32[1,16,8,128]{3,2,1,0:T(8,128)S(1)}, f32[1,16,8,128]{3,2,1,0:T(8,128)}, u32[]{:S(2)}) copy-start(f32[1,16,8,128]{3,2,1,0:T(8,128)} %param.17) | copy-start | bytes 196612
  40.7 19.6 %all-to-all-start.2 = ((f32[8,48,128]{2,1,0:T(8,128)}), f32[8,48,128]{2,1,0:T(8,128)S(1)}, u32[]{:S(2)}, u32[]{:S(2)}) async-start(f32[8,48,128]{2,1,0:T(8,128)} %shard_map.130), calls=%async_computation.2 | async-start | bytes 393216 | tf_op jit(solution)/shard_map/all_to_all | solution.py:435
  45.6 5.2 %collective-permute-start = (f32[112,128]{1,0:T(8,128)S(1)}, f32[112,128]{1,0:T(8,128)S(1)}, u32[]{:S(2)}, u32[]{:S(2)}) collective-permute-start(f32[112,128]{1,0:T(8,128)S(1)} %copy-done.13), channel_id=1, source_target_pairs={{0,1},{1,0},{2,3},{3,2},{4,5},{5,4},{6,7},{7,6},{8,9},{9,8},{10,11... | collective-permute-start | bytes 172040 | tf_op jit(solution)/shard_map/ppermute | solution.py:425
  46.2 12.2 %collective-permute-start.1 = (f32[112,128]{1,0:T(8,128)S(1)}, f32[112,128]{1,0:T(8,128)S(1)}, u32[]{:S(2)}, u32[]{:S(2)}) collective-permute-start(f32[112,128]{1,0:T(8,128)S(1)} %copy-done.12), channel_id=1, source_target_pairs={{1,2},{2,1},{3,4},{4,3},{5,6},{6,5},{9,10},{10,9},{11,12},{12,11},... | collective-permute-start | bytes 172040 | tf_op jit(solution)/shard_map/ppermute | solution.py:424
  61.7 9.0 %collective-permute-start.5 = (f32[6,8,128]{2,1,0:T(8,128)S(1)}, f32[6,8,128]{2,1,0:T(8,128)S(1)}, u32[]{:S(2)}, u32[]{:S(2)}) collective-permute-start(f32[6,8,128]{2,1,0:T(8,128)S(1)} %get-tuple-element.33), channel_id=1, source_target_pairs={{64,128},{128,64},{65,129},{129,65},{66,130},{130,66},{67,131},{13... | collective-permute-start | bytes 73736 | tf_op jit(solution)/shard_map/ppermute | solution.py:416
  62.4 8.3 %collective-permute-start.4 = (f32[6,8,128]{2,1,0:T(8,128)S(1)}, f32[6,8,128]{2,1,0:T(8,128)S(1)}, u32[]{:S(2)}, u32[]{:S(2)}) collective-permute-start(f32[6,8,128]{2,1,0:T(8,128)S(1)} %get-tuple-element.33), channel_id=1, source_target_pairs={{0,64},{64,0},{128,192},{192,128},{1,65},{65,1},{129,193},{193,129... | collective-permute-start | bytes 73736 | tf_op jit(solution)/shard_map/ppermute | solution.py:415
  85.8 17.2 %all-to-all-start.4 = ((f32[8,56,128]{2,1,0:T(8,128)}), f32[8,56,128]{2,1,0:T(8,128)S(1)}, u32[]{:S(2)}, u32[]{:S(2)}) async-start(f32[8,56,128]{2,1,0:T(8,128)} %shard_map.134), calls=%async_computation.4 | async-start | bytes 458752 | tf_op jit(solution)/shard_map/all_to_all | solution.py:435
  90.6 5.1 %collective-permute-start.6 = (f32[80,128]{1,0:T(8,128)S(1)}, f32[80,128]{1,0:T(8,128)S(1)}, u32[]{:S(2)}, u32[]{:S(2)}) collective-permute-start(f32[80,128]{1,0:T(8,128)S(1)} %get-tuple-element.35), channel_id=1, source_target_pairs={{0,1},{1,0},{2,3},{3,2},{4,5},{5,4},{6,7},{7,6},{8,9},{9,8},{10,11... | collective-permute-start | bytes 122888 | tf_op jit(solution)/shard_map/ppermute | solution.py:425
  91.1 11.9 %collective-permute-start.7 = (f32[80,128]{1,0:T(8,128)S(1)}, f32[80,128]{1,0:T(8,128)S(1)}, u32[]{:S(2)}, u32[]{:S(2)}) collective-permute-start(f32[80,128]{1,0:T(8,128)S(1)} %get-tuple-element.36), channel_id=1, source_target_pairs={{1,2},{2,1},{3,4},{4,3},{5,6},{6,5},{9,10},{10,9},{11,12},{12,11},... | collective-permute-start | bytes 122888 | tf_op jit(solution)/shard_map/ppermute | solution.py:424
  103.8 7.3 %collective-permute-start.9 = (f32[6,8,128]{2,1,0:T(8,128)S(1)}, f32[6,8,128]{2,1,0:T(8,128)S(1)}, u32[]{:S(2)}, u32[]{:S(2)}) collective-permute-start(f32[6,8,128]{2,1,0:T(8,128)S(1)} %get-tuple-element.39), channel_id=1, source_target_pairs={{64,128},{128,64},{65,129},{129,65},{66,130},{130,66},{67,131},{13... | collective-permute-start | bytes 73736 | tf_op jit(solution)/shard_map/ppermute | solution.py:416
  104.4 6.6 %collective-permute-start.8 = (f32[6,8,128]{2,1,0:T(8,128)S(1)}, f32[6,8,128]{2,1,0:T(8,128)S(1)}, u32[]{:S(2)}, u32[]{:S(2)}) collective-permute-start(f32[6,8,128]{2,1,0:T(8,128)S(1)} %get-tuple-element.39), channel_id=1, source_target_pairs={{0,64},{64,0},{128,192},{192,128},{1,65},{65,1},{129,193},{193,129... | collective-permute-start | bytes 73736 | tf_op jit(solution)/shard_map/ppermute | solution.py:415
  126.2 17.2 %all-to-all-start.6 = ((f32[8,56,128]{2,1,0:T(8,128)}), f32[8,56,128]{2,1,0:T(8,128)S(1)}, u32[]{:S(2)}, u32[]{:S(2)}) async-start(f32[8,56,128]{2,1,0:T(8,128)} %shard_map.138), calls=%async_computation.6 | async-start | bytes 458752 | tf_op jit(solution)/shard_map/all_to_all | solution.py:435
  131.0 5.2 %collective-permute-start.10 = (f32[80,128]{1,0:T(8,128)S(1)}, f32[80,128]{1,0:T(8,128)S(1)}, u32[]{:S(2)}, u32[]{:S(2)}) collective-permute-start(f32[80,128]{1,0:T(8,128)S(1)} %get-tuple-element.41), channel_id=1, source_target_pairs={{0,1},{1,0},{2,3},{3,2},{4,5},{5,4},{6,7},{7,6},{8,9},{9,8},{10,11... | collective-permute-start | bytes 122888 | tf_op jit(solution)/shard_map/ppermute | solution.py:425
  131.5 11.9 %collective-permute-start.11 = (f32[80,128]{1,0:T(8,128)S(1)}, f32[80,128]{1,0:T(8,128)S(1)}, u32[]{:S(2)}, u32[]{:S(2)}) collective-permute-start(f32[80,128]{1,0:T(8,128)S(1)} %get-tuple-element.42), channel_id=1, source_target_pairs={{1,2},{2,1},{3,4},{4,3},{5,6},{6,5},{9,10},{10,9},{11,12},{12,11},... | collective-permute-start | bytes 122888 | tf_op jit(solution)/shard_map/ppermute | solution.py:424
  144.2 7.3 %collective-permute-start.13 = (f32[6,8,128]{2,1,0:T(8,128)S(1)}, f32[6,8,128]{2,1,0:T(8,128)S(1)}, u32[]{:S(2)}, u32[]{:S(2)}) collective-permute-start(f32[6,8,128]{2,1,0:T(8,128)S(1)} %get-tuple-element.45), channel_id=1, source_target_pairs={{64,128},{128,64},{65,129},{129,65},{66,130},{130,66},{67,131},{13... | collective-permute-start | bytes 73736 | tf_op jit(solution)/shard_map/ppermute | solution.py:416
  144.9 6.6 %collective-permute-start.12 = (f32[6,8,128]{2,1,0:T(8,128)S(1)}, f32[6,8,128]{2,1,0:T(8,128)S(1)}, u32[]{:S(2)}, u32[]{:S(2)}) collective-permute-start(f32[6,8,128]{2,1,0:T(8,128)S(1)} %get-tuple-element.45), channel_id=1, source_target_pairs={{0,64},{64,0},{128,192},{192,128},{1,65},{65,1},{129,193},{193,129... | collective-permute-start | bytes 73736 | tf_op jit(solution)/shard_map/ppermute | solution.py:415
  166.7 17.2 %all-to-all-start.8 = ((f32[8,56,128]{2,1,0:T(8,128)}), f32[8,56,128]{2,1,0:T(8,128)S(1)}, u32[]{:S(2)}, u32[]{:S(2)}) async-start(f32[8,56,128]{2,1,0:T(8,128)} %shard_map.142), calls=%async_computation.8 | async-start | bytes 458752 | tf_op jit(solution)/shard_map/all_to_all | solution.py:435
  171.5 5.2 %collective-permute-start.14 = (f32[80,128]{1,0:T(8,128)S(1)}, f32[80,128]{1,0:T(8,128)S(1)}, u32[]{:S(2)}, u32[]{:S(2)}) collective-permute-start(f32[80,128]{1,0:T(8,128)S(1)} %get-tuple-element.47), channel_id=1, source_target_pairs={{0,1},{1,0},{2,3},{3,2},{4,5},{5,4},{6,7},{7,6},{8,9},{9,8},{10,11... | collective-permute-start | bytes 122888 | tf_op jit(solution)/shard_map/ppermute | solution.py:425
  171.9 11.9 %collective-permute-start.15 = (f32[80,128]{1,0:T(8,128)S(1)}, f32[80,128]{1,0:T(8,128)S(1)}, u32[]{:S(2)}, u32[]{:S(2)}) collective-permute-start(f32[80,128]{1,0:T(8,128)S(1)} %get-tuple-element.48), channel_id=1, source_target_pairs={{1,2},{2,1},{3,4},{4,3},{5,6},{6,5},{9,10},{10,9},{11,12},{12,11},... | collective-permute-start | bytes 122888 | tf_op jit(solution)/shard_map/ppermute | solution.py:424
  (12 other events, 106.6 us)

commit v9 on v7

--- a/solution.py
+++ b/solution.py
@@ -123,7 +123,7 @@
         return last, first
 
     zero = jnp.zeros((8, 128), jnp.float32)
-    last, first = lax.fori_loop(0, PLANES, one, (zero, zero))
+    last, first = lax.fori_loop(0, PLANES, one, (zero, zero), unroll=4)
     send[lax.rem(row + 1, size), 8:16, :] = last
     send[lax.rem(row + size - 1, size), 8:16, :] = first
 
@@ -156,7 +156,7 @@
             send[j, 40 + a : 41 + a, :] = got[e >> 3, pl.ds(40 + (e & 7), 1), :]
         return carry
 
-    lax.fori_loop(0, size, one, 0)
+    lax.fori_loop(0, size, one, 0, unroll=2)
     if step:
         edges = refs[0]
         send[lax.rem(row + 1, size), 48:56, :] = edges[0]
@@ -223,7 +223,7 @@
         coef[12, k] = 1.0 - total
         return carry
 
-    lax.fori_loop(0, PLANES, one, 0)
+    lax.fori_loop(0, PLANES, one, 0, unroll=4)
 
 
 def advance(k, before, here, after, coef, matrix, left, right, low, high):
@@ -317,7 +317,7 @@
     last, first = note(0, [ends[0, v] for v in range(NV)], zero, zero)
     last, first = note(PLANES - 1, [ends[1, v] for v in range(NV)], last, first)
     carry = ([field[v, 0] for v in range(NV)], [field[v, 1] for v in range(NV)], last, first)
-    _, _, last, first = lax.fori_loop(1, PLANES - 1, one, carry)
+    _, _, last, first = lax.fori_loop(1, PLANES - 1, one, carry, unroll=7)
     edges[0] = last
     edges[1] = first
 
@@ -340,7 +340,7 @@
         return here, after
 
     carry = ([field[v, 0] for v in range(NV)], [field[v, 1] for v in range(NV)])
-    lax.fori_loop(1, PLANES - 1, one, carry)
+    lax.fori_loop(1, PLANES - 1, one, carry, unroll=7)
 
 
 def body(
@@ -399,11 +399,11 @@
             gather_kernel,
             [(rad_size, TILE_ROWS, 128)],
             [ids],
-            [one_way, other_way, inflow_plane, out_pressure, edges if step else table],
+            [one_way, other_way, inflow_plane, out_pressure, edges if step else beside],
         )
         got = lax.all_to_all(send, "rad", 0, 0)
+        high = lax.ppermute(second_swap, "rad", swaps(rad_size, 1))
         low = lax.ppermute(first_swap, "rad", swaps(rad_size, 0))
-        high = lax.ppermute(second_swap, "rad", swaps(rad_size, 1))
         strip = [pltpu.VMEM(low.shape, jnp.float32)] * 2
         if step == 0:
             (coef,) = call(coef_kernel, [(13, PLANES, ROWS, 128)], [ids], own[1:] + [table, low, high], scratch=strip)

time: 185 us -> 184 us (level)
  the two profiles are of different devices: /device:TPU:14 before, /device:TPU:46 now
where the time goes in v9:
time: 184 us; the launch traced here: 182 us
  starting transfers between devices  65 us (35%)
  waiting for transfers between devices  51.2 us (28%)
  blocking collectives  41.4 us (22%)
  Pallas kernels  23.3 us (13%)
    all_to_all x3, blocking collectives, body(): got = lax.all_to_all(send, 'rad', 0, 0)  41.4 us
    ppermute x4, waiting for transfers between devices, body(): high = lax.ppermute(second_swap, 'rad', swaps(rad_size, 1))  31.6 us
    pallas_call x17, Pallas kernels, call(): pl.pallas_call(kernel, out_shape=[jax.ShapeDtypeStruct(o, jnp.float32) fo...  23.3 us
    all_to_all x4, starting transfers between devices, body(): across = lax.all_to_all(send, 'row', 0, 0)  19.3 us
    ppermute x4, starting transfers between devices, body(): high = lax.ppermute(second_swap, 'rad', swaps(rad_size, 1))  16.2 us
    ppermute x4, starting transfers between devices, body(): other_way = lax.ppermute(beside, 'sec', swaps(sections, 1))  12.6 us
    all_to_all x1, starting transfers between devices, body(): got = lax.all_to_all(send, 'rad', 0, 0)  9.6 us
    all_to_all x1, waiting for transfers between devices, body(): got = lax.all_to_all(send, 'rad', 0, 0)  9.47 us
  transfers between devices with their start and end apart: 22, of which 13 were waited for; matrix products, arithmetic and copies ran while one was open for 0% of the time, Pallas kernels for 4%

profile of v9, /device:TPU:46, one launch (start us, length us, event | category | flops | bytes accessed | tf_op | source)
XLA Modules:
  0.0 182.5 jit_solution(17064601503629781762)
XLA Ops:
  0.6 3.1 %shard_map.127 = (f32[6,8,128]{2,1,0:T(8,128)}, f32[8,128]{1,0:T(8,128)}, f32[8,16,128]{2,1,0:T(8,128)}, f32[112,128]{1,0:T(8,128)}, f32[112,128]{1,0:T(8,128)}) custom-call(s32[6]{0:T(128)} %stack.15.ids, f32[5]{0:T(128)} %weight.9, s32[8]{0:T(128)} %bitcast.34, s32[8]{0:T(128)} %bitcast.35, f32[5,16,8,128]{3,2,1,0:T(8,128)} %bitcast.15, ...), custom_call_target="tpu_custom_call" | custom-call | bytes 208896 | tf_op jit(solution)/shard_map/pallas_call | solution.py:41
  3.7 4.9 %all-to-all-start = ((f32[8,16,128]{2,1,0:T(8,128)}), f32[8,16,128]{2,1,0:T(8,128)S(1)}, u32[]{:S(2)}, u32[]{:S(2)}) async-start(f32[8,16,128]{2,1,0:T(8,128)} %get-tuple-element.28), calls=%async_computation | async-start | bytes 131072 | tf_op jit(solution)/shard_map/all_to_all | solution.py:390
  8.7 3.8 %collective-permute-start.3 = (f32[6,8,128]{2,1,0:T(8,128)S(1)}, f32[6,8,128]{2,1,0:T(8,128)S(1)}, u32[]{:S(2)}, u32[]{:S(2)}) collective-permute-start(f32[6,8,128]{2,1,0:T(8,128)S(1)} %copy-done.9), channel_id=1, source_target_pairs={{64,128},{128,64},{65,129},{129,65},{66,130},{130,66},{67,131},{13... | collective-permute-start | bytes 73736 | tf_op jit(solution)/shard_map/ppermute | solution.py:397
  17.7 9.6 %all-to-all-start.1 = ((f32[8,48,128]{2,1,0:T(8,128)}), f32[8,48,128]{2,1,0:T(8,128)S(1)}, u32[]{:S(2)}, u32[]{:S(2)}) async-start(f32[8,48,128]{2,1,0:T(8,128)} %shard_map.129), calls=%async_computation.1 | async-start | bytes 393216 | tf_op jit(solution)/shard_map/all_to_all | solution.py:404
  27.3 9.5 %all-to-all-done.1.got = f32[8,48,128]{2,1,0:T(8,128)S(1)} async-done(((f32[8,48,128]{2,1,0:T(8,128)}), f32[8,48,128]{2,1,0:T(8,128)S(1)}, u32[]{:S(2)}, u32[]{:S(2)}) %all-to-all-start.1) | async-done | bytes 196640 | tf_op jit(solution)/shard_map/all_to_all | solution.py:404
  38.4 4.9 %all-to-all-start.2 = ((f32[8,48,128]{2,1,0:T(8,128)}), f32[8,48,128]{2,1,0:T(8,128)S(1)}, u32[]{:S(2)}, u32[]{:S(2)}) async-start(f32[8,48,128]{2,1,0:T(8,128)} %shard_map.130), calls=%async_computation.2 | async-start | bytes 393216 | tf_op jit(solution)/shard_map/all_to_all | solution.py:416
  43.9 4.0 %collective-permute-start.1 = (f32[112,128]{1,0:T(8,128)S(1)}, f32[112,128]{1,0:T(8,128)S(1)}, u32[]{:S(2)}, u32[]{:S(2)}) collective-permute-start(f32[112,128]{1,0:T(8,128)S(1)} %copy-done.13), channel_id=1, source_target_pairs={{1,2},{2,1},{3,4},{4,3},{5,6},{6,5},{9,10},{10,9},{11,12},{12,11},... | collective-permute-start | bytes 172040 | tf_op jit(solution)/shard_map/ppermute | solution.py:405
  48.1 8.0 %collective-permute-done.1.second_swap.from_second = f32[112,128]{1,0:T(8,128)S(1)} collective-permute-done((f32[112,128]{1,0:T(8,128)S(1)}, f32[112,128]{1,0:T(8,128)S(1)}, u32[]{:S(2)}, u32[]{:S(2)}) %collective-permute-start.1) | collective-permute-done | bytes 57376 | tf_op jit(solution)/shard_map/ppermute | solution.py:405
  58.6 2.9 %collective-permute-start.5 = (f32[6,8,128]{2,1,0:T(8,128)S(1)}, f32[6,8,128]{2,1,0:T(8,128)S(1)}, u32[]{:S(2)}, u32[]{:S(2)}) collective-permute-start(f32[6,8,128]{2,1,0:T(8,128)S(1)} %get-tuple-element.35), channel_id=1, source_target_pairs={{64,128},{128,64},{65,129},{129,65},{66,130},{130,66},{67,131},{13... | collective-permute-start | bytes 73736 | tf_op jit(solution)/shard_map/ppermute | solution.py:397
  66.0 13.8 %all_to_all.45.got = f32[8,48,128]{2,1,0:T(8,128)S(1)} all-to-all(f32[8,48,128]{2,1,0:T(8,128)S(1)} %shard_map.133), channel_id=1, replica_groups=mesh['sec'=4,'row'=8,'rad'=8] {'rad'}, dimensions={0} | all-to-all | bytes 393216 | tf_op jit(solution)/shard_map/all_to_all | solution.py:404
  81.4 4.8 %all-to-all-start.4 = ((f32[8,56,128]{2,1,0:T(8,128)}), f32[8,56,128]{2,1,0:T(8,128)S(1)}, u32[]{:S(2)}, u32[]{:S(2)}) async-start(f32[8,56,128]{2,1,0:T(8,128)} %shard_map.134), calls=%async_computation.4 | async-start | bytes 458752 | tf_op jit(solution)/shard_map/all_to_all | solution.py:416
  86.7 4.0 %collective-permute-start.7 = (f32[80,128]{1,0:T(8,128)S(1)}, f32[80,128]{1,0:T(8,128)S(1)}, u32[]{:S(2)}, u32[]{:S(2)}) collective-permute-start(f32[80,128]{1,0:T(8,128)S(1)} %get-tuple-element.38), channel_id=1, source_target_pairs={{1,2},{2,1},{3,4},{4,3},{5,6},{6,5},{9,10},{10,9},{11,12},{12,11},... | collective-permute-start | bytes 122888 | tf_op jit(solution)/shard_map/ppermute | solution.py:405
  90.8 7.9 %collective-permute-done.7.second_swap.from_second = f32[80,128]{1,0:T(8,128)S(1)} collective-permute-done((f32[80,128]{1,0:T(8,128)S(1)}, f32[80,128]{1,0:T(8,128)S(1)}, u32[]{:S(2)}, u32[]{:S(2)}) %collective-permute-start.7) | collective-permute-done | bytes 40992 | tf_op jit(solution)/shard_map/ppermute | solution.py:405
  99.4 2.9 %collective-permute-start.9 = (f32[6,8,128]{2,1,0:T(8,128)S(1)}, f32[6,8,128]{2,1,0:T(8,128)S(1)}, u32[]{:S(2)}, u32[]{:S(2)}) collective-permute-start(f32[6,8,128]{2,1,0:T(8,128)S(1)} %get-tuple-element.41), channel_id=1, source_target_pairs={{64,128},{128,64},{65,129},{129,65},{66,130},{130,66},{67,131},{13... | collective-permute-start | bytes 73736 | tf_op jit(solution)/shard_map/ppermute | solution.py:397
  106.8 13.8 %all_to_all.46.got = f32[8,48,128]{2,1,0:T(8,128)S(1)} all-to-all(f32[8,48,128]{2,1,0:T(8,128)S(1)} %shard_map.137), channel_id=1, replica_groups=mesh['sec'=4,'row'=8,'rad'=8] {'rad'}, dimensions={0} | all-to-all | bytes 393216 | tf_op jit(solution)/shard_map/all_to_all | solution.py:404
  122.3 4.8 %all-to-all-start.6 = ((f32[8,56,128]{2,1,0:T(8,128)}), f32[8,56,128]{2,1,0:T(8,128)S(1)}, u32[]{:S(2)}, u32[]{:S(2)}) async-start(f32[8,56,128]{2,1,0:T(8,128)} %shard_map.138), calls=%async_computation.6 | async-start | bytes 458752 | tf_op jit(solution)/shard_map/all_to_all | solution.py:416
  127.5 4.0 %collective-permute-start.11 = (f32[80,128]{1,0:T(8,128)S(1)}, f32[80,128]{1,0:T(8,128)S(1)}, u32[]{:S(2)}, u32[]{:S(2)}) collective-permute-start(f32[80,128]{1,0:T(8,128)S(1)} %get-tuple-element.44), channel_id=1, source_target_pairs={{1,2},{2,1},{3,4},{4,3},{5,6},{6,5},{9,10},{10,9},{11,12},{12,11},... | collective-permute-start | bytes 122888 | tf_op jit(solution)/shard_map/ppermute | solution.py:405
  131.6 7.9 %collective-permute-done.11.second_swap.from_second = f32[80,128]{1,0:T(8,128)S(1)} collective-permute-done((f32[80,128]{1,0:T(8,128)S(1)}, f32[80,128]{1,0:T(8,128)S(1)}, u32[]{:S(2)}, u32[]{:S(2)}) %collective-permute-start.11) | collective-permute-done | bytes 40992 | tf_op jit(solution)/shard_map/ppermute | solution.py:405
  140.2 2.9 %collective-permute-start.13 = (f32[6,8,128]{2,1,0:T(8,128)S(1)}, f32[6,8,128]{2,1,0:T(8,128)S(1)}, u32[]{:S(2)}, u32[]{:S(2)}) collective-permute-start(f32[6,8,128]{2,1,0:T(8,128)S(1)} %get-tuple-element.47), channel_id=1, source_target_pairs={{64,128},{128,64},{65,129},{129,65},{66,130},{130,66},{67,131},{13... | collective-permute-start | bytes 73736 | tf_op jit(solution)/shard_map/ppermute | solution.py:397
  147.7 13.8 %all_to_all.47.got = f32[8,48,128]{2,1,0:T(8,128)S(1)} all-to-all(f32[8,48,128]{2,1,0:T(8,128)S(1)} %shard_map.141), channel_id=1, replica_groups=mesh['sec'=4,'row'=8,'rad'=8] {'rad'}, dimensions={0} | all-to-all | bytes 393216 | tf_op jit(solution)/shard_map/all_to_all | solution.py:404
  163.1 4.8 %all-to-all-start.8 = ((f32[8,56,128]{2,1,0:T(8,128)}), f32[8,56,128]{2,1,0:T(8,128)S(1)}, u32[]{:S(2)}, u32[]{:S(2)}) async-start(f32[8,56,128]{2,1,0:T(8,128)} %shard_map.142), calls=%async_computation.8 | async-start | bytes 458752 | tf_op jit(solution)/shard_map/all_to_all | solution.py:416
  168.4 4.0 %collective-permute-start.15 = (f32[80,128]{1,0:T(8,128)S(1)}, f32[80,128]{1,0:T(8,128)S(1)}, u32[]{:S(2)}, u32[]{:S(2)}) collective-permute-start(f32[80,128]{1,0:T(8,128)S(1)} %get-tuple-element.50), channel_id=1, source_target_pairs={{1,2},{2,1},{3,4},{4,3},{5,6},{6,5},{9,10},{10,9},{11,12},{12,11},... | collective-permute-start | bytes 122888 | tf_op jit(solution)/shard_map/ppermute | solution.py:405
  172.4 7.8 %collective-permute-done.15.second_swap = f32[80,128]{1,0:T(8,128)S(1)} collective-permute-done((f32[80,128]{1,0:T(8,128)S(1)}, f32[80,128]{1,0:T(8,128)S(1)}, u32[]{:S(2)}, u32[]{:S(2)}) %collective-permute-start.15) | collective-permute-done | bytes 40992 | tf_op jit(solution)/shard_map/ppermute | solution.py:405
  180.3 2.2 %shard_map.143 = f32[5,16,8,128]{3,2,1,0:T(8,128)} custom-call(s32[6]{0:T(128)S(1)} %copy-done.5, s32[8,16]{1,0:T(8,128)S(1)} %bitcast.25, f32[5]{0:T(128)S(1)} %copy-done.10, f32[5]{0:T(128)S(1)} %copy-done.11, f32[5,16,8,128]{3,2,1,0:T(8,128)S(1)} %get-tuple-element.46.field, f32[13,16,8,128]{3,2,1,0:T(8,128)S(1)} %shard_map.128.coef, ...), custom_call_target="tpu_custom_call" | custom-call | flops 4915200 | bytes 2088960 | tf_op jit(solution)/shard_map/pallas_call | solution.py:41
  (76 shorter events, 31.8 us)
Async XLA Ops:
  3.7 13.9 %all-to-all-start = ((f32[8,16,128]{2,1,0:T(8,128)}), f32[8,16,128]{2,1,0:T(8,128)S(1)}, u32[]{:S(2)}, u32[]{:S(2)}) async-start(f32[8,16,128]{2,1,0:T(8,128)} %get-tuple-element.28), calls=%async_computation | async-start | bytes 131072 | tf_op jit(solution)/shard_map/all_to_all | solution.py:390
  8.7 5.7 %collective-permute-start.3 = (f32[6,8,128]{2,1,0:T(8,128)S(1)}, f32[6,8,128]{2,1,0:T(8,128)S(1)}, u32[]{:S(2)}, u32[]{:S(2)}) collective-permute-start(f32[6,8,128]{2,1,0:T(8,128)S(1)} %copy-done.9), channel_id=1, source_target_pairs={{64,128},{128,64},{65,129},{129,65},{66,130},{130,66},{67,131},{13... | collective-permute-start | bytes 73736 | tf_op jit(solution)/shard_map/ppermute | solution.py:397
  12.5 3.9 %collective-permute-start.2 = (f32[6,8,128]{2,1,0:T(8,128)S(1)}, f32[6,8,128]{2,1,0:T(8,128)S(1)}, u32[]{:S(2)}, u32[]{:S(2)}) collective-permute-start(f32[6,8,128]{2,1,0:T(8,128)S(1)} %copy-done.9), channel_id=1, source_target_pairs={{0,64},{64,0},{128,192},{192,128},{1,65},{65,1},{129,193},{193,129... | collective-permute-start | bytes 73736 | tf_op jit(solution)/shard_map/ppermute | solution.py:396
  17.7 19.1 %all-to-all-start.1 = ((f32[8,48,128]{2,1,0:T(8,128)}), f32[8,48,128]{2,1,0:T(8,128)S(1)}, u32[]{:S(2)}, u32[]{:S(2)}) async-start(f32[8,48,128]{2,1,0:T(8,128)} %shard_map.129), calls=%async_computation.1 | async-start | bytes 393216 | tf_op jit(solution)/shard_map/all_to_all | solution.py:404
  38.4 17.7 %copy-start.2 = (f32[1,16,8,128]{3,2,1,0:T(8,128)S(1)}, f32[1,16,8,128]{3,2,1,0:T(8,128)}, u32[]{:S(2)}) copy-start(f32[1,16,8,128]{3,2,1,0:T(8,128)} %param.16) | copy-start | bytes 196612
  38.4 17.7 %copy-start.3 = (f32[1,16,8,128]{3,2,1,0:T(8,128)S(1)}, f32[1,16,8,128]{3,2,1,0:T(8,128)}, u32[]{:S(2)}) copy-start(f32[1,16,8,128]{3,2,1,0:T(8,128)} %param.17) | copy-start | bytes 196612
  38.4 18.7 %all-to-all-start.2 = ((f32[8,48,128]{2,1,0:T(8,128)}), f32[8,48,128]{2,1,0:T(8,128)S(1)}, u32[]{:S(2)}, u32[]{:S(2)}) async-start(f32[8,48,128]{2,1,0:T(8,128)} %shard_map.130), calls=%async_computation.2 | async-start | bytes 393216 | tf_op jit(solution)/shard_map/all_to_all | solution.py:416
  43.4 4.7 %collective-permute-start = (f32[112,128]{1,0:T(8,128)S(1)}, f32[112,128]{1,0:T(8,128)S(1)}, u32[]{:S(2)}, u32[]{:S(2)}) collective-permute-start(f32[112,128]{1,0:T(8,128)S(1)} %copy-done.14), channel_id=1, source_target_pairs={{0,1},{1,0},{2,3},{3,2},{4,5},{5,4},{6,7},{7,6},{8,9},{9,8},{10,11... | collective-permute-start | bytes 172040 | tf_op jit(solution)/shard_map/ppermute | solution.py:406
  43.9 12.2 %collective-permute-start.1 = (f32[112,128]{1,0:T(8,128)S(1)}, f32[112,128]{1,0:T(8,128)S(1)}, u32[]{:S(2)}, u32[]{:S(2)}) collective-permute-start(f32[112,128]{1,0:T(8,128)S(1)} %copy-done.13), channel_id=1, source_target_pairs={{1,2},{2,1},{3,4},{4,3},{5,6},{6,5},{9,10},{10,9},{11,12},{12,11},... | collective-permute-start | bytes 172040 | tf_op jit(solution)/shard_map/ppermute | solution.py:405
  58.6 5.7 %collective-permute-start.5 = (f32[6,8,128]{2,1,0:T(8,128)S(1)}, f32[6,8,128]{2,1,0:T(8,128)S(1)}, u32[]{:S(2)}, u32[]{:S(2)}) collective-permute-start(f32[6,8,128]{2,1,0:T(8,128)S(1)} %get-tuple-element.35), channel_id=1, source_target_pairs={{64,128},{128,64},{65,129},{129,65},{66,130},{130,66},{67,131},{13... | collective-permute-start | bytes 73736 | tf_op jit(solution)/shard_map/ppermute | solution.py:397
  61.5 3.9 %collective-permute-start.4 = (f32[6,8,128]{2,1,0:T(8,128)S(1)}, f32[6,8,128]{2,1,0:T(8,128)S(1)}, u32[]{:S(2)}, u32[]{:S(2)}) collective-permute-start(f32[6,8,128]{2,1,0:T(8,128)S(1)} %get-tuple-element.35), channel_id=1, source_target_pairs={{0,64},{64,0},{128,192},{192,128},{1,65},{65,1},{129,193},{193,129... | collective-permute-start | bytes 73736 | tf_op jit(solution)/shard_map/ppermute | solution.py:396
  81.4 17.2 %all-to-all-start.4 = ((f32[8,56,128]{2,1,0:T(8,128)}), f32[8,56,128]{2,1,0:T(8,128)S(1)}, u32[]{:S(2)}, u32[]{:S(2)}) async-start(f32[8,56,128]{2,1,0:T(8,128)} %shard_map.134), calls=%async_computation.4 | async-start | bytes 458752 | tf_op jit(solution)/shard_map/all_to_all | solution.py:416
  86.2 4.5 %collective-permute-start.6 = (f32[80,128]{1,0:T(8,128)S(1)}, f32[80,128]{1,0:T(8,128)S(1)}, u32[]{:S(2)}, u32[]{:S(2)}) collective-permute-start(f32[80,128]{1,0:T(8,128)S(1)} %get-tuple-element.37), channel_id=1, source_target_pairs={{0,1},{1,0},{2,3},{3,2},{4,5},{5,4},{6,7},{7,6},{8,9},{9,8},{10,11... | collective-permute-start | bytes 122888 | tf_op jit(solution)/shard_map/ppermute | solution.py:406
  86.7 11.9 %collective-permute-start.7 = (f32[80,128]{1,0:T(8,128)S(1)}, f32[80,128]{1,0:T(8,128)S(1)}, u32[]{:S(2)}, u32[]{:S(2)}) collective-permute-start(f32[80,128]{1,0:T(8,128)S(1)} %get-tuple-element.38), channel_id=1, source_target_pairs={{1,2},{2,1},{3,4},{4,3},{5,6},{6,5},{9,10},{10,9},{11,12},{12,11},... | collective-permute-start | bytes 122888 | tf_op jit(solution)/shard_map/ppermute | solution.py:405
  99.4 5.7 %collective-permute-start.9 = (f32[6,8,128]{2,1,0:T(8,128)S(1)}, f32[6,8,128]{2,1,0:T(8,128)S(1)}, u32[]{:S(2)}, u32[]{:S(2)}) collective-permute-start(f32[6,8,128]{2,1,0:T(8,128)S(1)} %get-tuple-element.41), channel_id=1, source_target_pairs={{64,128},{128,64},{65,129},{129,65},{66,130},{130,66},{67,131},{13... | collective-permute-start | bytes 73736 | tf_op jit(solution)/shard_map/ppermute | solution.py:397
  102.3 3.9 %collective-permute-start.8 = (f32[6,8,128]{2,1,0:T(8,128)S(1)}, f32[6,8,128]{2,1,0:T(8,128)S(1)}, u32[]{:S(2)}, u32[]{:S(2)}) collective-permute-start(f32[6,8,128]{2,1,0:T(8,128)S(1)} %get-tuple-element.41), channel_id=1, source_target_pairs={{0,64},{64,0},{128,192},{192,128},{1,65},{65,1},{129,193},{193,129... | collective-permute-start | bytes 73736 | tf_op jit(solution)/shard_map/ppermute | solution.py:396
  122.3 17.2 %all-to-all-start.6 = ((f32[8,56,128]{2,1,0:T(8,128)}), f32[8,56,128]{2,1,0:T(8,128)S(1)}, u32[]{:S(2)}, u32[]{:S(2)}) async-start(f32[8,56,128]{2,1,0:T(8,128)} %shard_map.138), calls=%async_computation.6 | async-start | bytes 458752 | tf_op jit(solution)/shard_map/all_to_all | solution.py:416
  127.0 4.5 %collective-permute-start.10 = (f32[80,128]{1,0:T(8,128)S(1)}, f32[80,128]{1,0:T(8,128)S(1)}, u32[]{:S(2)}, u32[]{:S(2)}) collective-permute-start(f32[80,128]{1,0:T(8,128)S(1)} %get-tuple-element.43), channel_id=1, source_target_pairs={{0,1},{1,0},{2,3},{3,2},{4,5},{5,4},{6,7},{7,6},{8,9},{9,8},{10,11... | collective-permute-start | bytes 122888 | tf_op jit(solution)/shard_map/ppermute | solution.py:406
  127.5 11.9 %collective-permute-start.11 = (f32[80,128]{1,0:T(8,128)S(1)}, f32[80,128]{1,0:T(8,128)S(1)}, u32[]{:S(2)}, u32[]{:S(2)}) collective-permute-start(f32[80,128]{1,0:T(8,128)S(1)} %get-tuple-element.44), channel_id=1, source_target_pairs={{1,2},{2,1},{3,4},{4,3},{5,6},{6,5},{9,10},{10,9},{11,12},{12,11},... | collective-permute-start | bytes 122888 | tf_op jit(solution)/shard_map/ppermute | solution.py:405
  140.2 5.7 %collective-permute-start.13 = (f32[6,8,128]{2,1,0:T(8,128)S(1)}, f32[6,8,128]{2,1,0:T(8,128)S(1)}, u32[]{:S(2)}, u32[]{:S(2)}) collective-permute-start(f32[6,8,128]{2,1,0:T(8,128)S(1)} %get-tuple-element.47), channel_id=1, source_target_pairs={{64,128},{128,64},{65,129},{129,65},{66,130},{130,66},{67,131},{13... | collective-permute-start | bytes 73736 | tf_op jit(solution)/shard_map/ppermute | solution.py:397
  143.2 3.9 %collective-permute-start.12 = (f32[6,8,128]{2,1,0:T(8,128)S(1)}, f32[6,8,128]{2,1,0:T(8,128)S(1)}, u32[]{:S(2)}, u32[]{:S(2)}) collective-permute-start(f32[6,8,128]{2,1,0:T(8,128)S(1)} %get-tuple-element.47), channel_id=1, source_target_pairs={{0,64},{64,0},{128,192},{192,128},{1,65},{65,1},{129,193},{193,129... | collective-permute-start | bytes 73736 | tf_op jit(solution)/shard_map/ppermute | solution.py:396
  163.1 17.2 %all-to-all-start.8 = ((f32[8,56,128]{2,1,0:T(8,128)}), f32[8,56,128]{2,1,0:T(8,128)S(1)}, u32[]{:S(2)}, u32[]{:S(2)}) async-start(f32[8,56,128]{2,1,0:T(8,128)} %shard_map.142), calls=%async_computation.8 | async-start | bytes 458752 | tf_op jit(solution)/shard_map/all_to_all | solution.py:416
  167.9 4.5 %collective-permute-start.14 = (f32[80,128]{1,0:T(8,128)S(1)}, f32[80,128]{1,0:T(8,128)S(1)}, u32[]{:S(2)}, u32[]{:S(2)}) collective-permute-start(f32[80,128]{1,0:T(8,128)S(1)} %get-tuple-element.49), channel_id=1, source_target_pairs={{0,1},{1,0},{2,3},{3,2},{4,5},{5,4},{6,7},{7,6},{8,9},{9,8},{10,11... | collective-permute-start | bytes 122888 | tf_op jit(solution)/shard_map/ppermute | solution.py:406
  168.4 11.9 %collective-permute-start.15 = (f32[80,128]{1,0:T(8,128)S(1)}, f32[80,128]{1,0:T(8,128)S(1)}, u32[]{:S(2)}, u32[]{:S(2)}) collective-permute-start(f32[80,128]{1,0:T(8,128)S(1)} %get-tuple-element.50), channel_id=1, source_target_pairs={{1,2},{2,1},{3,4},{4,3},{5,6},{6,5},{9,10},{10,9},{11,12},{12,11},... | collective-permute-start | bytes 122888 | tf_op jit(solution)/shard_map/ppermute | solution.py:405
  (13 other events, 115.3 us)
